TPU v7x, 256 devices: a whole 4x4x8 slice. The times are simulated.
256 devices in a mesh: sec: 64 (over z, x, core), row: 4 (over y).
Axes of the slice: x: 4, y: 4, z: 8, core: 2. Of those that a mesh axis runs over, the one named last changes fastest.
Arguments:
- left_block: bfloat16 [128, 2048, 128], P('sec', 'row'), may hold values from -6 to 6
- right_block: bfloat16 [128, 128, 2048], P('sec'), may hold values from -6 to 6
- left_ops: float32 [4, 16, 16], replicated, may hold values from -1.5 to 1.5
- right_ops: float32 [4, 16, 16], replicated, may hold values from -1.5 to 1.5
- charges: int32 [128], replicated, may hold values from 0 to 6
- live_states: int32 [128], replicated, may hold values from 64 to 128
- kept: int32 [128], replicated, may hold values from 64 to 128
- start: int32 [128, 128], replicated, may hold values from 0 to 511, all different within a row
Outputs:
- basis: float32 [128, 2048, 128], P('sec', 'row')
- right_new: float32 [128, 128, 2048], P('sec', None, 'row')
Inputs may be any that keep to these rules, and one draw needn't show every extreme that they name: The 128 start columns of a sector are distinct.
All inputs are finite; a program needn't handle non-finite values.
Results may differ from a plain program's by a relative error of at most 0.0065.
Values may be sent and summed in bfloat16 or wider, within the bound.
No kernel may reach another device: no remote copies, remote signals or barrier semaphores. Data moves between devices by JAX's collectives and lax.ppermute only.
A program may use at most 64 MiB of HBM per device.

v0:
```python
import functools

import jax
import jax.numpy as jnp
from jax import lax
from jax.sharding import Mesh
from jax.sharding import PartitionSpec as P

SITE = 16
ITERS = 2
SEC = ("sec_0", "sec_1", "sec_2")
SEC_ROW = ("sec_0", "sec_1", "sec_2", "row")


chemical = 0.4
highest = lax.Precision.HIGHEST


def copy_for_each(array, axis):
    copies = jnp.broadcast_to(array, (lax.axis_size(axis), *array.shape))
    return lax.all_to_all(copies, axis, split_axis=0, concat_axis=0, tiled=True)


def of_everyone(array, axis):
    everything = copy_for_each(array, axis)
    return jnp.sum(everything, axis=0)


def cut_along(array, dim, devices):
    lengths = array.shape
    tiles = array.reshape(*lengths[:dim], devices, lengths[dim] // devices, *lengths[dim + 1 :])
    return jnp.moveaxis(tiles, dim, 0)


def summed_on_arrival(array, axis, dim):
    tiles = cut_along(array, dim, lax.axis_size(axis))
    arrived = lax.all_to_all(tiles, axis, split_axis=0, concat_axis=0, tiled=True)
    return arrived.sum(axis=0)


def from_partner(value, axis, distance):
    mask = 2**distance
    pairs = [(source, source ^ mask) for source in range(lax.axis_size(axis))]
    return lax.ppermute(value, axis, pairs)


def by_axis(array, axes):
    return functools.reduce(lax.psum, axes, array)


def gate_rows(tensor_block, operators):
    site_dim = operators.shape[1]
    grouped = tensor_block.astype(jnp.float32).reshape(
        tensor_block.shape[0] // site_dim, site_dim, tensor_block.shape[1]
    )
    mixed_rows = jnp.einsum("tij,ajk->aitk", operators, grouped, precision=highest)
    return mixed_rows.reshape(
        tensor_block.shape[0], operators.shape[0] * tensor_block.shape[1]
    ).astype(jnp.bfloat16)


def gate_columns(tensor_block, operators):
    site_dim = operators.shape[1]
    grouped = tensor_block.astype(jnp.float32).reshape(
        tensor_block.shape[0], site_dim, tensor_block.shape[1] // site_dim
    )
    mixed_columns = jnp.einsum("tij,kjb->tkib", operators, grouped, precision=highest)
    return mixed_columns.reshape(
        operators.shape[0] * tensor_block.shape[0], tensor_block.shape[1]
    ).astype(jnp.bfloat16)


def triangular_apply(factor, matrix):

    def single(lower_factor, right_side):
        return jax.scipy.linalg.solve_triangular(lower_factor, right_side.T, lower=True).T

    return jax.vmap(single)(factor, matrix)


def orthonormal(krylov):
    gram_matrix = of_everyone(jnp.einsum("sri,srj->sij", krylov, krylov, precision=highest), "row")
    factor = jnp.linalg.cholesky(gram_matrix)
    return triangular_apply(factor, krylov)


def truncate(
    left_part, right_tensor, left_ids, right_ids, left_ops, right_ops, charges, kept, start
):
    left_gated = jax.vmap(gate_rows, in_axes=(0, None))(left_part, left_ops)
    right_gated = jax.vmap(gate_columns, in_axes=(0, None))(right_tensor, right_ops)
    weight = jnp.exp(-chemical * jnp.take(charges, right_ids).astype(jnp.float32))
    theta_block = weight[:, None, None] * jnp.einsum(
        "srk,skc->src", left_gated, right_gated, preferred_element_type=jnp.float32
    )
    columns = jnp.take(start, left_ids, axis=0)
    selector = (
        jnp.arange(left_gated.shape[2], dtype=jnp.int32)[None, :, None] == columns[:, None, :]
    ).astype(jnp.bfloat16)
    krylov = jnp.einsum("srk,skj->srj", left_gated, selector, preferred_element_type=jnp.float32)
    for round_index in range(ITERS):
        ortho_block = orthonormal(krylov)
        projected = lax.psum(
            jnp.einsum("src,srj->scj", theta_block, ortho_block, precision=highest), "row"
        )
        krylov = jnp.einsum("src,scj->srj", theta_block, projected, precision=highest)
    ortho_block = orthonormal(krylov)
    right_part = summed_on_arrival(
        jnp.einsum("srj,src->sjc", ortho_block, theta_block, precision=highest), "row", 2
    )
    keep_mask = (
        jnp.arange(ortho_block.shape[2], dtype=jnp.int32)[None, :]
        < jnp.take(kept, right_ids)[:, None]
    ).astype(jnp.float32)
    return (ortho_block * keep_mask[:, None, :], right_part * keep_mask[:, :, None])


def on_device(left_block, right_block, left_ops, right_ops, charges, live_states, kept, start):
    slot_count = left_block.shape[0]
    sector_count = slot_count * lax.axis_size(SEC)
    top_bit = lax.axis_size(SEC).bit_length() - 2
    home_ids = lax.axis_index(SEC) * slot_count + jnp.arange(slot_count, dtype=jnp.int32)
    mirror_ids = (home_ids + sector_count // 2) % sector_count
    local_rows = left_block.shape[1]
    row_states = (
        lax.axis_index("row") * local_rows + jnp.arange(local_rows, dtype=jnp.int32)
    ) // SITE
    live_here = jnp.take(live_states, home_ids)
    left_masked = jnp.where(
        row_states[None, :, None] < live_here[:, None, None],
        left_block,
        jnp.zeros((), jnp.bfloat16),
    )
    arrived = from_partner(right_block, SEC, top_bit)
    ortho_block, right_part = truncate(
        left_masked, arrived, home_ids, mirror_ids, left_ops, right_ops, charges, kept, start
    )
    right_part = from_partner(right_part, SEC, top_bit)
    total_weight = by_axis(jnp.sum(right_part * right_part), SEC_ROW)
    return (ortho_block, right_part / jnp.sqrt(total_weight))


def solution(mesh):
    finer = Mesh(
        mesh.devices.reshape(8, 4, 2, mesh.shape["row"]), ("sec_0", "sec_1", "sec_2", "row")
    )
    in_specs = (P(SEC, "row", None), P(SEC, None, None), P(), P(), P(), P(), P(), P())
    out_specs = (P(SEC, "row", None), P(SEC, None, "row"))
    return jax.shard_map(
        on_device, mesh=finer, in_specs=in_specs, out_specs=out_specs, check_vma=False
    )
```

profile of v0, /device:TPU:1, one launch (start us, length us, event | category | flops | bytes accessed | tf_op | source)
XLA Modules:
  0.0 506.3 jit_solution(9267082927348624103)
XLA Ops:
  7.3 1.3 gather_fusion.2
  8.6 0.1 broadcast_compare_fusion
  8.7 1.2 broadcast_select_fusion
  9.8 1.7 fusion.15
  11.5 0.5 copy.48
  12.1 0.4 convert_element_type.38
  12.6 0.6 gather_fusion
  13.1 0.1 broadcast_select_fusion.1
  13.2 0.4 fusion.23
  13.6 1.0 fusion.41
  14.7 0.8 broadcast_in_dim.51
  15.5 5.0 all-to-all-start
  20.5 7.4 %collective-permute-start = (bf16[2,128,2048]{2,1,0:T(8,128)(2,1)}, bf16[2,128,2048]{2,1,0:T(8,128)(2,1)S(1)}, u32[]{:S(2)}, u32[]{:S(2)}) collective-permute-start(bf16[2,128,2048]{2,1,0:T(8,128)(2,1)} %param.14), channel_id=1, source_target_pairs={{0,128},{4,132},{8,136},{12,140},{16,144},{20,148},{24,152},{28,15... | collective-permute-start | bytes 3145736 | tf_op jit(solution)/shard_map/ppermute | solution.py:44
  27.9 0.6 gather_fusion.1
  28.6 0.1 copy.51
  28.8 23.5 %custom-call.10 = f32[2,128,128]{2,1,0:T(8,128)S(1)} custom-call(f32[2,128,128]{2,1,0:T(8,128)S(1)} %fusion.30), custom_call_target="Cholesky" | custom-call | tf_op jit(solution)/shard_map/jit(cholesky)/cholesky | solution.py:83
  52.3 0.1 compare_reduce_fusion.2
  52.4 0.1 select_bitcast_fusion.2
  52.5 19.7 %custom-call.11 = f32[2,1,128,128]{2,3,1,0:T(8,128)S(1)} custom-call(f32[2,1,128,128]{3,2,1,0:T(8,128)S(1)} %select_bitcast_fusion.2), custom_call_target="InvertDiagBlocksLowerTriangular" | custom-call | tf_op jit(solution)/shard_map/vmap(jit(_solve_triangular))/triangular_solve | solution.py:76
  72.2 0.6 fusion.21
  72.8 0.2 copy.82
  73.1 3.6 convert_bitcast_fusion
  76.7 2.7 copy.49
  79.4 7.5 %convert_element_type.41 = bf16[2,512,2048]{2,1,0:T(8,128)(2,1)} reshape(bf16[2,4,128,16,128]{4,3,2,1,0:T(8,128)(2,1)} %copy.49) | data formatting | bytes 8388608 | tf_op jit(solution)/shard_map/vmap()/convert_element_type | solution.py:70
  86.8 4.6 fusion.40
  91.4 3.2 copy-done.3
  94.7 15.0 %fusion.8 = f32[2,2048,128]{2,1,0:T(8,128)} fusion(f32[2,128,512]{2,1,0:T(8,128)S(1)} %fusion.21, f32[2,512,2048]{2,1,0:T(8,128)S(1)} %fusion.40, f32[2]{0:T(128)S(1)} %fusion.39), kind=kOutput, calls=%fused_computation.12 | convolution fusion | flops 3223322624 | bytes 11010056 | tf_op jit(solution)/shard_map/src,srj->scj/dot_general | solution.py:104
  109.7 66.6 %all-reduce.3.cloned.1.call-done = f32[2,2048,128]{2,1,0:T(8,128)} async-done(((f32[2,2048,128]{2,1,0:T(8,128)}), f32[2,2048,128]{2,1,0:T(8,128)}) %all-reduce.3.cloned.1.call-update) | async-done | bytes 2097168 | tf_op jit(solution)/shard_map/psum | solution.py:103
  176.2 9.5 %fusion.6 = f32[2,512,128]{2,1,0:T(8,128)S(1)} fusion(f32[2,2048,128]{2,1,0:T(8,128)} %all-reduce.3.cloned.1.call-done, f32[2,512,2048]{2,1,0:T(8,128)} %copy-done.3, f32[2]{0:T(128)S(1)} %fusion.39), kind=kOutput, calls=%fused_computation.10 | convolution fusion | flops 3223322624 | bytes 11010056 | tf_op jit(solution)/shard_map/src,scj->srj/dot_general | solution.py:106
  185.8 1.0 fusion.42
  186.8 11.0 %all_to_all.20 = f32[4,2,128,128]{3,2,1,0:T(8,128)S(1)} all-to-all(f32[4,2,128,128]{3,2,1,0:T(8,128)S(1)} %broadcast_in_dim.52), channel_id=1, replica_groups=mesh['sec_0'=8,'sec_1'=4,'sec_2'=2,'row'=4] {'row'}, dimensions={0} | all-to-all | bytes 1048576 | tf_op jit(solution)/shard_map/all_to_all | solution.py:21
  197.8 0.1 copy.56
  198.0 23.5 %custom-call.12 = f32[2,128,128]{2,1,0:T(8,128)S(1)} custom-call(f32[2,128,128]{2,1,0:T(8,128)S(1)} %fusion.28), custom_call_target="Cholesky" | custom-call | tf_op jit(solution)/shard_map/jit(cholesky)/cholesky | solution.py:83
  221.5 0.1 compare_reduce_fusion.1
  221.6 0.1 select_bitcast_fusion.1
  221.7 19.7 %custom-call.13 = f32[2,1,128,128]{2,3,1,0:T(8,128)S(1)} custom-call(f32[2,1,128,128]{3,2,1,0:T(8,128)S(1)} %select_bitcast_fusion.1), custom_call_target="InvertDiagBlocksLowerTriangular" | custom-call | tf_op jit(solution)/shard_map/vmap(jit(_solve_triangular))/triangular_solve | solution.py:76
  241.4 0.6 fusion.19
  242.0 16.9 %fusion.4 = f32[2,2048,128]{2,1,0:T(8,128)} fusion(f32[2,128,512]{2,1,0:T(8,128)S(1)} %fusion.19, f32[2,512,2048]{2,1,0:T(8,128)} %copy-done.3, f32[2]{0:T(128)S(1)} %fusion.39), kind=kOutput, calls=%fused_computation.8 | convolution fusion | flops 3223322624 | bytes 11010056 | tf_op jit(solution)/shard_map/src,srj->scj/dot_general | solution.py:104
  258.9 64.6 %all-reduce.5.cloned.1.call-done = f32[2,2048,128]{2,1,0:T(8,128)} async-done(((f32[2,2048,128]{2,1,0:T(8,128)}), f32[2,2048,128]{2,1,0:T(8,128)}) %all-reduce.5.cloned.1.call-update) | async-done | bytes 2097168 | tf_op jit(solution)/shard_map/psum | solution.py:103
  323.5 9.5 %fusion.2 = f32[2,512,128]{2,1,0:T(8,128)S(1)} fusion(f32[2,2048,128]{2,1,0:T(8,128)} %all-reduce.5.cloned.1.call-done, f32[2,512,2048]{2,1,0:T(8,128)} %copy-done.3, f32[2]{0:T(128)S(1)} %fusion.39), kind=kOutput, calls=%fused_computation.6 | convolution fusion | flops 3223322624 | bytes 11010056 | tf_op jit(solution)/shard_map/src,scj->srj/dot_general | solution.py:106
  333.0 1.0 fusion.43
  334.1 11.2 %all_to_all.21 = f32[4,2,128,128]{3,2,1,0:T(8,128)S(1)} all-to-all(f32[4,2,128,128]{3,2,1,0:T(8,128)S(1)} %broadcast_in_dim.53), channel_id=1, replica_groups=mesh['sec_0'=8,'sec_1'=4,'sec_2'=2,'row'=4] {'row'}, dimensions={0} | all-to-all | bytes 1048576 | tf_op jit(solution)/shard_map/all_to_all | solution.py:21
  345.3 0.1 copy.61
  345.5 23.5 %custom-call.14 = f32[2,128,128]{2,1,0:T(8,128)S(1)} custom-call(f32[2,128,128]{2,1,0:T(8,128)S(1)} %fusion.26), custom_call_target="Cholesky" | custom-call | tf_op jit(solution)/shard_map/jit(cholesky)/cholesky | solution.py:83
  369.0 0.1 compare_reduce_fusion
  369.1 0.1 select_bitcast_fusion
  369.2 19.7 %custom-call.15 = f32[2,1,128,128]{2,3,1,0:T(8,128)S(1)} custom-call(f32[2,1,128,128]{3,2,1,0:T(8,128)S(1)} %select_bitcast_fusion), custom_call_target="InvertDiagBlocksLowerTriangular" | custom-call | tf_op jit(solution)/shard_map/vmap(jit(_solve_triangular))/triangular_solve | solution.py:76
  388.9 0.6 fusion.17
  389.5 7.5 %fusion = f32[2,128,2048]{2,1,0:T(8,128)S(1)} fusion(f32[2,128,512]{2,1,0:T(8,128)S(1)} %fusion.17, f32[2,512,2048]{2,1,0:T(8,128)} %copy-done.3, f32[2]{0:T(128)S(1)} %fusion.39), kind=kOutput, calls=%fused_computation.4 | convolution fusion | flops 3223322624 | bytes 11010056 | tf_op jit(solution)/shard_map/srj,src->sjc/dot_general | solution.py:109
  397.0 1.6 copy.84
  398.6 3.6 all-to-all-start.3
  402.2 0.6 gather_fusion.3
  402.9 23.8 %all-to-all-done.3 = f32[4,2,128,512]{3,2,1,0:T(8,128)S(1)} async-done(((f32[4,2,128,512]{3,2,1,0:T(8,128)}), f32[4,2,128,512]{3,2,1,0:T(8,128)S(1)}, u32[]{:S(2)}, u32[]{:S(2)}) %all-to-all-start.3) | async-done | bytes 2097184 | tf_op jit(solution)/shard_map/all_to_all | solution.py:37
  426.7 0.3 reduce_sum.48
  427.0 0.1 broadcast_multiply_fusion
  427.1 5.5 %collective-permute-start.1 = (f32[2,128,512]{2,1,0:T(8,128)S(1)}, f32[2,128,512]{2,1,0:T(8,128)S(1)}, u32[]{:S(2)}, u32[]{:S(2)}) collective-permute-start(f32[2,128,512]{2,1,0:T(8,128)S(1)} %get-tuple-element.13), channel_id=1, source_target_pairs={{0,128},{4,132},{8,136},{12,140},{16,144},{20,148},{24,152},{28,15... | collective-permute-start | bytes 1572872 | tf_op jit(solution)/shard_map/ppermute | solution.py:44
  432.6 12.9 %collective-permute-done.1 = f32[2,128,512]{2,1,0:T(8,128)S(1)} collective-permute-done((f32[2,128,512]{2,1,0:T(8,128)S(1)}, f32[2,128,512]{2,1,0:T(8,128)S(1)}, u32[]{:S(2)}, u32[]{:S(2)}) %collective-permute-start.1) | collective-permute-done | bytes 524320 | tf_op jit(solution)/shard_map/ppermute | solution.py:44
  445.5 0.7 multiply_reduce_fusion
  446.2 21.8 %psum.44 = f32[]{:T(128)} all-reduce(f32[]{:T(128)} %multiply_reduce_fusion), channel_id=1, replica_groups=mesh['sec_0'=8,'sec_1'=4,'sec_2'=2,'row'=4] {'sec_0'}, use_global_device_ids=true, to_apply=%region_9.13 | all-reduce | flops 1 | bytes 8 | tf_op jit(solution)/shard_map/psum | solution.py:48
  468.0 9.0 %psum.45 = f32[]{:T(128)} all-reduce(f32[]{:T(128)} %psum.44), channel_id=1, replica_groups=mesh['sec_0'=8,'sec_1'=4,'sec_2'=2,'row'=4] {'sec_1'}, use_global_device_ids=true, to_apply=%region_10.14 | all-reduce | flops 1 | bytes 8 | tf_op jit(solution)/shard_map/psum | solution.py:48
  477.0 12.2 %psum.46 = f32[]{:T(128)} all-reduce(f32[]{:T(128)} %psum.45), channel_id=1, replica_groups=mesh['sec_0'=8,'sec_1'=4,'sec_2'=2,'row'=4] {'sec_2'}, use_global_device_ids=true, to_apply=%region_11.15 | all-reduce | flops 1 | bytes 8 | tf_op jit(solution)/shard_map/psum | solution.py:48
  489.2 1.0 copy.65
  490.2 7.5 %psum.47 = f32[]{:T(128)} all-reduce(f32[]{:T(128)} %psum.46), channel_id=1, replica_groups=mesh['sec_0'=8,'sec_1'=4,'sec_2'=2,'row'=4] {'row'}, use_global_device_ids=true, to_apply=%region_12.16 | all-reduce | flops 1 | bytes 8 | tf_op jit(solution)/shard_map/psum | solution.py:48
  498.4 0.9 broadcast_divide_fusion
  (39 shorter events, 0.6 us)
Async XLA Ops:
  7.2 5.4 %copy-start = (s32[128,128]{1,0:T(8,128)S(1)}, s32[128,128]{1,0:T(8,128)}, u32[]{:S(2)}) copy-start(s32[128,128]{1,0:T(8,128)} %param.20) | copy-start | bytes 196612
  7.2 20.7 %copy-start.1 = (s32[128]{0:T(128)S(1)}, s32[128]{0:T(128)}, u32[]{:S(2)}) copy-start(s32[128]{0:T(128)} %param.17) | copy-start | bytes 1540
  7.2 65.9 %copy-start.4 = (f32[4,16,16]{2,1,0:T(8,128)S(1)}, f32[4,16,16]{2,1,0:T(8,128)}, u32[]{:S(2)}) copy-start(f32[4,16,16]{2,1,0:T(8,128)} %param.16) | copy-start | bytes 12292
  15.5 13.1 %all-to-all-start = ((f32[4,2,128,128]{3,2,1,0:T(8,128)}), f32[4,2,128,128]{3,2,1,0:T(8,128)S(1)}, u32[]{:S(2)}, u32[]{:S(2)}) async-start(f32[4,2,128,128]{3,2,1,0:T(8,128)} %broadcast_in_dim.51), calls=%async_computation | async-start | bytes 1048576 | tf_op jit(solution)/shard_map/all_to_all | solution.py:21
  20.5 155.7 %all-reduce.3.cloned.1.call-start = ((), (), s32[]{:S(2)}) async-start(), calls=%async_computation.4 | async-start | bytes 4194304 | tf_op jit(solution)/shard_map/psum | solution.py:103
  20.5 52.3 %collective-permute-start = (bf16[2,128,2048]{2,1,0:T(8,128)(2,1)}, bf16[2,128,2048]{2,1,0:T(8,128)(2,1)S(1)}, u32[]{:S(2)}, u32[]{:S(2)}) collective-permute-start(bf16[2,128,2048]{2,1,0:T(8,128)(2,1)} %param.14), channel_id=1, source_target_pairs={{0,128},{4,132},{8,136},{12,140},{16,144},{20,148},{24,152},{28,15... | collective-permute-start | bytes 3145736 | tf_op jit(solution)/shard_map/ppermute | solution.py:44
  91.4 3.2 copy-start.3
  109.6 213.9 %all-reduce.5.cloned.1.call-start = ((), (), s32[]{:S(2)}) async-start(), calls=%async_computation.5 | async-start | bytes 4194304 | tf_op jit(solution)/shard_map/psum | solution.py:103
  389.5 12.7 %copy-start.2 = (s32[128]{0:T(128)S(1)}, s32[128]{0:T(128)}, u32[]{:S(2)}) copy-start(s32[128]{0:T(128)} %param.19) | copy-start | bytes 1540
  398.6 28.1 %all-to-all-start.3 = ((f32[4,2,128,512]{3,2,1,0:T(8,128)}), f32[4,2,128,512]{3,2,1,0:T(8,128)S(1)}, u32[]{:S(2)}, u32[]{:S(2)}) async-start(f32[4,2,128,512]{3,2,1,0:T(8,128)} %bitcast.91), calls=%async_computation.3 | async-start | bytes 4194304 | tf_op jit(solution)/shard_map/all_to_all | solution.py:37
  427.1 18.4 %collective-permute-start.1 = (f32[2,128,512]{2,1,0:T(8,128)S(1)}, f32[2,128,512]{2,1,0:T(8,128)S(1)}, u32[]{:S(2)}, u32[]{:S(2)}) collective-permute-start(f32[2,128,512]{2,1,0:T(8,128)S(1)} %get-tuple-element.13), channel_id=1, source_target_pairs={{0,128},{4,132},{8,136},{12,140},{16,144},{20,148},{24,152},{28,15... | collective-permute-start | bytes 1572872 | tf_op jit(solution)/shard_map/ppermute | solution.py:44
Sparse Core Ops, SparseCore 0:
  109.8 66.4 all-reduce.2
  259.0 64.4 all-reduce.4
where the time goes:
time: 511 us; the launch traced here: 506 us
  waiting for transfers between devices  168 us (33%)
  other arithmetic  134 us (26%)
  matrix products  73.7 us (14%)
  blocking collectives  72.7 us (14%)
  local copies, waits for them, and re-layouts  21.5 us (4%)
  starting transfers between devices  21.5 us (4%)
  between operations  15.4 us (3%)
    psum x2, waiting for transfers between devices, truncate(): lax.psum(jnp.einsum('src,srj->scj', theta_block, ortho_block, precision=h...  131 us
    another operation x10, other arithmetic, orthonormal(): factor = jnp.linalg.cholesky(gram_matrix)  70.8 us
    another operation x7, other arithmetic, single(): jax.scipy.linalg.solve_triangular(lower_factor, right_side.T, lower=True)  59.3 us
    psum x4, blocking collectives, by_axis(): return functools.reduce(lax.psum, axes, array)  50.5 us
    dot_general x2, matrix products, truncate(): jnp.einsum('src,srj->scj', theta_block, ortho_block, precision=highest)  31.8 us
    all_to_all x1, waiting for transfers between devices, summed_on_arrival(): lax.all_to_all(tiles, axis, split_axis=0, concat_axis=0, tiled=True)  23.8 us
    all_to_all x2, blocking collectives, copy_for_each(): return lax.all_to_all(copies, axis, split_axis=0, concat_axis=0, tiled=True)  22.2 us
    dot_general x2, matrix products, truncate(): jnp.einsum('src,scj->srj', theta_block, projected, precision=highest)  19 us
  transfers between devices with their start and end apart: 6, of which 4 were waited for; matrix products, arithmetic and copies ran while one was open for 9% of the time, Pallas kernels for 0%

commit v1 on v0

v1 whole, which is shorter than its diff:
```python
import functools

import jax
import jax.numpy as jnp
from jax import lax
from jax.experimental import pallas as pl
from jax.experimental.pallas import tpu as pltpu
from jax.sharding import Mesh
from jax.sharding import PartitionSpec as P

SITE = 16
ITERS = 2
SEC = ("sec_0", "sec_1", "sec_2")
SEC_ROW = ("sec_0", "sec_1", "sec_2", "row")
WINDOW = 32

chemical = 0.4
highest = lax.Precision.HIGHEST


def from_partner(value, axis, distance):
    mask = 2**distance
    pairs = [(source, source ^ mask) for source in range(lax.axis_size(axis))]
    return lax.ppermute(value, axis, pairs)


def dot_over(left, right, left_dim, right_dim, precision=None):
    return lax.dot_general(
        left,
        right,
        (((left_dim,), (right_dim,)), ((), ())),
        precision=precision,
        preferred_element_type=jnp.float32,
    )


def two_parts(values):
    high = values.astype(jnp.bfloat16)
    low = (values - high.astype(jnp.float32)).astype(jnp.bfloat16)
    return high, low


def one_hot(shape, row_key, col_key):
    rows = lax.broadcasted_iota(jnp.int32, shape, 0)
    cols = lax.broadcasted_iota(jnp.int32, shape, 1)
    return row_key(rows) == col_key(cols)


def as_weights(mask):
    return jnp.where(mask, 1.0, 0.0).astype(jnp.bfloat16)


def lower_inverse(grams, window):
    n = grams[0].shape[0]
    lane = lax.broadcasted_iota(jnp.int32, (8, n), 1)
    sub = lax.broadcasted_iota(jnp.int32, (8, n), 0)
    rows = [[g[8 * q : 8 * q + 8, :] for q in range(n // 8)] for g in grams]
    span = window // 8
    for first in range(0, n // 8, span):
        last = first + span
        for q in range(first, last):
            k = 8 * q
            inside = (lane >= k) & (lane < k + 8)
            unit = (lane - k == sub).astype(jnp.float32)
            for mat in rows:
                cols = {
                    r: [jnp.broadcast_to(mat[r][:, k + m : k + m + 1], (8, n)) for m in range(8)]
                    for r in range(q, last)
                }
                for r in range(q, last):
                    mat[r] = jnp.where(inside, unit if r == q else 0.0, mat[r])
                for m in range(8):
                    pivot = jnp.broadcast_to(cols[q][m][m : m + 1, :], (8, n))
                    scale = lax.rsqrt(pivot)
                    head = jnp.broadcast_to(mat[q][m : m + 1, :], (8, n)) * scale
                    below = {r: cols[r][m] * scale for r in range(q, last)}
                    below[q] = jnp.where(sub > m, below[q], 0.0)
                    for j in range(m + 1, 8):
                        weight = jnp.broadcast_to(below[q][j : j + 1, :], (8, n))
                        for r in range(q, last):
                            cols[r][j] = cols[r][j] - below[r] * weight
                    for r in range(q, last):
                        mat[r] = mat[r] - below[r] * head
                    mat[q] = jnp.where(sub == m, head, mat[q])
        if last < n // 8:
            inblock = (lane >= 8 * first) & (lane < 8 * last)
            for mat in rows:
                panel = jnp.concatenate(mat[first:last], axis=0)
                panel_row = lax.broadcasted_iota(jnp.int32, panel.shape, 0) + 8 * first
                panel_lane = lax.broadcasted_iota(jnp.int32, panel.shape, 1)
                panel = jnp.where((panel_lane > panel_row) & (panel_lane < 8 * last), 0.0, panel)
                update = dot_over(panel, panel, 0, 0, highest)
                for r in range(last, n // 8):
                    mat[r] = jnp.where(inblock, 0.0, mat[r]) - update[8 * r : 8 * r + 8, :]
    full_row = lax.broadcasted_iota(jnp.int32, (n, n), 0)
    full_col = lax.broadcasted_iota(jnp.int32, (n, n), 1)
    return [jnp.where(full_col <= full_row, jnp.concatenate(mat, axis=0), 0.0) for mat in rows]


def right_kernel(
    row_ref, right_ref, right_ops_ref, left_ops_ref,
    square_ref, local_ref, left_mix_ref,
    right_mix, gated,
):
    terms, site = left_ops_ref.shape[0], SITE
    states = right_ref.shape[1]
    wide = site * site
    local_cols = local_ref.shape[2]

    @pl.when(pl.program_id(0) == 0)
    def _():
        spread = as_weights(
            one_hot((terms * wide, terms * site), lambda r: r // site, lambda c: c)
        )
        widen = as_weights(one_hot((site, wide), lambda r: r, lambda c: c // site))
        same = one_hot((terms * wide, wide), lambda r: r % site, lambda c: c % site)
        for part, piece in enumerate(two_parts(right_ops_ref[...])):
            tall = dot_over(spread, piece, 1, 0).astype(jnp.bfloat16)
            full = dot_over(tall, widen, 1, 0)
            right_mix[part] = jnp.where(same, full, 0.0).astype(jnp.bfloat16)
        tall_pick = as_weights(one_hot((wide, site), lambda r: r % site, lambda c: c))
        wide_pick = as_weights(one_hot((site, wide), lambda r: r, lambda c: c % site))
        group = one_hot((wide, wide), lambda r: r // site, lambda c: c // site)
        for t in range(terms):
            for part, piece in enumerate(two_parts(left_ops_ref[t])):
                tall = dot_over(tall_pick, piece, 1, 1).astype(jnp.bfloat16)
                full = dot_over(tall, wide_pick, 1, 0)
                left_mix_ref[t, part] = jnp.where(group, full, 0.0).astype(jnp.bfloat16)

    for pair in range(states // (2 * site)):
        base = pair * 2 * site
        halves = [
            jnp.concatenate(
                [
                    right_ref[0, base + h * site : base + (h + 1) * site, j * states : (j + 1) * states]
                    for j in range(site)
                ],
                axis=0,
            )
            for h in range(2)
        ]
        block = jnp.concatenate(halves, axis=1)
        for t in range(terms):
            rows = pl.ds(t * wide, wide)
            mixed = dot_over(right_mix[0, rows, :], block, 1, 0) + dot_over(
                right_mix[1, rows, :], block, 1, 0
            )
            mixed = mixed.astype(jnp.bfloat16)
            for h in range(2):
                for i in range(site):
                    gated[
                        t * states + base + h * site : t * states + base + (h + 1) * site,
                        i * states : (i + 1) * states,
                    ] = mixed[i * site : (i + 1) * site, h * states : (h + 1) * states]
    square_ref[0] = dot_over(gated[...], gated[...], 1, 1)
    offset = pl.multiple_of(row_ref[0] * local_cols, local_cols)
    local_ref[0] = gated[:, pl.ds(offset, local_cols)]


def krylov_kernel(
    row_ref, live_ref, kept_ref, weight_ref, left_ref, left_mix_ref, square_ref, local_ref, start_ref,
    basis_ref, right_ref, total_ref,
    gated, gram, block, image,
):
    chunks, slots, chunk_rows, states = left_ref.shape
    terms = left_mix_ref.shape[0]
    wide = left_mix_ref.shape[2]
    keep = block.shape[1]
    for s in range(slots):
        pieces = []
        for c in range(chunks):
            turned = left_ref[c, s].T
            for b in range(chunk_rows // wide):
                lane = lax.broadcasted_iota(jnp.int32, (states, wide), 1)
                alive = lane < live_ref[s] * SITE - (c * chunk_rows + b * wide)
                piece = turned[:, b * wide : (b + 1) * wide].astype(jnp.float32)
                pieces.append(jnp.where(alive, piece, 0.0).astype(jnp.bfloat16))
        tall = jnp.concatenate(pieces, axis=0)
        for t in range(terms):
            mixed = dot_over(tall, left_mix_ref[t, 0], 1, 0) + dot_over(
                tall, left_mix_ref[t, 1], 1, 0
            )
            mixed = mixed.astype(jnp.bfloat16)
            for b in range(len(pieces)):
                gated[s, t * states : (t + 1) * states, b * wide : (b + 1) * wide] = mixed[
                    b * states : (b + 1) * states, :
                ]
        gram[s] = dot_over(gated[s], gated[s], 1, 1)
        spots = lax.broadcasted_iota(jnp.int32, (keep, terms * states), 1)
        block[s] = jnp.where(spots == start_ref[s], 1.0, 0.0)

    def step(index, carry):
        images = [dot_over(block[s], gram[s], 1, 0, highest) for s in range(slots)]
        grams = [dot_over(images[s], block[s], 1, 1, highest) for s in range(slots)]
        inverses = lower_inverse(grams, WINDOW)
        for s in range(slots):
            image[s] = dot_over(inverses[s], images[s], 1, 0, highest)

        @pl.when(index < ITERS)
        def _():
            for s in range(slots):
                scale = weight_ref[s] * weight_ref[s]
                block[s] = scale * dot_over(image[s], square_ref[s], 1, 0, highest)

        @pl.when(index == ITERS)
        def _():
            for s in range(slots):
                block[s] = dot_over(inverses[s], block[s], 1, 0, highest)

        return carry

    lax.fori_loop(0, ITERS + 1, step, 0)
    offset = pl.multiple_of(row_ref[0] * chunk_rows, chunk_rows)
    total = jnp.zeros((1, 1), jnp.float32)
    for s in range(slots):
        mine = gated[s, :, pl.ds(offset, chunk_rows)]
        high, low = two_parts(block[s])
        basis = dot_over(high, mine, 1, 0) + dot_over(low, mine, 1, 0)
        keeps = lax.broadcasted_iota(jnp.int32, basis.shape, 0) < kept_ref[s]
        basis_ref[s] = jnp.where(keeps, basis, 0.0).T.astype(jnp.bfloat16)
        high, low = two_parts(image[s])
        part = dot_over(high, local_ref[s], 1, 0) + dot_over(low, local_ref[s], 1, 0)
        keeps = lax.broadcasted_iota(jnp.int32, part.shape, 0) < kept_ref[s]
        part = jnp.where(keeps, part * weight_ref[s], 0.0)
        right_ref[s] = part
        total += jnp.sum(jnp.sum(part * part, axis=0, keepdims=True), axis=1, keepdims=True)
    total_ref[...] = total


def smem():
    return pl.BlockSpec(memory_space=pltpu.SMEM)


def vmem():
    return pl.BlockSpec(memory_space=pltpu.VMEM)


def whole(shape):
    return pl.BlockSpec(shape, lambda s: (0,) * len(shape))


def slot(shape):
    return pl.BlockSpec((1, *shape), lambda s: (s,) + (0,) * len(shape))


def gate_right(row, right_block, right_ops, left_ops, local_cols):
    slots, states, cols = right_block.shape
    terms = left_ops.shape[0]
    bond, wide = terms * states, SITE * SITE
    return pl.pallas_call(
        right_kernel,
        grid=(slots,),
        in_specs=[smem(), slot((states, cols)), whole((terms * SITE, SITE)), whole(left_ops.shape)],
        out_specs=[
            slot((bond, bond)),
            slot((bond, local_cols)),
            whole((terms, 2, wide, wide)),
        ],
        out_shape=[
            jax.ShapeDtypeStruct((slots, bond, bond), jnp.float32),
            jax.ShapeDtypeStruct((slots, bond, local_cols), jnp.bfloat16),
            jax.ShapeDtypeStruct((terms, 2, wide, wide), jnp.bfloat16),
        ],
        scratch_shapes=[
            pltpu.VMEM((2, terms * wide, wide), jnp.bfloat16),
            pltpu.VMEM((bond, cols), jnp.bfloat16),
        ],
        compiler_params=pltpu.CompilerParams(vmem_limit_bytes=40 << 20),
        cost_estimate=pl.CostEstimate(flops=int(1e10), bytes_accessed=6 << 20, transcendentals=0),
        name="right_gate",
    )(row, right_block, right_ops.reshape(terms * SITE, SITE), left_ops)


def krylov_part(row, live, kept, weight, left_all, left_mix, square, local, start):
    chunks, slots, chunk_rows, states = left_all.shape
    bond, local_cols = local.shape[1:]
    keep = start.shape[1]
    return pl.pallas_call(
        krylov_kernel,
        in_specs=[smem()] * 4 + [vmem()] * 5,
        out_specs=[vmem()] * 3,
        out_shape=[
            jax.ShapeDtypeStruct((slots, chunk_rows, keep), jnp.bfloat16),
            jax.ShapeDtypeStruct((slots, keep, local_cols), jnp.float32),
            jax.ShapeDtypeStruct((1, 1), jnp.float32),
        ],
        scratch_shapes=[
            pltpu.VMEM((slots, bond, chunks * chunk_rows), jnp.bfloat16),
            pltpu.VMEM((slots, bond, bond), jnp.float32),
            pltpu.VMEM((slots, keep, bond), jnp.float32),
            pltpu.VMEM((slots, keep, bond), jnp.float32),
        ],
        compiler_params=pltpu.CompilerParams(vmem_limit_bytes=48 << 20),
        cost_estimate=pl.CostEstimate(flops=int(2e10), bytes_accessed=6 << 20, transcendentals=0),
        name="krylov",
    )(row, live, kept, weight, left_all, left_mix, square, local, start)


def on_device(left_block, right_block, left_ops, right_ops, charges, live_states, kept, start):
    slots = left_block.shape[0]
    sectors = slots * lax.axis_size(SEC)
    top_bit = lax.axis_size(SEC).bit_length() - 2
    right_first = lax.axis_index(SEC) * slots
    left_first = (right_first + sectors // 2) % sectors
    cut = lambda table, first: lax.dynamic_slice_in_dim(table, first, slots, 0)
    row = lax.axis_index("row").astype(jnp.int32).reshape(1)
    live = cut(live_states, left_first)
    kept_here = cut(kept, right_first)
    weight = jnp.exp(-chemical * cut(charges, right_first).astype(jnp.float32))
    start_here = cut(start, left_first)[:, :, None]
    left_theirs = from_partner(left_block, SEC, top_bit)
    left_all = lax.all_gather(left_theirs, "row", axis=0, tiled=False)
    local_cols = right_block.shape[2] // lax.axis_size("row")
    square, local, left_mix = gate_right(row, right_block, right_ops, left_ops, local_cols)
    basis, right_part, total = krylov_part(
        row, live, kept_here, weight, left_all, left_mix, square, local, start_here
    )
    basis = from_partner(basis, SEC, top_bit).astype(jnp.float32)
    total = lax.psum(total[0, 0], SEC_ROW)
    return basis, right_part / jnp.sqrt(total)


def solution(mesh):
    finer = Mesh(
        mesh.devices.reshape(8, 4, 2, mesh.shape["row"]), ("sec_0", "sec_1", "sec_2", "row")
    )
    in_specs = (P(SEC, "row", None), P(SEC, None, None), P(), P(), P(), P(), P(), P())
    out_specs = (P(SEC, "row", None), P(SEC, None, "row"))
    return jax.shard_map(
        on_device, mesh=finer, in_specs=in_specs, out_specs=out_specs, check_vma=False
    )
```

time: 511 us -> 178 us (0.35)
  waiting for transfers between devices: 168 us -> 25.7 us
  other arithmetic: 134 us -> 2.42 us
  matrix products: 73.7 us -> 0 us
  Pallas kernels: 0 us -> 35.7 us
  local copies, waits for them, and re-layouts: 21.5 us -> 10.7 us
  starting transfers between devices: 21.5 us -> 13.3 us
    psum x2 -> x0, waiting for transfers between devices: 131 us -> none  [truncate(): lax.psum(jnp.einsum('src,srj->scj', theta_block, ortho_block, precision=h...]
    another operation x17 -> x0, other arithmetic: 130 us -> none  [the longest x10 70.8 us: orthonormal(): factor = jnp.linalg.cholesky(gram_matrix)]
    dot_general x12 -> x0, matrix products: 71.7 us -> none  [the longest x2 31.8 us: truncate(): jnp.einsum('src,srj->scj', theta_block, ortho_block, precision=highest)]
    pallas_call x0 -> x2, Pallas kernels: none -> 35.7 us  [the longest x1 29.3 us: krylov_part(): pl.pallas_call(krylov_kernel, in_specs=[smem()] * 4 + [vmem()] * 5, out_s...]
    psum x4 -> x1, blocking collectives: 50.5 us -> 75 us  [on_device(): total = lax.psum(total[0, 0], SEC_ROW)]
    all_to_all x2 -> x0, waiting for transfers between devices: 23.8 us -> none  [the longest x1 23.8 us: summed_on_arrival(): lax.all_to_all(tiles, axis, split_axis=0, concat_axis=0, tiled=True)]
    all_to_all x2 -> x0, blocking collectives: 22.2 us -> none  [copy_for_each(): return lax.all_to_all(copies, axis, split_axis=0, concat_axis=0, tiled=True)]
    all_gather x0 -> x1, waiting for transfers between devices: none -> 19.9 us  [on_device(): left_all = lax.all_gather(left_theirs, 'row', axis=0, tiled=False)]
  transfers between devices with their start and end apart: 6 -> 3, of which waited for: 4 -> 2; matrix products, arithmetic and copies ran while one was open for 9% -> 2% of each run, Pallas kernels for 0% -> 4%
where the time goes in v1:
time: 178 us
  blocking collectives  75 us (42%)
  Pallas kernels  35.7 us (20%)
  waiting for transfers between devices  25.7 us (14%)
  between operations  14.8 us (8%)
  starting transfers between devices  13.3 us (7%)
  local copies, waits for them, and re-layouts  10.7 us (6%)
  other arithmetic  2.42 us (1%)
    psum x1, blocking collectives, on_device(): total = lax.psum(total[0, 0], SEC_ROW)  75 us
    pallas_call x1, Pallas kernels, krylov_part(): pl.pallas_call(krylov_kernel, in_specs=[smem()] * 4 + [vmem()] * 5, out_s...  29.3 us
    all_gather x1, waiting for transfers between devices, on_device(): left_all = lax.all_gather(left_theirs, 'row', axis=0, tiled=False)  19.9 us
    ppermute x2, starting transfers between devices, from_partner(): return lax.ppermute(value, axis, pairs)  13.3 us
    unnamed x20, local copies, waits for them, and re-layouts  9.08 us
    pallas_call x1, Pallas kernels, gate_right(): pl.pallas_call(right_kernel, grid=(slots,), in_specs=[smem(), slot((state...  6.47 us
    ppermute x2, waiting for transfers between devices, from_partner(): return lax.ppermute(value, axis, pairs)  5.71 us
  transfers between devices with their start and end apart: 3, of which 2 were waited for; matrix products, arithmetic and copies ran while one was open for 2% of the time, Pallas kernels for 4%

profile of v1, /device:TPU:1, one launch (start us, length us, event | category | flops | bytes accessed | tf_op | source)
XLA Modules:
  0.0 177.6 jit_solution(9417257114082832050)
XLA Ops:
  7.2 0.0 copy-start
  7.2 0.0 all-gather.3.cloned.1.call-start
  7.2 7.8 %collective-permute-start = (bf16[2,512,128]{2,1,0:T(8,128)(2,1)}, bf16[2,512,128]{2,1,0:T(8,128)(2,1)S(1)}, u32[]{:S(2)}, u32[]{:S(2)}) collective-permute-start(bf16[2,512,128]{2,1,0:T(8,128)(2,1)} %param.8), channel_id=1, source_target_pairs={{0,128},{4,132},{8,136},{12,140},{16,144},{20,148},{24,152},{28,15... | collective-permute-start | bytes 786440 | tf_op jit(solution)/shard_map/ppermute | solution.py:24
  15.1 5.7 %collective-permute-done = bf16[2,512,128]{2,1,0:T(8,128)(2,1)S(1)} collective-permute-done((bf16[2,512,128]{2,1,0:T(8,128)(2,1)}, bf16[2,512,128]{2,1,0:T(8,128)(2,1)S(1)}, u32[]{:S(2)}, u32[]{:S(2)}) %collective-permute-start) | collective-permute-done | bytes 262176 | tf_op jit(solution)/shard_map/ppermute | solution.py:24
  20.8 0.0 copy-start.9
  20.8 0.7 copy-done.9
  21.5 0.0 all-gather.3.cloned.1.call-update
  21.5 0.7 dynamic_slice.12.live_ref
  22.2 0.0 copy-done
  22.3 0.1 copy.11.start_ref
  22.4 0.7 dynamic_slice.13.kept_ref
  23.1 0.7 multiply_exponential_fusion.weight_ref
  23.9 0.0 copy-start.1
  23.9 1.2 copy-done.1
  25.1 0.0 copy-start.3
  25.1 0.8 copy-done.3
  25.9 0.0 copy-start.4
  25.9 0.8 copy-done.4
  26.6 6.5 %right_gate.1 = (f32[2,512,512]{2,1,0:T(8,128)S(1)}, bf16[2,512,512]{2,1,0:T(8,128)(2,1)S(1)}, bf16[4,2,256,256]{3,2,1,0:T(8,128)(2,1)S(1)}) custom-call(s32[1]{0:T(128)} %bitcast.row_ref, bf16[2,128,2048]{2,1,0:T(8,128)(2,1)S(1)} %copy-done.1, f32[64,16]{1,0:T(8,128)S(1)} %bitcast.7, f32[4,16,16]{2,1,0:T(8,128)S(1)} %copy-done.4), custom_call_target="tpu_custom_call" | custom-call | flops 10000000000 | bytes 6291456 | tf_op jit(solution)/shard_map/right_gate/pallas_call | solution.py:250
  33.1 0.0 copy-start.5
  33.1 1.0 copy-done.5
  34.1 0.0 copy-start.7
  34.1 1.0 copy-done.7
  35.1 19.9 %all-gather.3.cloned.1.call-done = bf16[8,512,128]{2,1,0:T(8,128)(2,1)} async-done(((bf16[2,512,128]{2,1,0:T(8,128)(2,1)}), bf16[8,512,128]{2,1,0:T(8,128)(2,1)}) %all-gather.3.cloned.1.call-update) | async-done | bytes 1048592 | tf_op jit(solution)/shard_map/all_gather | solution.py:312
  55.0 0.0 copy-start.2
  55.0 1.2 copy-done.2
  56.2 0.0 copy-start.6
  56.2 1.2 copy-done.6
  57.4 0.0 copy-start.8
  57.4 1.2 copy-done.8
  58.7 29.3 %krylov.1 = (bf16[2,512,128]{2,1,0:T(8,128)(2,1)S(1)}, f32[2,128,512]{2,1,0:T(8,128)S(1)}, f32[1,1]{1,0:T(1,128)}) custom-call(s32[1]{0:T(128)} %bitcast.row_ref, s32[2]{0:T(128)S(1)} %dynamic_slice.12.live_ref, s32[2]{0:T(128)S(1)} %dynamic_slice.13.kept_ref, f32[2]{0:T(128)S(1)} %multiply_exponential_fusion.weight_ref, ...), custom_call_target="tpu_custom_call" | custom-call | flops 20000000000 | bytes 6291456 | tf_op jit(solution)/shard_map/krylov/pallas_call | solution.py:278
  87.9 5.5 %collective-permute-start.1 = (bf16[2,512,128]{2,1,0:T(8,128)(2,1)S(1)}, bf16[2,512,128]{2,1,0:T(8,128)(2,1)S(1)}, u32[]{:S(2)}, u32[]{:S(2)}) collective-permute-start(bf16[2,512,128]{2,1,0:T(8,128)(2,1)S(1)} %get-tuple-element.11), channel_id=1, source_target_pairs={{0,128},{4,132},{8,136},{12,140},{16,144},{20,148},{24,152},{28,15... | collective-permute-start | bytes 786440 | tf_op jit(solution)/shard_map/ppermute | solution.py:24
  93.4 75.0 %psum.7 = f32[]{:T(128)} all-reduce(f32[]{:T(128)} %bitcast.4), channel_id=1, replica_groups=mesh['sec_0'=8,'sec_1'=4,'sec_2'=2,'row'=4] {'sec_0','sec_1','sec_2','row'}, use_global_device_ids=true, to_apply=%region_0.1 | all-reduce | flops 1 | bytes 8 | tf_op jit(solution)/shard_map/psum | solution.py:319
  169.1 0.9 broadcast_divide_fusion
  169.9 0.0 collective-permute-done.1
  169.9 0.8 convert_element_type.7
  (1 shorter events, 0.0 us)
Async XLA Ops:
  7.2 15.1 %copy-start = (s32[128,128]{1,0:T(8,128)S(1)}, s32[128,128]{1,0:T(8,128)}, u32[]{:S(2)}) copy-start(s32[128,128]{1,0:T(8,128)} %param.15) | copy-start | bytes 196612
  7.2 47.8 %all-gather.3.cloned.1.call-start = ((), (), s32[]{:S(2)}) async-start(), calls=%async_computation | async-start | bytes 1310720 | tf_op jit(solution)/shard_map/all_gather | solution.py:312
  7.2 13.5 %collective-permute-start = (bf16[2,512,128]{2,1,0:T(8,128)(2,1)}, bf16[2,512,128]{2,1,0:T(8,128)(2,1)S(1)}, u32[]{:S(2)}, u32[]{:S(2)}) collective-permute-start(bf16[2,512,128]{2,1,0:T(8,128)(2,1)} %param.8), channel_id=1, source_target_pairs={{0,128},{4,132},{8,136},{12,140},{16,144},{20,148},{24,152},{28,15... | collective-permute-start | bytes 786440 | tf_op jit(solution)/shard_map/ppermute | solution.py:24
  20.8 0.7 copy-start.9
  23.9 1.2 copy-start.1
  25.1 0.8 copy-start.3
  25.9 0.8 copy-start.4
  33.1 1.0 copy-start.5
  34.1 1.0 copy-start.7
  55.0 1.2 copy-start.2
  56.2 1.2 copy-start.6
  57.4 1.2 copy-start.8
  87.9 82.0 %collective-permute-start.1 = (bf16[2,512,128]{2,1,0:T(8,128)(2,1)S(1)}, bf16[2,512,128]{2,1,0:T(8,128)(2,1)S(1)}, u32[]{:S(2)}, u32[]{:S(2)}) collective-permute-start(bf16[2,512,128]{2,1,0:T(8,128)(2,1)S(1)} %get-tuple-element.11), channel_id=1, source_target_pairs={{0,128},{4,132},{8,136},{12,140},{16,144},{20,148},{24,152},{28,15... | collective-permute-start | bytes 786440 | tf_op jit(solution)/shard_map/ppermute | solution.py:24
Sparse Core Ops, SparseCore 0:
  21.6 33.3 all-gather.2

commit v2 on v1

--- a/solution.py
+++ b/solution.py
@@ -157,22 +157,24 @@
     local_ref[0] = gated[:, pl.ds(offset, local_cols)]
 
 
-def krylov_kernel(
-    row_ref, live_ref, kept_ref, weight_ref, left_ref, left_mix_ref, square_ref, local_ref, start_ref,
-    basis_ref, right_ref, total_ref,
-    gated, gram, block, image,
-):
-    chunks, slots, chunk_rows, states = left_ref.shape
+def krylov_kernel(row_ref, live_ref, kept_ref, weight_ref, *refs):
+    chunks = len(refs) - 12
+    left_refs = refs[:chunks]
+    (left_mix_ref, square_ref, local_ref, start_ref) = refs[chunks : chunks + 4]
+    (basis_ref, right_ref, total_ref) = refs[chunks + 4 : chunks + 7]
+    (gated, gram, block, image, final) = refs[chunks + 7 :]
+    slots, chunk_rows, states = left_refs[0].shape
     terms = left_mix_ref.shape[0]
     wide = left_mix_ref.shape[2]
     keep = block.shape[1]
     for s in range(slots):
         pieces = []
         for c in range(chunks):
-            turned = left_ref[c, s].T
+            turned = left_refs[c][s].T
+            first_row = lax.rem(row_ref[0] + (chunks - c), chunks) * chunk_rows
             for b in range(chunk_rows // wide):
                 lane = lax.broadcasted_iota(jnp.int32, (states, wide), 1)
-                alive = lane < live_ref[s] * SITE - (c * chunk_rows + b * wide)
+                alive = lane < live_ref[s] * SITE - (first_row + b * wide)
                 piece = turned[:, b * wide : (b + 1) * wide].astype(jnp.float32)
                 pieces.append(jnp.where(alive, piece, 0.0).astype(jnp.bfloat16))
         tall = jnp.concatenate(pieces, axis=0)
@@ -196,35 +198,32 @@
         for s in range(slots):
             image[s] = dot_over(inverses[s], images[s], 1, 0, highest)
 
-        @pl.when(index < ITERS)
-        def _():
-            for s in range(slots):
-                scale = weight_ref[s] * weight_ref[s]
-                block[s] = scale * dot_over(image[s], square_ref[s], 1, 0, highest)
-
         @pl.when(index == ITERS)
         def _():
             for s in range(slots):
-                block[s] = dot_over(inverses[s], block[s], 1, 0, highest)
-
+                final[s] = dot_over(inverses[s], block[s], 1, 0, highest)
+
+        for s in range(slots):
+            scale = weight_ref[s] * weight_ref[s]
+            block[s] = scale * dot_over(image[s], square_ref[s], 1, 0, highest)
         return carry
 
     lax.fori_loop(0, ITERS + 1, step, 0)
-    offset = pl.multiple_of(row_ref[0] * chunk_rows, chunk_rows)
     total = jnp.zeros((1, 1), jnp.float32)
     for s in range(slots):
-        mine = gated[s, :, pl.ds(offset, chunk_rows)]
-        high, low = two_parts(block[s])
+        keeps = lax.broadcasted_iota(jnp.int32, block.shape[1:], 0) < kept_ref[s]
+        squared = jnp.where(keeps, block[s] * image[s], 0.0)
+        total += jnp.sum(jnp.sum(squared, axis=0, keepdims=True), axis=1, keepdims=True)
+        high, low = two_parts(final[s])
+        mine = gated[s, :, :chunk_rows]
         basis = dot_over(high, mine, 1, 0) + dot_over(low, mine, 1, 0)
         keeps = lax.broadcasted_iota(jnp.int32, basis.shape, 0) < kept_ref[s]
         basis_ref[s] = jnp.where(keeps, basis, 0.0).T.astype(jnp.bfloat16)
         high, low = two_parts(image[s])
         part = dot_over(high, local_ref[s], 1, 0) + dot_over(low, local_ref[s], 1, 0)
         keeps = lax.broadcasted_iota(jnp.int32, part.shape, 0) < kept_ref[s]
-        part = jnp.where(keeps, part * weight_ref[s], 0.0)
-        right_ref[s] = part
-        total += jnp.sum(jnp.sum(part * part, axis=0, keepdims=True), axis=1, keepdims=True)
-    total_ref[...] = total
+        right_ref[s] = jnp.where(keeps, part * weight_ref[s], 0.0)
+    total_ref[...] = jnp.broadcast_to(total, total_ref.shape)
 
 
 def smem():
@@ -265,35 +264,36 @@
             pltpu.VMEM((2, terms * wide, wide), jnp.bfloat16),
             pltpu.VMEM((bond, cols), jnp.bfloat16),
         ],
-        compiler_params=pltpu.CompilerParams(vmem_limit_bytes=40 << 20),
+        compiler_params=pltpu.CompilerParams(vmem_limit_bytes=20 << 20),
         cost_estimate=pl.CostEstimate(flops=int(1e10), bytes_accessed=6 << 20, transcendentals=0),
         name="right_gate",
     )(row, right_block, right_ops.reshape(terms * SITE, SITE), left_ops)
 
 
-def krylov_part(row, live, kept, weight, left_all, left_mix, square, local, start):
-    chunks, slots, chunk_rows, states = left_all.shape
+def krylov_part(row, live, kept, weight, left_chunks, left_mix, square, local, start, peers):
+    slots, chunk_rows, states = left_chunks[0].shape
     bond, local_cols = local.shape[1:]
     keep = start.shape[1]
     return pl.pallas_call(
         krylov_kernel,
-        in_specs=[smem()] * 4 + [vmem()] * 5,
+        in_specs=[smem()] * 4 + [vmem()] * (len(left_chunks) + 4),
         out_specs=[vmem()] * 3,
         out_shape=[
             jax.ShapeDtypeStruct((slots, chunk_rows, keep), jnp.bfloat16),
             jax.ShapeDtypeStruct((slots, keep, local_cols), jnp.float32),
-            jax.ShapeDtypeStruct((1, 1), jnp.float32),
+            jax.ShapeDtypeStruct((peers, keep), jnp.float32),
         ],
         scratch_shapes=[
-            pltpu.VMEM((slots, bond, chunks * chunk_rows), jnp.bfloat16),
+            pltpu.VMEM((slots, bond, len(left_chunks) * chunk_rows), jnp.bfloat16),
             pltpu.VMEM((slots, bond, bond), jnp.float32),
             pltpu.VMEM((slots, keep, bond), jnp.float32),
             pltpu.VMEM((slots, keep, bond), jnp.float32),
-        ],
-        compiler_params=pltpu.CompilerParams(vmem_limit_bytes=48 << 20),
+            pltpu.VMEM((slots, keep, bond), jnp.float32),
+        ],
+        compiler_params=pltpu.CompilerParams(vmem_limit_bytes=24 << 20),
         cost_estimate=pl.CostEstimate(flops=int(2e10), bytes_accessed=6 << 20, transcendentals=0),
         name="krylov",
-    )(row, live, kept, weight, left_all, left_mix, square, local, start)
+    )(row, live, kept, weight, *left_chunks, left_mix, square, local, start)
 
 
 def on_device(left_block, right_block, left_ops, right_ops, charges, live_states, kept, start):
@@ -309,15 +309,22 @@
     weight = jnp.exp(-chemical * cut(charges, right_first).astype(jnp.float32))
     start_here = cut(start, left_first)[:, :, None]
     left_theirs = from_partner(left_block, SEC, top_bit)
-    left_all = lax.all_gather(left_theirs, "row", axis=0, tiled=False)
     local_cols = right_block.shape[2] // lax.axis_size("row")
     square, local, left_mix = gate_right(row, right_block, right_ops, left_ops, local_cols)
+    left_theirs, square = lax.optimization_barrier((left_theirs, square))
+    rows = lax.axis_size("row")
+    left_chunks = [left_theirs] + [
+        lax.ppermute(left_theirs, "row", [(i, (i + d) % rows) for i in range(rows)])
+        for d in range(1, rows)
+    ]
     basis, right_part, total = krylov_part(
-        row, live, kept_here, weight, left_all, left_mix, square, local, start_here
+        row, live, kept_here, weight, left_chunks, left_mix, square, local, start_here,
+        lax.axis_size(SEC),
     )
-    basis = from_partner(basis, SEC, top_bit).astype(jnp.float32)
-    total = lax.psum(total[0, 0], SEC_ROW)
-    return basis, right_part / jnp.sqrt(total)
+    basis = from_partner(basis, SEC, top_bit)
+    totals = lax.all_to_all(total, SEC, split_axis=0, concat_axis=0, tiled=True)
+    total = jnp.sum(totals[:, 0])
+    return basis.astype(jnp.float32), right_part / jnp.sqrt(total)
 
 
 def solution(mesh):

time: 178 us -> 98.9 us (0.56)
  the two profiles are of different devices: /device:TPU:1 before, /device:TPU:32 now
where the time goes in v2:
time: 98.9 us; the launch traced here: 98.5 us
  Pallas kernels  36.6 us (37%)
  starting transfers between devices  25.9 us (26%)
  waiting for transfers between devices  24 us (24%)
  local copies, waits for them, and re-layouts  8.17 us (8%)
  other arithmetic  2.38 us (2%)
  between operations  1.39 us (1%)
    pallas_call x1, Pallas kernels, krylov_part(): pl.pallas_call(krylov_kernel, in_specs=[smem()] * 4 + [vmem()] * (len(lef...  30.2 us
    ppermute x3, waiting for transfers between devices, on_device(): lax.ppermute(left_theirs, 'row', [(i, (i + d) % rows) for i in range(rows)])  12.2 us
    ppermute x2, starting transfers between devices, from_partner(): return lax.ppermute(value, axis, pairs)  11.1 us
    all_to_all x1, starting transfers between devices, on_device(): totals = lax.all_to_all(total, SEC, split_axis=0, concat_axis=0, tiled=True)  10.2 us
    ppermute x2, waiting for transfers between devices, from_partner(): return lax.ppermute(value, axis, pairs)  7.96 us
    unnamed x22, local copies, waits for them, and re-layouts  7.87 us
    pallas_call x1, Pallas kernels, gate_right(): pl.pallas_call(right_kernel, grid=(slots,), in_specs=[smem(), slot((state...  6.46 us
    ppermute x3, starting transfers between devices, on_device(): lax.ppermute(left_theirs, 'row', [(i, (i + d) % rows) for i in range(rows)])  4.62 us
  transfers between devices with their start and end apart: 6, of which 6 were waited for; matrix products, arithmetic and copies ran while one was open for 2% of the time, Pallas kernels for 7%

profile of v2, /device:TPU:32, one launch (start us, length us, event | category | flops | bytes accessed | tf_op | source)
XLA Modules:
  0.0 98.5 jit_solution(16820208995256040321)
XLA Ops:
  0.6 0.0 copy-start
  0.6 6.4 %collective-permute-start = (bf16[2,512,128]{2,1,0:T(8,128)(2,1)}, bf16[2,512,128]{2,1,0:T(8,128)(2,1)S(1)}, u32[]{:S(2)}, u32[]{:S(2)}) collective-permute-start(bf16[2,512,128]{2,1,0:T(8,128)(2,1)} %param.8), channel_id=1, source_target_pairs={{0,128},{4,132},{8,136},{12,140},{16,144},{20,148},{24,152},{28,15... | collective-permute-start | bytes 786440 | tf_op jit(solution)/shard_map/ppermute | solution.py:24
  7.0 0.0 copy-start.1
  7.0 1.2 %copy-done.1 = bf16[2,128,2048]{2,1,0:T(8,128)(2,1)S(1)} copy-done((bf16[2,128,2048]{2,1,0:T(8,128)(2,1)S(1)}, bf16[2,128,2048]{2,1,0:T(8,128)(2,1)}, u32[]{:S(2)}) %copy-start.1) | copy-done | bytes 1048600
  8.2 0.0 copy-start.2
  8.3 0.8 copy-done.2
  9.0 0.0 copy-start.3
  9.0 0.8 copy-done.3
  9.8 0.0 copy-start.8
  9.8 0.0 copy-start.9
  9.8 0.0 copy-start.10
  9.8 6.5 %right_gate.1 = (f32[2,512,512]{2,1,0:T(8,128)S(1)}, bf16[2,512,512]{2,1,0:T(8,128)(2,1)S(1)}, bf16[4,2,256,256]{3,2,1,0:T(8,128)(2,1)S(1)}) custom-call(s32[1]{0:T(128)} %bitcast.row_ref, bf16[2,128,2048]{2,1,0:T(8,128)(2,1)S(1)} %copy-done.1, f32[64,16]{1,0:T(8,128)S(1)} %bitcast.8, f32[4,16,16]{2,1,0:T(8,128)S(1)} %copy-done.3), custom_call_target="tpu_custom_call" | custom-call | flops 10000000000 | bytes 6291456 | tf_op jit(solution)/shard_map/right_gate/pallas_call | solution.py:249
  16.2 0.0 copy-start.4
  16.3 1.3 %copy-done.4 = f32[2,512,512]{2,1,0:T(8,128)} copy-done((f32[2,512,512]{2,1,0:T(8,128)}, f32[2,512,512]{2,1,0:T(8,128)S(1)}, u32[]{:S(2)}) %copy-start.4) | copy-done | bytes 2097176
  17.6 0.0 copy-start.6
  17.6 1.0 copy-done.6
  18.6 0.7 collective-permute-done.refs_0_
  19.2 3.0 %collective-permute-start.3 = (bf16[2,512,128]{2,1,0:T(8,128)(2,1)S(1)}, bf16[2,512,128]{2,1,0:T(8,128)(2,1)S(1)}, u32[]{:S(2)}, u32[]{:S(2)}) collective-permute-start(bf16[2,512,128]{2,1,0:T(8,128)(2,1)S(1)} %collective-permute-done.refs_0_), channel_id=1, source_target_pairs={{0,3},{1,0},{2,1},{3,2},{4,7},{5,4},{6,5},{7,6},{8,11},{9,8},{10,9... | collective-permute-start | bytes 786440 | tf_op jit(solution)/shard_map/ppermute | solution.py:317
  22.3 0.6 collective-permute-start.2
  22.9 1.0 collective-permute-start.1
  23.9 0.0 copy-done.8
  23.9 0.1 dynamic_slice.12.live_ref
  23.9 0.0 copy-done
  24.0 0.1 copy.11.refs_7_
  24.1 0.0 copy-done.9
  24.1 0.1 dynamic_slice.13.kept_ref
  24.2 0.0 copy-done.10
  24.2 0.1 multiply_exponential_fusion.weight_ref
  24.3 8.5 %collective-permute-done.3.refs_3_ = bf16[2,512,128]{2,1,0:T(8,128)(2,1)S(1)} collective-permute-done((bf16[2,512,128]{2,1,0:T(8,128)(2,1)S(1)}, bf16[2,512,128]{2,1,0:T(8,128)(2,1)S(1)}, u32[]{:S(2)}, u32[]{:S(2)}) %collective-permute-start.3) | collective-permute-done | bytes 262176 | tf_op jit(solution)/shard_map/ppermute | solution.py:317
  32.8 0.2 collective-permute-done.2.refs_2_
  33.0 3.5 %collective-permute-done.1.refs_1_ = bf16[2,512,128]{2,1,0:T(8,128)(2,1)S(1)} collective-permute-done((bf16[2,512,128]{2,1,0:T(8,128)(2,1)S(1)}, bf16[2,512,128]{2,1,0:T(8,128)(2,1)S(1)}, u32[]{:S(2)}, u32[]{:S(2)}) %collective-permute-start.1) | collective-permute-done | bytes 262176 | tf_op jit(solution)/shard_map/ppermute | solution.py:317
  36.5 0.0 copy-start.5
  36.5 1.6 %copy-done.5 = f32[2,512,512]{2,1,0:T(8,128)S(1)} copy-done((f32[2,512,512]{2,1,0:T(8,128)S(1)}, f32[2,512,512]{2,1,0:T(8,128)}, u32[]{:S(2)}) %copy-start.5) | copy-done | bytes 2097176
  38.1 0.0 copy-start.7
  38.1 1.2 %copy-done.7 = bf16[4,2,256,256]{3,2,1,0:T(8,128)(2,1)S(1)} copy-done((bf16[4,2,256,256]{3,2,1,0:T(8,128)(2,1)S(1)}, bf16[4,2,256,256]{3,2,1,0:T(8,128)(2,1)}, u32[]{:S(2)}) %copy-start.7) | copy-done | bytes 1048600
  39.3 30.2 %krylov.1 = (bf16[2,512,128]{2,1,0:T(8,128)(2,1)S(1)}, f32[2,128,512]{2,1,0:T(8,128)S(1)}, f32[64,128]{1,0:T(8,128)}) custom-call(s32[1]{0:T(128)} %bitcast.row_ref, s32[2]{0:T(128)S(1)} %dynamic_slice.12.live_ref, s32[2]{0:T(128)S(1)} %dynamic_slice.13.kept_ref, f32[2]{0:T(128)S(1)} %multiply_exponential_fusion.weight_ref, ...), custom_call_target="tpu_custom_call" | custom-call | flops 20000000000 | bytes 6291456 | tf_op jit(solution)/shard_map/krylov/pallas_call | solution.py:277
  69.5 10.2 %all-to-all-start = ((f32[64,1,128]{2,1,0:T(1,128)}), f32[64,1,128]{2,1,0:T(1,128)S(1)}, u32[]{:S(2)}, u32[]{:S(2)}) async-start(f32[64,1,128]{2,1,0:T(1,128)} %bitcast.4), calls=%async_computation | async-start | bytes 65536 | tf_op jit(solution)/shard_map/all_to_all | solution.py:325
  79.7 4.7 %collective-permute-start.4 = (bf16[2,512,128]{2,1,0:T(8,128)(2,1)S(1)}, bf16[2,512,128]{2,1,0:T(8,128)(2,1)S(1)}, u32[]{:S(2)}, u32[]{:S(2)}) collective-permute-start(bf16[2,512,128]{2,1,0:T(8,128)(2,1)S(1)} %get-tuple-element.15), channel_id=1, source_target_pairs={{0,128},{4,132},{8,136},{12,140},{16,144},{20,148},{24,152},{28,15... | collective-permute-start | bytes 786440 | tf_op jit(solution)/shard_map/ppermute | solution.py:24
  84.4 3.8 %all-to-all-done = f32[64,1,128]{2,1,0:T(1,128)S(1)} async-done(((f32[64,1,128]{2,1,0:T(1,128)}), f32[64,1,128]{2,1,0:T(1,128)S(1)}, u32[]{:S(2)}, u32[]{:S(2)}) %all-to-all-start) | async-done | bytes 32800 | tf_op jit(solution)/shard_map/all_to_all | solution.py:325
  88.3 0.6 slice_reduce_fusion
  89.6 0.9 broadcast_divide_fusion
  90.4 7.3 %collective-permute-done.4 = bf16[2,512,128]{2,1,0:T(8,128)(2,1)S(1)} collective-permute-done((bf16[2,512,128]{2,1,0:T(8,128)(2,1)S(1)}, bf16[2,512,128]{2,1,0:T(8,128)(2,1)S(1)}, u32[]{:S(2)}, u32[]{:S(2)}) %collective-permute-start.4) | collective-permute-done | bytes 262176 | tf_op jit(solution)/shard_map/ppermute | solution.py:24
  97.7 0.8 convert_element_type.7
  (1 shorter events, 0.0 us)
Async XLA Ops:
  0.6 23.3 %copy-start = (s32[128,128]{1,0:T(8,128)S(1)}, s32[128,128]{1,0:T(8,128)}, u32[]{:S(2)}) copy-start(s32[128,128]{1,0:T(8,128)} %param.15) | copy-start | bytes 196612
  0.6 18.6 %collective-permute-start = (bf16[2,512,128]{2,1,0:T(8,128)(2,1)}, bf16[2,512,128]{2,1,0:T(8,128)(2,1)S(1)}, u32[]{:S(2)}, u32[]{:S(2)}) collective-permute-start(bf16[2,512,128]{2,1,0:T(8,128)(2,1)} %param.8), channel_id=1, source_target_pairs={{0,128},{4,132},{8,136},{12,140},{16,144},{20,148},{24,152},{28,15... | collective-permute-start | bytes 786440 | tf_op jit(solution)/shard_map/ppermute | solution.py:24
  7.0 1.2 %copy-start.1 = (bf16[2,128,2048]{2,1,0:T(8,128)(2,1)S(1)}, bf16[2,128,2048]{2,1,0:T(8,128)(2,1)}, u32[]{:S(2)}) copy-start(bf16[2,128,2048]{2,1,0:T(8,128)(2,1)} %right_ref.1) | copy-start | bytes 3145732
  8.2 0.8 copy-start.2
  9.0 0.8 copy-start.3
  9.8 14.1 %copy-start.8 = (s32[128]{0:T(128)S(1)}, s32[128]{0:T(128)}, u32[]{:S(2)}) copy-start(s32[128]{0:T(128)} %param.13) | copy-start | bytes 1540
  9.8 14.3 %copy-start.9 = (s32[128]{0:T(128)S(1)}, s32[128]{0:T(128)}, u32[]{:S(2)}) copy-start(s32[128]{0:T(128)} %param.14) | copy-start | bytes 1540
  9.8 14.4 %copy-start.10 = (s32[128]{0:T(128)S(1)}, s32[128]{0:T(128)}, u32[]{:S(2)}) copy-start(s32[128]{0:T(128)} %param.12) | copy-start | bytes 1540
  16.2 1.3 %copy-start.4 = (f32[2,512,512]{2,1,0:T(8,128)}, f32[2,512,512]{2,1,0:T(8,128)S(1)}, u32[]{:S(2)}) copy-start(f32[2,512,512]{2,1,0:T(8,128)S(1)} %get-tuple-element.13.refs_5_) | copy-start | bytes 6291460
  17.6 1.0 copy-start.6
  19.2 13.6 %collective-permute-start.3 = (bf16[2,512,128]{2,1,0:T(8,128)(2,1)S(1)}, bf16[2,512,128]{2,1,0:T(8,128)(2,1)S(1)}, u32[]{:S(2)}, u32[]{:S(2)}) collective-permute-start(bf16[2,512,128]{2,1,0:T(8,128)(2,1)S(1)} %collective-permute-done.refs_0_), channel_id=1, source_target_pairs={{0,3},{1,0},{2,1},{3,2},{4,7},{5,4},{6,5},{7,6},{8,11},{9,8},{10,9... | collective-permute-start | bytes 786440 | tf_op jit(solution)/shard_map/ppermute | solution.py:317
  22.3 10.7 %collective-permute-start.2 = (bf16[2,512,128]{2,1,0:T(8,128)(2,1)S(1)}, bf16[2,512,128]{2,1,0:T(8,128)(2,1)S(1)}, u32[]{:S(2)}, u32[]{:S(2)}) collective-permute-start(bf16[2,512,128]{2,1,0:T(8,128)(2,1)S(1)} %collective-permute-done.refs_0_), channel_id=1, source_target_pairs={{0,2},{1,3},{2,0},{3,1},{4,6},{5,7},{6,4},{7,5},{8,10},{9,11},{10,... | collective-permute-start | bytes 786440 | tf_op jit(solution)/shard_map/ppermute | solution.py:317
  22.9 13.6 %collective-permute-start.1 = (bf16[2,512,128]{2,1,0:T(8,128)(2,1)S(1)}, bf16[2,512,128]{2,1,0:T(8,128)(2,1)S(1)}, u32[]{:S(2)}, u32[]{:S(2)}) collective-permute-start(bf16[2,512,128]{2,1,0:T(8,128)(2,1)S(1)} %collective-permute-done.refs_0_), channel_id=1, source_target_pairs={{0,1},{1,2},{2,3},{3,0},{4,5},{5,6},{6,7},{7,4},{8,9},{9,10},{10,1... | collective-permute-start | bytes 786440 | tf_op jit(solution)/shard_map/ppermute | solution.py:317
  36.5 1.6 %copy-start.5 = (f32[2,512,512]{2,1,0:T(8,128)S(1)}, f32[2,512,512]{2,1,0:T(8,128)}, u32[]{:S(2)}) copy-start(f32[2,512,512]{2,1,0:T(8,128)} %copy-done.4) | copy-start | bytes 6291460
  38.1 1.2 %copy-start.7 = (bf16[4,2,256,256]{3,2,1,0:T(8,128)(2,1)S(1)}, bf16[4,2,256,256]{3,2,1,0:T(8,128)(2,1)}, u32[]{:S(2)}) copy-start(bf16[4,2,256,256]{3,2,1,0:T(8,128)(2,1)} %copy-done.6) | copy-start | bytes 3145732
  69.5 18.8 %all-to-all-start = ((f32[64,1,128]{2,1,0:T(1,128)}), f32[64,1,128]{2,1,0:T(1,128)S(1)}, u32[]{:S(2)}, u32[]{:S(2)}) async-start(f32[64,1,128]{2,1,0:T(1,128)} %bitcast.4), calls=%async_computation | async-start | bytes 65536 | tf_op jit(solution)/shard_map/all_to_all | solution.py:325
  79.7 18.0 %collective-permute-start.4 = (bf16[2,512,128]{2,1,0:T(8,128)(2,1)S(1)}, bf16[2,512,128]{2,1,0:T(8,128)(2,1)S(1)}, u32[]{:S(2)}, u32[]{:S(2)}) collective-permute-start(bf16[2,512,128]{2,1,0:T(8,128)(2,1)S(1)} %get-tuple-element.15), channel_id=1, source_target_pairs={{0,128},{4,132},{8,136},{12,140},{16,144},{20,148},{24,152},{28,15... | collective-permute-start | bytes 786440 | tf_op jit(solution)/shard_map/ppermute | solution.py:24

commit v3 on v2

v3 whole, which is shorter than its diff:
```python
import functools

import jax
import jax.numpy as jnp
from jax import lax
from jax.experimental import pallas as pl
from jax.experimental.pallas import tpu as pltpu
from jax.sharding import Mesh
from jax.sharding import PartitionSpec as P

SITE = 16
ITERS = 2
SEC = ("sec_0", "sec_1", "sec_2")
SEC_ROW = ("sec_0", "sec_1", "sec_2", "row")
WINDOW = 32

chemical = 0.4
highest = lax.Precision.HIGHEST


def from_partner(value, axis, distance):
    mask = 2**distance
    pairs = [(source, source ^ mask) for source in range(lax.axis_size(axis))]
    return lax.ppermute(value, axis, pairs)


def dot_over(left, right, left_dim, right_dim, precision=None):
    return lax.dot_general(
        left,
        right,
        (((left_dim,), (right_dim,)), ((), ())),
        precision=precision,
        preferred_element_type=jnp.float32,
    )


def two_parts(values):
    high = values.astype(jnp.bfloat16)
    low = (values - high.astype(jnp.float32)).astype(jnp.bfloat16)
    return high, low


def one_hot(shape, row_key, col_key):
    rows = lax.broadcasted_iota(jnp.int32, shape, 0)
    cols = lax.broadcasted_iota(jnp.int32, shape, 1)
    return row_key(rows) == col_key(cols)


def as_weights(mask):
    return jnp.where(mask, 1.0, 0.0).astype(jnp.bfloat16)


def lower_inverse(grams, window):
    n = grams[0].shape[0]
    lane = lax.broadcasted_iota(jnp.int32, (8, n), 1)
    sub = lax.broadcasted_iota(jnp.int32, (8, n), 0)
    rows = [[g[8 * q : 8 * q + 8, :] for q in range(n // 8)] for g in grams]
    span = window // 8
    for first in range(0, n // 8, span):
        last = first + span
        for q in range(first, last):
            k = 8 * q
            inside = (lane >= k) & (lane < k + 8)
            unit = (lane - k == sub).astype(jnp.float32)
            for mat in rows:
                cols = {
                    r: [jnp.broadcast_to(mat[r][:, k + m : k + m + 1], (8, n)) for m in range(8)]
                    for r in range(q, last)
                }
                for r in range(q, last):
                    mat[r] = jnp.where(inside, unit if r == q else 0.0, mat[r])
                for m in range(8):
                    pivot = jnp.broadcast_to(cols[q][m][m : m + 1, :], (8, n))
                    scale = lax.rsqrt(pivot)
                    head = jnp.broadcast_to(mat[q][m : m + 1, :], (8, n)) * scale
                    below = {r: cols[r][m] * scale for r in range(q, last)}
                    below[q] = jnp.where(sub > m, below[q], 0.0)
                    for j in range(m + 1, 8):
                        weight = jnp.broadcast_to(below[q][j : j + 1, :], (8, n))
                        for r in range(q, last):
                            cols[r][j] = cols[r][j] - below[r] * weight
                    for r in range(q, last):
                        mat[r] = mat[r] - below[r] * head
                    mat[q] = jnp.where(sub == m, head, mat[q])
        if last < n // 8:
            inblock = (lane >= 8 * first) & (lane < 8 * last)
            for mat in rows:
                panel = jnp.concatenate(mat[first:last], axis=0)
                panel_row = lax.broadcasted_iota(jnp.int32, panel.shape, 0) + 8 * first
                panel_lane = lax.broadcasted_iota(jnp.int32, panel.shape, 1)
                panel = jnp.where((panel_lane > panel_row) & (panel_lane < 8 * last), 0.0, panel)
                update = dot_over(panel, panel, 0, 0, highest)
                for r in range(last, n // 8):
                    mat[r] = jnp.where(inblock, 0.0, mat[r]) - update[8 * r : 8 * r + 8, :]
    full_row = lax.broadcasted_iota(jnp.int32, (n, n), 0)
    full_col = lax.broadcasted_iota(jnp.int32, (n, n), 1)
    return [jnp.where(full_col <= full_row, jnp.concatenate(mat, axis=0), 0.0) for mat in rows]


def three_pass(left, right, right_dim):
    (left_high, left_low), (right_high, right_low) = left, right
    return (
        dot_over(left_high, right_high, 1, right_dim)
        + dot_over(left_high, right_low, 1, right_dim)
        + dot_over(left_low, right_high, 1, right_dim)
    )


def right_kernel(
    slot, row_ref, right_ref, right_ops_ref, high_ref, low_ref, local_ref, right_mix, gated, right, sem
):
    states = right.shape[0]
    terms = gated.shape[0] // states
    wide = SITE * SITE
    local_cols = local_ref.shape[1]
    fetch = pltpu.make_async_copy(right_ref.at[slot], right, sem)
    fetch.start()
    spread = as_weights(one_hot((terms * wide, terms * SITE), lambda r: r // SITE, lambda c: c))
    widen = as_weights(one_hot((SITE, wide), lambda r: r, lambda c: c // SITE))
    same = one_hot((terms * wide, wide), lambda r: r % SITE, lambda c: c % SITE)
    for part, piece in enumerate(two_parts(right_ops_ref[...])):
        tall = dot_over(spread, piece, 1, 0).astype(jnp.bfloat16)
        full = dot_over(tall, widen, 1, 0)
        right_mix[:, part * wide : (part + 1) * wide] = jnp.where(same, full, 0.0).astype(
            jnp.bfloat16
        )
    fetch.wait()
    for pair in range(states // (2 * SITE)):
        base = pair * 2 * SITE
        halves = [
            jnp.concatenate(
                [
                    right[base + h * SITE : base + (h + 1) * SITE, j * states : (j + 1) * states]
                    for j in range(SITE)
                ],
                axis=0,
            )
            for h in range(2)
        ]
        block = jnp.concatenate(halves, axis=1)
        block = jnp.concatenate([block, block], axis=0)
        for t in range(terms):
            mixed = dot_over(right_mix[t * wide : (t + 1) * wide, :], block, 1, 0)
            mixed = mixed.astype(jnp.bfloat16)
            for h in range(2):
                for i in range(SITE):
                    gated[
                        t * states + base + h * SITE : t * states + base + (h + 1) * SITE,
                        i * states : (i + 1) * states,
                    ] = mixed[i * SITE : (i + 1) * SITE, h * states : (h + 1) * states]
    high_ref[...], low_ref[...] = two_parts(dot_over(gated[...], gated[...], 1, 1))
    offset = pl.multiple_of(row_ref[0] * local_cols, local_cols)
    local_ref[...] = gated[:, pl.ds(offset, local_cols)]


def gate_chunk(left_ref, slot, live, first_row, left_mix_ref, out_ref, out_first):
    chunk_rows, states = left_ref.shape[1:]
    terms, _, wide = left_mix_ref.shape
    turned = left_ref[slot].T
    pieces = []
    for b in range(chunk_rows // wide):
        lane = lax.broadcasted_iota(jnp.int32, (states, wide), 1)
        alive = lane < live * SITE - (first_row + b * wide)
        piece = turned[:, b * wide : (b + 1) * wide].astype(jnp.float32)
        pieces.append(jnp.where(alive, piece, 0.0).astype(jnp.bfloat16))
    tall = jnp.concatenate(pieces, axis=0)
    tall = jnp.concatenate([tall, tall], axis=1)
    for t in range(terms):
        mixed = dot_over(tall, left_mix_ref[t], 1, 0).astype(jnp.bfloat16)
        for b in range(len(pieces)):
            out_ref[
                slot, t * states : (t + 1) * states, out_first + b * wide : out_first + (b + 1) * wide
            ] = mixed[b * states : (b + 1) * states, :]


def own_kernel(row_ref, live_ref, left_ref, left_ops_ref, gated_ref, gram_ref, left_mix_ref):
    terms = left_ops_ref.shape[0]
    wide = SITE * SITE
    tall_pick = as_weights(one_hot((wide, SITE), lambda r: r % SITE, lambda c: c))
    wide_pick = as_weights(one_hot((SITE, wide), lambda r: r, lambda c: c % SITE))
    group = one_hot((wide, wide), lambda r: r // SITE, lambda c: c // SITE)
    for t in range(terms):
        for part, piece in enumerate(two_parts(left_ops_ref[t])):
            tall = dot_over(tall_pick, piece, 1, 1).astype(jnp.bfloat16)
            full = dot_over(tall, wide_pick, 1, 0)
            left_mix_ref[t, part * wide : (part + 1) * wide, :] = jnp.where(
                group, full, 0.0
            ).astype(jnp.bfloat16)
    slots, chunk_rows = left_ref.shape[:2]
    for s in range(slots):
        gate_chunk(left_ref, s, live_ref[s], row_ref[0] * chunk_rows, left_mix_ref, gated_ref, 0)
        gram_ref[s] = dot_over(gated_ref[s], gated_ref[s], 1, 1)


def krylov_kernel(row_ref, live_ref, kept_ref, weight_ref, *refs):
    chunks = len(refs) - 15
    left_refs = refs[:chunks]
    (left_mix_ref, own_ref, own_gram_ref, start_ref) = refs[chunks : chunks + 4]
    square_refs = refs[chunks + 4 : chunks + 8]
    (basis_ref, image_ref) = refs[chunks + 8 : chunks + 10]
    (gated, gram_high, gram_low, block, final) = refs[chunks + 10 :]
    slots, chunk_rows, states = left_refs[0].shape
    bond = own_ref.shape[1]
    keep = block.shape[1]
    for s in range(slots):
        for c in range(chunks):
            first_row = lax.rem(row_ref[0] + (chunks - c), chunks + 1) * chunk_rows
            gate_chunk(left_refs[c], s, live_ref[s], first_row, left_mix_ref, gated, c * chunk_rows)
        gram = own_gram_ref[s] + dot_over(gated[s], gated[s], 1, 1)
        gram_high[s], gram_low[s] = two_parts(gram)
        spots = lax.broadcasted_iota(jnp.int32, (keep, bond), 1)
        block[s] = jnp.where(spots == start_ref[s], 1.0, 0.0)

    def step(index, carry):
        images = [
            three_pass(two_parts(block[s]), (gram_high[s], gram_low[s]), 0) for s in range(slots)
        ]
        grams = [dot_over(images[s], block[s], 1, 1, highest) for s in range(slots)]
        inverses = lower_inverse(grams, WINDOW)
        for s in range(slots):
            image_ref[s] = three_pass(two_parts(inverses[s]), two_parts(images[s]), 0)

        @pl.when(index == ITERS)
        def _():
            for s in range(slots):
                final[s] = three_pass(two_parts(inverses[s]), two_parts(block[s]), 0)

        @pl.when(index < ITERS)
        def _():
            for s in range(slots):
                squares = (square_refs[2 * s][...], square_refs[2 * s + 1][...])
                scale = weight_ref[s] * weight_ref[s]
                block[s] = scale * three_pass(two_parts(image_ref[s]), squares, 0)

        return carry

    lax.fori_loop(0, ITERS + 1, step, 0)
    for s in range(slots):
        high, low = two_parts(final[s])
        basis = dot_over(high, own_ref[s], 1, 0) + dot_over(low, own_ref[s], 1, 0)
        keeps = lax.broadcasted_iota(jnp.int32, basis.shape, 0) < kept_ref[s]
        basis_ref[s] = jnp.where(keeps, basis, 0.0).T.astype(jnp.bfloat16)


def truncate_kernel(kept_ref, weight_ref, image_ref, *refs):
    square_refs, local_refs, (right_ref, total_ref) = refs[:4], refs[4:6], refs[6:]
    total = jnp.zeros((1, 1), jnp.float32)
    for s in range(image_ref.shape[0]):
        image = image_ref[s]
        high, low = two_parts(image)
        keeps = lax.broadcasted_iota(jnp.int32, image.shape, 0) < kept_ref[s]
        scale = weight_ref[s] * weight_ref[s]
        squares = (square_refs[2 * s][...], square_refs[2 * s + 1][...])
        squared = scale * three_pass((high, low), squares, 0) * image
        squared = jnp.where(keeps, squared, 0.0)
        total += jnp.sum(jnp.sum(squared, axis=0, keepdims=True), axis=1, keepdims=True)
        local = local_refs[s][...]
        part = dot_over(high, local, 1, 0) + dot_over(low, local, 1, 0)
        keeps = lax.broadcasted_iota(jnp.int32, part.shape, 0) < kept_ref[s]
        right_ref[s] = jnp.where(keeps, part * weight_ref[s], 0.0)
    total_ref[...] = jnp.broadcast_to(total, total_ref.shape)


def scale_kernel(totals_ref, part_ref, right_ref):
    total = jnp.sum(totals_ref[...], axis=0, keepdims=True)[:, :1]
    for s in range(part_ref.shape[0]):
        right_ref[s] = part_ref[s] * (1.0 / jnp.sqrt(total))


def smem():
    return pl.BlockSpec(memory_space=pltpu.SMEM)


def vmem():
    return pl.BlockSpec(memory_space=pltpu.VMEM)


def shape_of(shape, dtype):
    return jax.ShapeDtypeStruct(shape, dtype)


def kernel_options(mebibytes, flops):
    return dict(
        compiler_params=pltpu.CompilerParams(vmem_limit_bytes=mebibytes << 20),
        cost_estimate=pl.CostEstimate(flops=int(flops), bytes_accessed=2 << 20, transcendentals=0),
    )


def gate_right(slot, row, right_block, right_ops, local_cols):
    _, states, cols = right_block.shape
    terms = right_ops.shape[0]
    bond, wide = terms * states, SITE * SITE
    return pl.pallas_call(
        functools.partial(right_kernel, slot),
        in_specs=[smem(), pl.BlockSpec(memory_space=pltpu.HBM), vmem()],
        out_specs=[vmem()] * 3,
        out_shape=[
            shape_of((bond, bond), jnp.bfloat16),
            shape_of((bond, bond), jnp.bfloat16),
            shape_of((bond, local_cols), jnp.bfloat16),
        ],
        scratch_shapes=[
            pltpu.VMEM((terms * wide, 2 * wide), jnp.bfloat16),
            pltpu.VMEM((bond, cols), jnp.bfloat16),
            pltpu.VMEM((states, cols), jnp.bfloat16),
            pltpu.SemaphoreType.DMA,
        ],
        name="right_gate",
        **kernel_options(12, 4e9),
    )(row, right_block, right_ops.reshape(terms * SITE, SITE))


def gate_own(row, live, left, left_ops):
    slots, chunk_rows, states = left.shape
    terms = left_ops.shape[0]
    bond, wide = terms * states, SITE * SITE
    return pl.pallas_call(
        own_kernel,
        in_specs=[smem()] * 2 + [vmem()] * 2,
        out_specs=[vmem()] * 3,
        out_shape=[
            shape_of((slots, bond, chunk_rows), jnp.bfloat16),
            shape_of((slots, bond, bond), jnp.float32),
            shape_of((terms, 2 * wide, wide), jnp.bfloat16),
        ],
        name="own_gate",
        **kernel_options(8, 2e9),
    )(row, live, left, left_ops)


def krylov_part(row, live, kept, weight, left_chunks, left_mix, own, own_gram, start, squares):
    slots, chunk_rows, states = left_chunks[0].shape
    bond = own.shape[1]
    keep = start.shape[1]
    return pl.pallas_call(
        krylov_kernel,
        in_specs=[smem()] * 4 + [vmem()] * (len(left_chunks) + 4 + len(squares)),
        out_specs=[vmem()] * 2,
        out_shape=[
            shape_of((slots, chunk_rows, keep), jnp.bfloat16),
            shape_of((slots, keep, bond), jnp.float32),
        ],
        scratch_shapes=[
            pltpu.VMEM((slots, bond, len(left_chunks) * chunk_rows), jnp.bfloat16),
            pltpu.VMEM((slots, bond, bond), jnp.bfloat16),
            pltpu.VMEM((slots, bond, bond), jnp.bfloat16),
            pltpu.VMEM((slots, keep, bond), jnp.float32),
            pltpu.VMEM((slots, keep, bond), jnp.float32),
        ],
        name="krylov",
        **kernel_options(16, 2e10),
    )(row, live, kept, weight, *left_chunks, left_mix, own, own_gram, start, *squares)


def truncated(kept, weight, image, squares, locals_, peers):
    slots, keep, _ = image.shape
    local_cols = locals_[0].shape[1]
    return pl.pallas_call(
        truncate_kernel,
        in_specs=[smem()] * 2 + [vmem()] * (1 + len(squares) + len(locals_)),
        out_specs=[vmem()] * 2,
        out_shape=[
            shape_of((slots, keep, local_cols), jnp.float32),
            shape_of((peers, keep), jnp.float32),
        ],
        name="truncate",
        **kernel_options(8, 2e9),
    )(kept, weight, image, *squares, *locals_)


def scaled(totals, part):
    return pl.pallas_call(
        scale_kernel,
        in_specs=[vmem()] * 2,
        out_specs=vmem(),
        out_shape=shape_of(part.shape, jnp.float32),
        name="scale",
        **kernel_options(4, 1e6),
    )(totals, part)


def on_device(left_block, right_block, left_ops, right_ops, charges, live_states, kept, start):
    slots = left_block.shape[0]
    sectors = slots * lax.axis_size(SEC)
    top_bit = lax.axis_size(SEC).bit_length() - 2
    right_first = lax.axis_index(SEC) * slots
    left_first = (right_first + sectors // 2) % sectors
    cut = lambda table, first: lax.dynamic_slice_in_dim(table, first, slots, 0)
    row = lax.axis_index("row").astype(jnp.int32).reshape(1)
    live = cut(live_states, left_first)
    kept_here = cut(kept, right_first)
    weight = jnp.exp(-chemical * cut(charges, right_first).astype(jnp.float32))
    start_here = cut(start, left_first)[:, :, None]
    local_cols = right_block.shape[2] // lax.axis_size("row")
    left_theirs = from_partner(left_block, SEC, top_bit)
    first = list(gate_right(0, row, right_block, right_ops, local_cols))
    left_theirs, first[0], row_later = lax.optimization_barrier((left_theirs, first[0], row))
    rows = lax.axis_size("row")
    left_chunks = [
        lax.ppermute(left_theirs, "row", [(i, (i + d) % rows) for i in range(rows)])
        for d in range(1, rows)
    ]
    second = gate_right(1, row_later, right_block, right_ops, local_cols)
    own, own_gram, left_mix = gate_own(row_later, live, left_theirs, left_ops)
    squares = (*first[:2], *second[:2])
    basis, image = krylov_part(
        row, live, kept_here, weight, left_chunks, left_mix, own, own_gram, start_here, squares
    )
    basis = from_partner(basis, SEC, top_bit)
    right_part, total = truncated(
        kept_here, weight, image, squares, (first[2], second[2]), lax.axis_size(SEC)
    )
    totals = lax.all_to_all(total, SEC, split_axis=0, concat_axis=0, tiled=True)
    return basis.astype(jnp.float32), scaled(totals, right_part)


def solution(mesh):
    finer = Mesh(
        mesh.devices.reshape(8, 4, 2, mesh.shape["row"]), ("sec_0", "sec_1", "sec_2", "row")
    )
    in_specs = (P(SEC, "row", None), P(SEC, None, None), P(), P(), P(), P(), P(), P())
    out_specs = (P(SEC, "row", None), P(SEC, None, "row"))
    return jax.shard_map(
        on_device, mesh=finer, in_specs=in_specs, out_specs=out_specs, check_vma=False
    )
```

time: 98.9 us -> 85.9 us (0.87)
  the two profiles are of different devices: /device:TPU:32 before, /device:TPU:1 now
where the time goes in v3:
time: 85.9 us; the launch traced here: 85.7 us
  Pallas kernels  35.1 us (41%)
  blocking collectives  24.8 us (29%)
  starting transfers between devices  11.8 us (14%)
  waiting for transfers between devices  8.08 us (9%)
  local copies, waits for them, and re-layouts  3.6 us (4%)
  other arithmetic  1.56 us (2%)
    all_to_all x1, blocking collectives, on_device(): totals = lax.all_to_all(total, SEC, split_axis=0, concat_axis=0, tiled=True)  24.8 us
    pallas_call x1, Pallas kernels, krylov_part(): pl.pallas_call(krylov_kernel, in_specs=[smem()] * 4 + [vmem()] * (len(lef...  23.2 us
    ppermute x3, waiting for transfers between devices, on_device(): lax.ppermute(left_theirs, 'row', [(i, (i + d) % rows) for i in range(rows)])  8.07 us
    ppermute x2, starting transfers between devices, from_partner(): return lax.ppermute(value, axis, pairs)  7.92 us
    pallas_call x2, Pallas kernels, gate_right(): pl.pallas_call(functools.partial(right_kernel, slot), in_specs=[smem(), p...  6.84 us
    ppermute x3, starting transfers between devices, on_device(): lax.ppermute(left_theirs, 'row', [(i, (i + d) % rows) for i in range(rows)])  3.86 us
    pallas_call x1, Pallas kernels, gate_own(): pl.pallas_call(own_kernel, in_specs=[smem()] * 2 + [vmem()] * 2, out_spec...  2.78 us
    unnamed x8, local copies, waits for them, and re-layouts  2 us
  transfers between devices with their start and end apart: 5, of which 2 were waited for; matrix products, arithmetic and copies ran while one was open for 3% of the time, Pallas kernels for 14%

profile of v3, /device:TPU:1, one launch (start us, length us, event | category | flops | bytes accessed | tf_op | source)
XLA Modules:
  0.0 85.7 jit_solution(8470881653679885161)
XLA Ops:
  0.6 0.0 copy-start
  0.6 7.8 %collective-permute-start = (bf16[2,512,128]{2,1,0:T(8,128)(2,1)}, bf16[2,512,128]{2,1,0:T(8,128)(2,1)S(1)}, u32[]{:S(2)}, u32[]{:S(2)}) collective-permute-start(bf16[2,512,128]{2,1,0:T(8,128)(2,1)} %param.8), channel_id=1, source_target_pairs={{0,128},{4,132},{8,136},{12,140},{16,144},{20,148},{24,152},{28,15... | collective-permute-start | bytes 786440 | tf_op jit(solution)/shard_map/ppermute | solution.py:24
  8.5 0.7 multiply_exponential_fusion.weight_ref
  9.2 0.7 dynamic_slice.13.kept_ref
  9.9 0.7 dynamic_slice.12.live_ref
  10.7 0.0 copy-done
  10.7 0.1 copy.11.refs_6_
  10.8 0.0 copy-start.1
  10.8 1.2 %copy-done.1 = bf16[2,128,2048]{2,1,0:T(8,128)(2,1)S(1)} copy-done((bf16[2,128,2048]{2,1,0:T(8,128)(2,1)S(1)}, bf16[2,128,2048]{2,1,0:T(8,128)(2,1)}, u32[]{:S(2)}) %copy-start.1) | copy-done | bytes 1048600
  12.0 0.0 copy-start.2
  12.1 0.8 copy-done.2
  12.8 3.4 %right_gate.2 = (bf16[512,512]{1,0:T(8,128)(2,1)S(1)}, bf16[512,512]{1,0:T(8,128)(2,1)S(1)}, bf16[512,512]{1,0:T(8,128)(2,1)S(1)}) custom-call(s32[1]{0:T(128)} %bitcast.row_ref, bf16[2,128,2048]{2,1,0:T(8,128)(2,1)S(1)} %copy-done.1, f32[64,16]{1,0:T(8,128)S(1)} %bitcast.10), custom_call_target="tpu_custom_call" | custom-call | flops 4000000000 | bytes 2097152 | tf_op jit(solution)/shard_map/right_gate/pallas_call | solution.py:293
  16.2 0.0 collective-permute-done.left_ref
  16.2 0.0 copy-start.3
  16.3 2.8 %collective-permute-start.3 = (bf16[2,512,128]{2,1,0:T(8,128)(2,1)S(1)}, bf16[2,512,128]{2,1,0:T(8,128)(2,1)S(1)}, u32[]{:S(2)}, u32[]{:S(2)}) collective-permute-start(bf16[2,512,128]{2,1,0:T(8,128)(2,1)S(1)} %collective-permute-done.left_ref), channel_id=1, source_target_pairs={{0,3},{1,0},{2,1},{3,2},{4,7},{5,4},{6,5},{7,6},{8,11},{9,8},{10,9... | collective-permute-start | bytes 786440 | tf_op jit(solution)/shard_map/ppermute | solution.py:400
  19.1 0.3 collective-permute-start.2
  19.4 0.7 collective-permute-start.1
  20.1 3.4 %right_gate.3 = (bf16[512,512]{1,0:T(8,128)(2,1)S(1)}, bf16[512,512]{1,0:T(8,128)(2,1)S(1)}, bf16[512,512]{1,0:T(8,128)(2,1)S(1)}) custom-call(s32[1]{0:T(128)} %bitcast.row_ref, bf16[2,128,2048]{2,1,0:T(8,128)(2,1)S(1)} %copy-done.1, f32[64,16]{1,0:T(8,128)S(1)} %bitcast.11), custom_call_target="tpu_custom_call" | custom-call | flops 4000000000 | bytes 2097152 | tf_op jit(solution)/shard_map/right_gate/pallas_call | solution.py:293
  23.5 0.0 copy-done.3
  23.6 2.8 %own_gate.1 = (bf16[2,512,512]{2,1,0:T(8,128)(2,1)S(1)}, f32[2,512,512]{2,1,0:T(8,128)S(1)}, bf16[4,512,256]{2,1,0:T(8,128)(2,1)S(1)}) custom-call(s32[1]{0:T(128)} %bitcast.row_ref, s32[2]{0:T(128)S(1)} %dynamic_slice.12.live_ref, bf16[2,512,128]{2,1,0:T(8,128)(2,1)S(1)} %collective-permute-done.left_ref, f32[4,16,16]{2,1,0:T(8,128)S(1)} %copy-done.3), custom_call_target="tpu_custom_call" | custom-call | flops 2000000000 | bytes 2097152 | tf_op jit(solution)/shard_map/own_gate/pallas_call | solution.py:317
  26.3 0.0 collective-permute-done.3.refs_2_
  26.4 0.9 collective-permute-done.2.refs_1_
  27.2 7.2 %collective-permute-done.1.refs_0_ = bf16[2,512,128]{2,1,0:T(8,128)(2,1)S(1)} collective-permute-done((bf16[2,512,128]{2,1,0:T(8,128)(2,1)S(1)}, bf16[2,512,128]{2,1,0:T(8,128)(2,1)S(1)}, u32[]{:S(2)}, u32[]{:S(2)}) %collective-permute-start.1) | collective-permute-done | bytes 262176 | tf_op jit(solution)/shard_map/ppermute | solution.py:400
  34.4 23.2 %krylov.1 = (bf16[2,512,128]{2,1,0:T(8,128)(2,1)S(1)}, f32[2,128,512]{2,1,0:T(8,128)S(1)}) custom-call(s32[1]{0:T(128)} %bitcast.row_ref, s32[2]{0:T(128)S(1)} %dynamic_slice.12.live_ref, s32[2]{0:T(128)S(1)} %dynamic_slice.13.kept_ref, f32[2]{0:T(128)S(1)} %multiply_exponential_fusion.weight_ref, bf16[2,512,128]{2,1,0:T(8,128)(2,1)S(1)} %collective-permute-done.1.refs_0_, ...), custom_call_target="tpu_custom_call" | custom-call | flops 20000000000 | bytes 2097152 | tf_op jit(solution)/shard_map/krylov/pallas_call | solution.py:335
  57.6 0.1 collective-permute-start.4
  57.7 1.4 %truncate.1 = (f32[2,128,512]{2,1,0:T(8,128)S(1)}, f32[64,128]{1,0:T(8,128)S(1)}) custom-call(s32[2]{0:T(128)S(1)} %dynamic_slice.13.kept_ref, f32[2]{0:T(128)S(1)} %multiply_exponential_fusion.weight_ref, f32[2,128,512]{2,1,0:T(8,128)S(1)} %get-tuple-element.29.image_ref, bf16[512,512]{1,0:T(8,128)(2,1)S(1)} %get-tuple-element.24.refs_7_.refs_0_, ...), custom_call_target="tpu_custom_call" | custom-call | flops 2000000000 | bytes 2097152 | tf_op jit(solution)/shard_map/truncate/pallas_call | solution.py:358
  59.1 24.8 %all_to_all.11 = f32[64,1,128]{2,1,0:T(1,128)S(1)} all-to-all(f32[64,1,128]{2,1,0:T(1,128)S(1)} %bitcast.9), channel_id=1, replica_groups=mesh['sec_0'=8,'sec_1'=4,'sec_2'=2,'row'=4] {'sec_0','sec_1','sec_2'}, dimensions={0} | all-to-all | bytes 65536 | tf_op jit(solution)/shard_map/all_to_all | solution.py:413
  83.9 0.9 %scale.1 = f32[2,128,512]{2,1,0:T(8,128)} custom-call(f32[64,128]{1,0:T(8,128)S(1)} %bitcast.8, f32[2,128,512]{2,1,0:T(8,128)S(1)} %get-tuple-element.33.part_ref), custom_call_target="tpu_custom_call" | custom-call | flops 1000000 | bytes 2097152 | tf_op jit(solution)/shard_map/scale/pallas_call | solution.py:372
  84.8 0.0 collective-permute-done.4
  84.8 0.8 convert_element_type.7
  (1 shorter events, 0.0 us)
Async XLA Ops:
  0.6 10.0 %copy-start = (s32[128,128]{1,0:T(8,128)S(1)}, s32[128,128]{1,0:T(8,128)}, u32[]{:S(2)}) copy-start(s32[128,128]{1,0:T(8,128)} %param.15) | copy-start | bytes 196612
  0.6 15.6 %collective-permute-start = (bf16[2,512,128]{2,1,0:T(8,128)(2,1)}, bf16[2,512,128]{2,1,0:T(8,128)(2,1)S(1)}, u32[]{:S(2)}, u32[]{:S(2)}) collective-permute-start(bf16[2,512,128]{2,1,0:T(8,128)(2,1)} %param.8), channel_id=1, source_target_pairs={{0,128},{4,132},{8,136},{12,140},{16,144},{20,148},{24,152},{28,15... | collective-permute-start | bytes 786440 | tf_op jit(solution)/shard_map/ppermute | solution.py:24
  10.8 1.2 %copy-start.1 = (bf16[2,128,2048]{2,1,0:T(8,128)(2,1)S(1)}, bf16[2,128,2048]{2,1,0:T(8,128)(2,1)}, u32[]{:S(2)}) copy-start(bf16[2,128,2048]{2,1,0:T(8,128)(2,1)} %right_ref.3) | copy-start | bytes 3145732
  12.0 0.8 copy-start.2
  16.2 7.3 %copy-start.3 = (f32[4,16,16]{2,1,0:T(8,128)S(1)}, f32[4,16,16]{2,1,0:T(8,128)}, u32[]{:S(2)}) copy-start(f32[4,16,16]{2,1,0:T(8,128)} %left_ops_ref.1) | copy-start | bytes 12292
  16.3 10.1 %collective-permute-start.3 = (bf16[2,512,128]{2,1,0:T(8,128)(2,1)S(1)}, bf16[2,512,128]{2,1,0:T(8,128)(2,1)S(1)}, u32[]{:S(2)}, u32[]{:S(2)}) collective-permute-start(bf16[2,512,128]{2,1,0:T(8,128)(2,1)S(1)} %collective-permute-done.left_ref), channel_id=1, source_target_pairs={{0,3},{1,0},{2,1},{3,2},{4,7},{5,4},{6,5},{7,6},{8,11},{9,8},{10,9... | collective-permute-start | bytes 786440 | tf_op jit(solution)/shard_map/ppermute | solution.py:400
  19.1 8.1 %collective-permute-start.2 = (bf16[2,512,128]{2,1,0:T(8,128)(2,1)S(1)}, bf16[2,512,128]{2,1,0:T(8,128)(2,1)S(1)}, u32[]{:S(2)}, u32[]{:S(2)}) collective-permute-start(bf16[2,512,128]{2,1,0:T(8,128)(2,1)S(1)} %collective-permute-done.left_ref), channel_id=1, source_target_pairs={{0,2},{1,3},{2,0},{3,1},{4,6},{5,7},{6,4},{7,5},{8,10},{9,11},{10,... | collective-permute-start | bytes 786440 | tf_op jit(solution)/shard_map/ppermute | solution.py:400
  19.4 15.0 %collective-permute-start.1 = (bf16[2,512,128]{2,1,0:T(8,128)(2,1)S(1)}, bf16[2,512,128]{2,1,0:T(8,128)(2,1)S(1)}, u32[]{:S(2)}, u32[]{:S(2)}) collective-permute-start(bf16[2,512,128]{2,1,0:T(8,128)(2,1)S(1)} %collective-permute-done.left_ref), channel_id=1, source_target_pairs={{0,1},{1,2},{2,3},{3,0},{4,5},{5,6},{6,7},{7,4},{8,9},{9,10},{10,1... | collective-permute-start | bytes 786440 | tf_op jit(solution)/shard_map/ppermute | solution.py:400
  57.6 27.2 %collective-permute-start.4 = (bf16[2,512,128]{2,1,0:T(8,128)(2,1)S(1)}, bf16[2,512,128]{2,1,0:T(8,128)(2,1)S(1)}, u32[]{:S(2)}, u32[]{:S(2)}) collective-permute-start(bf16[2,512,128]{2,1,0:T(8,128)(2,1)S(1)} %get-tuple-element.28), channel_id=1, source_target_pairs={{0,128},{4,132},{8,136},{12,140},{16,144},{20,148},{24,152},{28,15... | collective-permute-start | bytes 786440 | tf_op jit(solution)/shard_map/ppermute | solution.py:24

commit v4 on v3

v4 whole, which is shorter than its diff:
```python
import functools

import jax
import jax.numpy as jnp
from jax import lax
from jax.experimental import pallas as pl
from jax.experimental.pallas import tpu as pltpu
from jax.sharding import Mesh
from jax.sharding import PartitionSpec as P

SITE = 16
ITERS = 2
SEC = ("sec_0", "sec_1", "sec_2")
ROW = ("high", "low")
SEC_ROW = (*SEC, *ROW)
SEC_LOW = (*SEC, "low")
WINDOW = 64

chemical = 0.4
highest = lax.Precision.HIGHEST


def crossed(value, sec_mask, row_mask):
    rows = lax.axis_size(ROW)
    mask = sec_mask * rows + row_mask
    return lax.ppermute(value, SEC_ROW, [(i, i ^ mask) for i in range(lax.axis_size(SEC_ROW))])


def dot_over(left, right, left_dim, right_dim, precision=None):
    return lax.dot_general(
        left,
        right,
        (((left_dim,), (right_dim,)), ((), ())),
        precision=precision,
        preferred_element_type=jnp.float32,
    )


def two_parts(values):
    high = values.astype(jnp.bfloat16)
    low = (values - high.astype(jnp.float32)).astype(jnp.bfloat16)
    return high, low


def one_hot(shape, row_key, col_key):
    rows = lax.broadcasted_iota(jnp.int32, shape, 0)
    cols = lax.broadcasted_iota(jnp.int32, shape, 1)
    return row_key(rows) == col_key(cols)


def as_weights(mask):
    return jnp.where(mask, 1.0, 0.0).astype(jnp.bfloat16)


def lower_inverse(grams, window):
    n = grams[0].shape[0]
    lane = lax.broadcasted_iota(jnp.int32, (8, n), 1)
    sub = lax.broadcasted_iota(jnp.int32, (8, n), 0)
    rows = [[g[8 * q : 8 * q + 8, :] for q in range(n // 8)] for g in grams]
    span = window // 8
    for first in range(0, n // 8, span):
        last = first + span
        for q in range(first, last):
            k = 8 * q
            inside = (lane >= k) & (lane < k + 8)
            unit = (lane - k == sub).astype(jnp.float32)
            for mat in rows:
                cols = {
                    r: [jnp.broadcast_to(mat[r][:, k + m : k + m + 1], (8, n)) for m in range(8)]
                    for r in range(q, last)
                }
                for r in range(q, last):
                    mat[r] = jnp.where(inside, unit if r == q else 0.0, mat[r])
                pivot = jnp.broadcast_to(cols[q][0][0:1, :], (8, n))
                for m in range(8):
                    scale = lax.rsqrt(pivot)
                    weights = {
                        j: jnp.broadcast_to(cols[q][m][j : j + 1, :], (8, n)) * scale
                        for j in range(m + 1, 8)
                    }
                    if m < 7:
                        ahead = jnp.broadcast_to(cols[q][m + 1][m + 1 : m + 2, :], (8, n))
                        pivot = ahead - weights[m + 1] * weights[m + 1]
                    below = {r: cols[r][m] * scale for r in range(q, last)}
                    head = jnp.broadcast_to(mat[q][m : m + 1, :], (8, n)) * scale
                    for j in range(m + 1, 8):
                        for r in range(q, last):
                            cols[r][j] = cols[r][j] - below[r] * weights[j]
                    below[q] = jnp.where(sub > m, below[q], 0.0)
                    for r in range(q, last):
                        mat[r] = mat[r] - below[r] * head
                    mat[q] = jnp.where(sub == m, head, mat[q])
        if last < n // 8:
            inblock = (lane >= 8 * first) & (lane < 8 * last)
            for mat in rows:
                panel = jnp.concatenate(mat[first:last], axis=0)
                panel_row = lax.broadcasted_iota(jnp.int32, panel.shape, 0) + 8 * first
                panel_lane = lax.broadcasted_iota(jnp.int32, panel.shape, 1)
                panel = jnp.where((panel_lane > panel_row) & (panel_lane < 8 * last), 0.0, panel)
                update = dot_over(panel, panel, 0, 0, highest)
                for r in range(last, n // 8):
                    mat[r] = jnp.where(inblock, 0.0, mat[r]) - update[8 * r : 8 * r + 8, :]
    full_row = lax.broadcasted_iota(jnp.int32, (n, n), 0)
    full_col = lax.broadcasted_iota(jnp.int32, (n, n), 1)
    return [jnp.where(full_col <= full_row, jnp.concatenate(mat, axis=0), 0.0) for mat in rows]


def three_pass(left, right, right_dim):
    (left_high, left_low), (right_high, right_low) = left, right
    return (
        dot_over(left_high, right_high, 1, right_dim)
        + dot_over(left_high, right_low, 1, right_dim)
        + dot_over(left_low, right_high, 1, right_dim)
    )


def right_kernel(
    row_ref, right_ref, right_ops_ref, high_ref, low_ref, local_ref, right_mix, gated, right, sem
):
    states = right.shape[0]
    terms = gated.shape[0] // states
    wide = SITE * SITE
    local_cols = local_ref.shape[1]
    fetch = pltpu.make_async_copy(right_ref.at[lax.rem(row_ref[0], 2)], right, sem)
    fetch.start()
    spread = as_weights(one_hot((terms * wide, terms * SITE), lambda r: r // SITE, lambda c: c))
    widen = as_weights(one_hot((SITE, wide), lambda r: r, lambda c: c // SITE))
    same = one_hot((terms * wide, wide), lambda r: r % SITE, lambda c: c % SITE)
    for part, piece in enumerate(two_parts(right_ops_ref[...])):
        tall = dot_over(spread, piece, 1, 0).astype(jnp.bfloat16)
        full = dot_over(tall, widen, 1, 0)
        right_mix[:, part * wide : (part + 1) * wide] = jnp.where(same, full, 0.0).astype(
            jnp.bfloat16
        )
    fetch.wait()
    for pair in range(states // (2 * SITE)):
        base = pair * 2 * SITE
        halves = [
            jnp.concatenate(
                [
                    right[base + h * SITE : base + (h + 1) * SITE, j * states : (j + 1) * states]
                    for j in range(SITE)
                ],
                axis=0,
            )
            for h in range(2)
        ]
        block = jnp.concatenate(halves, axis=1)
        block = jnp.concatenate([block, block], axis=0)
        for t in range(terms):
            mixed = dot_over(right_mix[t * wide : (t + 1) * wide, :], block, 1, 0)
            mixed = mixed.astype(jnp.bfloat16)
            for h in range(2):
                for i in range(SITE):
                    gated[
                        t * states + base + h * SITE : t * states + base + (h + 1) * SITE,
                        i * states : (i + 1) * states,
                    ] = mixed[i * SITE : (i + 1) * SITE, h * states : (h + 1) * states]
    high_ref[...], low_ref[...] = two_parts(dot_over(gated[...], gated[...], 1, 1))
    offset = pl.multiple_of((row_ref[0] // 2) * local_cols, local_cols)
    local_ref[...] = gated[:, pl.ds(offset, local_cols)]


def build_left_mix(left_ops_ref, left_mix):
    terms, _, wide = left_mix.shape
    tall_pick = as_weights(one_hot((wide, SITE), lambda r: r % SITE, lambda c: c))
    wide_pick = as_weights(one_hot((SITE, wide), lambda r: r, lambda c: c % SITE))
    group = one_hot((wide, wide), lambda r: r // SITE, lambda c: c // SITE)
    for t in range(terms):
        for part, piece in enumerate(two_parts(left_ops_ref[t])):
            tall = dot_over(tall_pick, piece, 1, 1).astype(jnp.bfloat16)
            full = dot_over(tall, wide_pick, 1, 0)
            left_mix[t, part * wide : (part + 1) * wide, :] = jnp.where(
                group, full, 0.0
            ).astype(jnp.bfloat16)


def gate_chunk(left_ref, live, first_row, left_mix_ref, gated, out_first):
    chunk_rows, states = left_ref.shape
    terms, _, wide = left_mix_ref.shape
    turned = left_ref[...].T
    pieces = []
    for b in range(chunk_rows // wide):
        lane = lax.broadcasted_iota(jnp.int32, (states, wide), 1)
        alive = lane < live * SITE - (first_row + b * wide)
        piece = turned[:, b * wide : (b + 1) * wide].astype(jnp.float32)
        pieces.append(jnp.where(alive, piece, 0.0).astype(jnp.bfloat16))
    tall = jnp.concatenate(pieces, axis=0)
    tall = jnp.concatenate([tall, tall], axis=1)
    for t in range(terms):
        mixed = dot_over(tall, left_mix_ref[t], 1, 0).astype(jnp.bfloat16)
        for b in range(len(pieces)):
            gated[
                t * states : (t + 1) * states, out_first + b * wide : out_first + (b + 1) * wide
            ] = mixed[b * states : (b + 1) * states, :]


def krylov_kernel(row_ref, live_ref, kept_ref, weight_ref, *refs):
    chunks = len(refs) - 13
    left_refs = refs[:chunks]
    (left_ops_ref, start_ref, square_high, square_low) = refs[chunks : chunks + 4]
    (own_ref, other_ref, image_ref) = refs[chunks + 4 : chunks + 7]
    (gated, gram_high, gram_low, block, final, left_mix) = refs[chunks + 7 :]
    build_left_mix(left_ops_ref, left_mix)
    chunk_rows = left_refs[0].shape[0]
    bond, keep = image_ref.shape[1], image_ref.shape[0]
    for c in range(chunks):
        first_row = lax.bitwise_xor(row_ref[0], c) * chunk_rows
        gate_chunk(left_refs[c], live_ref[0], first_row, left_mix, gated, c * chunk_rows)
    gram_high[...], gram_low[...] = two_parts(dot_over(gated[...], gated[...], 1, 1))
    spots = lax.broadcasted_iota(jnp.int32, (keep, bond), 1)
    block[...] = jnp.where(spots == start_ref[...], 1.0, 0.0)

    def step(index, carry):
        images = three_pass(two_parts(block[...]), (gram_high[...], gram_low[...]), 0)
        (inverse,) = lower_inverse([dot_over(images, block[...], 1, 1, highest)], WINDOW)
        inverse = two_parts(inverse)
        image_ref[...] = three_pass(inverse, two_parts(images), 0)

        @pl.when(index == ITERS)
        def _():
            final[...] = three_pass(inverse, two_parts(block[...]), 0)

        @pl.when(index < ITERS)
        def _():
            squares = (square_high[...], square_low[...])
            scale = weight_ref[0] * weight_ref[0]
            block[...] = scale * three_pass(two_parts(image_ref[...]), squares, 0)

        return carry

    lax.fori_loop(0, ITERS + 1, step, 0)
    high, low = two_parts(final[...])
    for c, basis_ref in enumerate((own_ref, other_ref)):
        rows = gated[:, c * chunk_rows : (c + 1) * chunk_rows]
        basis = dot_over(high, rows, 1, 0) + dot_over(low, rows, 1, 0)
        keeps = lax.broadcasted_iota(jnp.int32, basis.shape, 0) < kept_ref[0]
        basis_ref[...] = jnp.where(keeps, basis, 0.0).T.astype(jnp.bfloat16)


def truncate_kernel(
    row_ref, kept_ref, weight_ref, image_ref, square_high, square_low, local_ref,
    own_ref, other_ref, total_ref,
):
    image = image_ref[...]
    high, low = two_parts(image)
    keeps = lax.broadcasted_iota(jnp.int32, image.shape, 0) < kept_ref[0]
    scale = weight_ref[0] * weight_ref[0]
    squared = scale * three_pass((high, low), (square_high[...], square_low[...]), 0) * image
    squared = jnp.where(keeps, squared, 0.0)
    total = jnp.sum(jnp.sum(squared, axis=0, keepdims=True), axis=1, keepdims=True)
    total_ref[...] = jnp.broadcast_to(total, total_ref.shape)
    cols = own_ref.shape[1]
    side = lax.rem(row_ref[0], 2)
    for out_ref, half in ((own_ref, side), (other_ref, 1 - side)):
        local = local_ref[:, pl.ds(pl.multiple_of(half * cols, cols), cols)]
        part = dot_over(high, local, 1, 0) + dot_over(low, local, 1, 0)
        keeps = lax.broadcasted_iota(jnp.int32, part.shape, 0) < kept_ref[0]
        out_ref[...] = jnp.where(keeps, part * weight_ref[0], 0.0).astype(out_ref.dtype)


def finish_kernel(
    row_ref, totals_ref, part_own, part_other, basis_own, basis_other, basis_ref, right_ref
):
    side = lax.rem(row_ref[0], 2)
    basis_ref[side] = basis_own[...].astype(jnp.float32)
    basis_ref[1 - side] = basis_other[...].astype(jnp.float32)
    total = jnp.sum(totals_ref[...], axis=0, keepdims=True)[:, :1]
    factor = 1.0 / jnp.sqrt(total)
    right_ref[side] = part_own[...] * factor
    right_ref[1 - side] = part_other[...].astype(jnp.float32) * factor


def smem():
    return pl.BlockSpec(memory_space=pltpu.SMEM)


def vmem():
    return pl.BlockSpec(memory_space=pltpu.VMEM)


def shape_of(shape, dtype):
    return jax.ShapeDtypeStruct(shape, dtype)


def kernel_options(mebibytes, flops):
    return dict(
        compiler_params=pltpu.CompilerParams(vmem_limit_bytes=mebibytes << 20),
        cost_estimate=pl.CostEstimate(flops=int(flops), bytes_accessed=2 << 20, transcendentals=0),
    )


def gate_right(row, right_block, right_ops, local_cols):
    _, states, cols = right_block.shape
    terms = right_ops.shape[0]
    bond, wide = terms * states, SITE * SITE
    return pl.pallas_call(
        right_kernel,
        in_specs=[smem(), pl.BlockSpec(memory_space=pltpu.HBM), vmem()],
        out_specs=[vmem()] * 3,
        out_shape=[
            shape_of((bond, bond), jnp.bfloat16),
            shape_of((bond, bond), jnp.bfloat16),
            shape_of((bond, local_cols), jnp.bfloat16),
        ],
        scratch_shapes=[
            pltpu.VMEM((terms * wide, 2 * wide), jnp.bfloat16),
            pltpu.VMEM((bond, cols), jnp.bfloat16),
            pltpu.VMEM((states, cols), jnp.bfloat16),
            pltpu.SemaphoreType.DMA,
        ],
        name="right_gate",
        **kernel_options(12, 4e9),
    )(row, right_block, right_ops.reshape(terms * SITE, SITE))


def krylov_part(row, live, kept, weight, left_chunks, left_ops, start, squares):
    chunk_rows, _ = left_chunks[0].shape
    bond = squares[0].shape[0]
    keep = start.shape[0]
    return pl.pallas_call(
        krylov_kernel,
        in_specs=[smem()] * 4 + [vmem()] * (len(left_chunks) + 4),
        out_specs=[vmem()] * 3,
        out_shape=[
            shape_of((chunk_rows, keep), jnp.bfloat16),
            shape_of((chunk_rows, keep), jnp.bfloat16),
            shape_of((keep, bond), jnp.float32),
        ],
        scratch_shapes=[
            pltpu.VMEM((bond, len(left_chunks) * chunk_rows), jnp.bfloat16),
            pltpu.VMEM((bond, bond), jnp.bfloat16),
            pltpu.VMEM((bond, bond), jnp.bfloat16),
            pltpu.VMEM((keep, bond), jnp.float32),
            pltpu.VMEM((keep, bond), jnp.float32),
            pltpu.VMEM((left_ops.shape[0], 2 * SITE * SITE, SITE * SITE), jnp.bfloat16),
        ],
        name="krylov",
        **kernel_options(14, 2e10),
    )(row, live, kept, weight, *left_chunks, left_ops, start, *squares)


def truncated(row, kept, weight, image, squares, local, peers):
    keep, _ = image.shape
    cols = local.shape[1] // 2
    return pl.pallas_call(
        truncate_kernel,
        in_specs=[smem()] * 3 + [vmem()] * 4,
        out_specs=[vmem()] * 3,
        out_shape=[
            shape_of((keep, cols), jnp.float32),
            shape_of((keep, cols), jnp.bfloat16),
            shape_of((peers, keep), jnp.float32),
        ],
        name="truncate",
        **kernel_options(8, 2e9),
    )(row, kept, weight, image, *squares, local)


def finished(row, totals, part_own, part_other, basis_own, basis_other):
    keep, cols = part_own.shape
    return pl.pallas_call(
        finish_kernel,
        in_specs=[smem()] + [vmem()] * 5,
        out_specs=[vmem()] * 2,
        out_shape=[
            shape_of((2, *basis_own.shape), jnp.float32),
            shape_of((2, keep, cols), jnp.float32),
        ],
        name="finish",
        **kernel_options(4, 1e6),
    )(row, totals, part_own, part_other, basis_own, basis_other)


def on_device(left_block, right_block, left_ops, right_ops, charges, live_states, kept, start):
    slots = left_block.shape[0]
    sec_size, row_size = lax.axis_size(SEC), lax.axis_size(ROW)
    sectors = slots * sec_size
    sec_half = sec_size // 2
    side = lax.axis_index("low")
    row = lax.axis_index(ROW).astype(jnp.int32).reshape(1)
    mine = jnp.where(side == 0, left_block[0], left_block[1])
    neighbours = jnp.where(side == 0, left_block[1], left_block[0])
    left_chunks = [crossed((mine, neighbours)[d % 2], sec_half, d) for d in range(row_size)]
    right_id = lax.axis_index(SEC) * slots + side
    left_id = (right_id + sectors // 2) % sectors
    cut = lambda table, which: lax.dynamic_slice_in_dim(table, which, 1, 0)
    live = cut(live_states, left_id)
    kept_here = cut(kept, right_id)
    weight = jnp.exp(-chemical * cut(charges, right_id).astype(jnp.float32))
    start_here = cut(start, left_id).reshape(-1, 1)
    local_cols = 2 * right_block.shape[2] // row_size
    high, low, local = gate_right(row, right_block, right_ops, local_cols)
    basis_own, basis_other, image = krylov_part(
        row, live, kept_here, weight, left_chunks, left_ops, start_here, (high, low)
    )
    basis_own = crossed(basis_own, sec_half, 0)
    basis_other = crossed(basis_other, sec_half, 1)
    part_own, part_other, total = truncated(
        row, kept_here, weight, image, (high, low), local, lax.axis_size(SEC_LOW)
    )
    part_other = crossed(part_other, 0, 1)
    totals = lax.all_to_all(total, SEC_LOW, split_axis=0, concat_axis=0, tiled=True)
    return tuple(finished(row, totals, part_own, part_other, basis_own, basis_other))


def solution(mesh):
    finer = Mesh(mesh.devices.reshape(8, 4, 2, 2, 2), SEC_ROW)
    in_specs = (P(SEC, ROW, None), P(SEC, None, None), P(), P(), P(), P(), P(), P())
    out_specs = (P(SEC, ROW, None), P(SEC, None, ROW))
    return jax.shard_map(
        on_device, mesh=finer, in_specs=in_specs, out_specs=out_specs, check_vma=False
    )
```

time: 85.9 us -> 86.8 us (1.010)
  starting transfers between devices: 11.8 us -> 24.2 us
  Pallas kernels: 35.1 us -> 25.5 us
  blocking collectives: 24.8 us -> 21 us
  local copies, waits for them, and re-layouts: 3.6 us -> 4.47 us
    ppermute x5 -> x7, starting transfers between devices: 11.8 us -> 24.2 us  [crossed(): lax.ppermute(value, SEC_ROW, [(i, i ^ mask) for i in range(lax.axis_size(...]
    pallas_call x5 -> x3, Pallas kernels: 11.9 us -> 5.79 us  [the longest x1 3.45 us: gate_right(): pl.pallas_call(right_kernel, in_specs=[smem(), pl.BlockSpec(memory_space=...]
    all_to_all x1, blocking collectives: 24.8 us -> 21 us  [on_device(): lax.all_to_all(total, SEC_LOW, split_axis=0, concat_axis=0, tiled=True)]
    pallas_call x1, Pallas kernels: 23.2 us -> 19.7 us  [krylov_part(): pl.pallas_call(krylov_kernel, in_specs=[smem()] * 4 + [vmem()] * (len(lef...]
    select_n x0 -> x1, other arithmetic: none -> 1.02 us  [on_device(): neighbours = jnp.where(side == 0, left_block[1], left_block[0])]
    ppermute x5 -> x7, waiting for transfers between devices: 8.08 us -> 8.86 us  [crossed(): lax.ppermute(value, SEC_ROW, [(i, i ^ mask) for i in range(lax.axis_size(...]
    unnamed x8 -> x14, local copies, waits for them, and re-layouts: 2 us -> 2.61 us
    dynamic_slice x2 -> x3, local copies, waits for them, and re-layouts: 1.46 us -> 1.75 us  [on_device(): cut = lambda table, which: lax.dynamic_slice_in_dim(table, which, 1, 0)]
  transfers between devices with their start and end apart: 5 -> 7, of which waited for: 2 -> 3; matrix products, arithmetic and copies ran while one was open for 3% -> 2% of each run, Pallas kernels for 14% -> 4%
where the time goes in v4:
time: 86.8 us; the launch traced here: 86.5 us
  Pallas kernels  25.5 us (29%)
  starting transfers between devices  24.2 us (28%)
  blocking collectives  21 us (24%)
  waiting for transfers between devices  8.86 us (10%)
  local copies, waits for them, and re-layouts  4.47 us (5%)
  between operations  1.44 us (2%)
  other arithmetic  1.02 us (1%)
    ppermute x7, starting transfers between devices, crossed(): lax.ppermute(value, SEC_ROW, [(i, i ^ mask) for i in range(lax.axis_size(...  24.2 us
    all_to_all x1, blocking collectives, on_device(): lax.all_to_all(total, SEC_LOW, split_axis=0, concat_axis=0, tiled=True)  21 us
    pallas_call x1, Pallas kernels, krylov_part(): pl.pallas_call(krylov_kernel, in_specs=[smem()] * 4 + [vmem()] * (len(lef...  19.7 us
    ppermute x7, waiting for transfers between devices, crossed(): lax.ppermute(value, SEC_ROW, [(i, i ^ mask) for i in range(lax.axis_size(...  8.86 us
    pallas_call x1, Pallas kernels, gate_right(): pl.pallas_call(right_kernel, in_specs=[smem(), pl.BlockSpec(memory_space=...  3.45 us
    unnamed x14, local copies, waits for them, and re-layouts  2.61 us
    dynamic_slice x3, local copies, waits for them, and re-layouts, on_device(): cut = lambda table, which: lax.dynamic_slice_in_dim(table, which, 1, 0)  1.75 us
  transfers between devices with their start and end apart: 7, of which 3 were waited for; matrix products, arithmetic and copies ran while one was open for 2% of the time, Pallas kernels for 4%

profile of v4, /device:TPU:1, one launch (start us, length us, event | category | flops | bytes accessed | tf_op | source)
XLA Modules:
  0.0 86.5 jit_solution(467512118438526297)
XLA Ops:
  0.6 0.0 copy-start
  0.7 0.0 copy-start.2
  0.7 1.0 %select_bitcast_fusion = (bf16[512,128]{1,0:T(8,128)(2,1)S(1)}, bf16[512,128]{1,0:T(8,128)(2,1)S(1)}) fusion(pred[]{:T(512)S(6)} %eq.6, bf16[2,512,128]{2,1,0:T(8,128)(2,1)} %param.8), kind=kLoop, calls=%fused_computation | loop fusion | flops 131072 | bytes 524289 | tf_op jit(solution)/shard_map/jit(_where)/select_n | solution.py:383
  1.7 10.3 %collective-permute-start.3 = (bf16[512,128]{1,0:T(8,128)(2,1)S(1)}, bf16[512,128]{1,0:T(8,128)(2,1)S(1)}, u32[]{:S(2)}, u32[]{:S(2)}) collective-permute-start(bf16[512,128]{1,0:T(8,128)(2,1)S(1)} %get-tuple-element.20), channel_id=1, source_target_pairs={{0,131},{1,130},{2,129},{3,128},{4,135},{5,134},{6,133},{7,132},{8... | collective-permute-start | bytes 393224 | tf_op jit(solution)/shard_map/ppermute | solution.py:26
  12.0 0.0 collective-permute-start.1
  12.0 5.9 %collective-permute-start.2 = (bf16[512,128]{1,0:T(8,128)(2,1)S(1)}, bf16[512,128]{1,0:T(8,128)(2,1)S(1)}, u32[]{:S(2)}, u32[]{:S(2)}) collective-permute-start(bf16[512,128]{1,0:T(8,128)(2,1)S(1)} %get-tuple-element.21), channel_id=1, source_target_pairs={{0,130},{1,131},{2,128},{3,129},{4,134},{5,135},{6,132},{7,133},{8... | collective-permute-start | bytes 393224 | tf_op jit(solution)/shard_map/ppermute | solution.py:26
  17.9 0.4 collective-permute-start
  18.3 0.0 copy-done.2
  18.3 0.0 copy-start.1
  18.3 1.2 %copy-done.1 = bf16[2,128,2048]{2,1,0:T(8,128)(2,1)S(1)} copy-done((bf16[2,128,2048]{2,1,0:T(8,128)(2,1)S(1)}, bf16[2,128,2048]{2,1,0:T(8,128)(2,1)}, u32[]{:S(2)}) %copy-start.1) | copy-done | bytes 1048600
  19.6 3.5 %right_gate.1 = (bf16[512,512]{1,0:T(8,128)(2,1)S(1)}, bf16[512,512]{1,0:T(8,128)(2,1)S(1)}, bf16[512,1024]{1,0:T(8,128)(2,1)S(1)}) custom-call(s32[1]{0:T(128)} %bitcast.row_ref, bf16[2,128,2048]{2,1,0:T(8,128)(2,1)S(1)} %copy-done.1, f32[64,16]{1,0:T(8,128)S(1)} %bitcast.14), custom_call_target="tpu_custom_call" | custom-call | flops 4000000000 | bytes 2097152 | tf_op jit(solution)/shard_map/right_gate/pallas_call | solution.py:297
  23.1 0.0 copy-start.4
  23.1 0.6 copy-done.4
  23.7 0.0 copy-start.5
  23.7 0.6 dynamic_slice.12.kept_ref
  24.3 0.1 copy-done.5
  24.4 0.6 dynamic_slice.13
  25.6 0.0 copy-start.6
  25.7 0.6 copy-done.6
  26.3 0.6 dynamic_slice.14.live_ref
  26.9 0.0 copy-done
  26.9 0.0 copy-start.3
  26.9 0.1 copy.11.refs_5_
  27.0 0.0 collective-permute-done.3.refs_3_
  27.0 1.4 %collective-permute-done.1.refs_1_ = bf16[512,128]{1,0:T(8,128)(2,1)S(1)} collective-permute-done((bf16[512,128]{1,0:T(8,128)(2,1)S(1)}, bf16[512,128]{1,0:T(8,128)(2,1)S(1)}, u32[]{:S(2)}, u32[]{:S(2)}) %collective-permute-start.1) | collective-permute-done | bytes 131104 | tf_op jit(solution)/shard_map/ppermute | solution.py:26
  28.4 2.6 %collective-permute-done.2.refs_2_ = bf16[512,128]{1,0:T(8,128)(2,1)S(1)} collective-permute-done((bf16[512,128]{1,0:T(8,128)(2,1)S(1)}, bf16[512,128]{1,0:T(8,128)(2,1)S(1)}, u32[]{:S(2)}, u32[]{:S(2)}) %collective-permute-start.2) | collective-permute-done | bytes 131104 | tf_op jit(solution)/shard_map/ppermute | solution.py:26
  31.0 4.9 %collective-permute-done.refs_0_ = bf16[512,128]{1,0:T(8,128)(2,1)S(1)} collective-permute-done((bf16[512,128]{1,0:T(8,128)(2,1)S(1)}, bf16[512,128]{1,0:T(8,128)(2,1)S(1)}, u32[]{:S(2)}, u32[]{:S(2)}) %collective-permute-start) | collective-permute-done | bytes 131104 | tf_op jit(solution)/shard_map/ppermute | solution.py:26
  35.9 0.0 copy-done.3
  35.9 19.7 %krylov.1 = (bf16[512,128]{1,0:T(8,128)(2,1)S(1)}, bf16[512,128]{1,0:T(8,128)(2,1)S(1)}, f32[128,512]{1,0:T(8,128)S(1)}) custom-call(s32[1]{0:T(128)} %bitcast.row_ref, s32[1]{0:T(128)} %dynamic_slice.14.live_ref, s32[1]{0:T(128)} %dynamic_slice.12.kept_ref, f32[1]{0:T(128)S(6)} %exp.3.weight_ref, bf16[512,128]{1,0:T(8,128)(2,1)S(1)} %collective-permute-done.refs_0_, ...), custom_call_target="tpu_custom_call" | custom-call | flops 20000000000 | bytes 2097152 | tf_op jit(solution)/shard_map/krylov/pallas_call | solution.py:321
  55.6 1.3 %truncate.1 = (f32[128,512]{1,0:T(8,128)S(1)}, bf16[128,512]{1,0:T(8,128)(2,1)S(1)}, f32[128,128]{1,0:T(8,128)S(1)}) custom-call(s32[1]{0:T(128)} %bitcast.row_ref, s32[1]{0:T(128)} %dynamic_slice.12.kept_ref, f32[1]{0:T(128)S(6)} %exp.3.weight_ref, f32[128,512]{1,0:T(8,128)S(1)} %get-tuple-element.13.image_ref, ...), custom_call_target="tpu_custom_call" | custom-call | flops 2000000000 | bytes 2097152 | tf_op jit(solution)/shard_map/truncate/pallas_call | solution.py:346
  56.9 2.4 %collective-permute-start.4 = (bf16[128,512]{1,0:T(8,128)(2,1)S(1)}, bf16[128,512]{1,0:T(8,128)(2,1)S(1)}, u32[]{:S(2)}, u32[]{:S(2)}) collective-permute-start(bf16[128,512]{1,0:T(8,128)(2,1)S(1)} %get-tuple-element.17), channel_id=1, source_target_pairs={{0,1},{1,0},{2,3},{3,2},{4,5},{5,4},{6,7},{7,6},{8,9},{9,8},{10,11... | collective-permute-start | bytes 393224 | tf_op jit(solution)/shard_map/ppermute | solution.py:26
  59.3 1.9 %collective-permute-start.5 = (bf16[512,128]{1,0:T(8,128)(2,1)S(1)}, bf16[512,128]{1,0:T(8,128)(2,1)S(1)}, u32[]{:S(2)}, u32[]{:S(2)}) collective-permute-start(bf16[512,128]{1,0:T(8,128)(2,1)S(1)} %get-tuple-element.18), channel_id=1, source_target_pairs={{0,128},{1,129},{2,130},{3,131},{4,132},{5,133},{6,134},{7,135},{8... | collective-permute-start | bytes 393224 | tf_op jit(solution)/shard_map/ppermute | solution.py:26
  61.2 3.3 %collective-permute-start.6 = (bf16[512,128]{1,0:T(8,128)(2,1)S(1)}, bf16[512,128]{1,0:T(8,128)(2,1)S(1)}, u32[]{:S(2)}, u32[]{:S(2)}) collective-permute-start(bf16[512,128]{1,0:T(8,128)(2,1)S(1)} %get-tuple-element.19), channel_id=1, source_target_pairs={{0,129},{1,128},{2,131},{3,130},{4,133},{5,132},{6,135},{7,134},{8... | collective-permute-start | bytes 393224 | tf_op jit(solution)/shard_map/ppermute | solution.py:26
  64.5 21.0 %all_to_all.11 = f32[128,1,128]{2,1,0:T(1,128)S(1)} all-to-all(f32[128,1,128]{2,1,0:T(1,128)S(1)} %bitcast.13), channel_id=1, replica_groups=mesh['sec_0'=8,'sec_1'=4,'sec_2'=2,'high'=2,'low'=2] {'sec_0','sec_1','s..., dimensions={0} | all-to-all | bytes 131072 | tf_op jit(solution)/shard_map/all_to_all | solution.py:403
  85.5 0.0 collective-permute-done.4.part_other
  85.5 0.0 collective-permute-done.5.basis_own
  85.5 0.0 collective-permute-done.6.basis_other
  85.5 1.0 %finish.1 = (f32[2,512,128]{2,1,0:T(8,128)}, f32[2,128,512]{2,1,0:T(8,128)}) custom-call(s32[1]{0:T(128)} %bitcast.row_ref, f32[128,128]{1,0:T(8,128)S(1)} %bitcast.12, f32[128,512]{1,0:T(8,128)S(1)} %get-tuple-element.16.part_own, bf16[128,512]{1,0:T(8,128)(2,1)S(1)} %collective-permute-done.4.part_other, ...), custom_call_target="tpu_custom_call" | custom-call | flops 1000000 | bytes 2097152 | tf_op jit(solution)/shard_map/finish/pallas_call | solution.py:362
  (1 shorter events, 0.0 us)
Async XLA Ops:
  0.6 26.3 %copy-start = (s32[128,128]{1,0:T(8,128)S(1)}, s32[128,128]{1,0:T(8,128)}, u32[]{:S(2)}) copy-start(s32[128,128]{1,0:T(8,128)} %param.15) | copy-start | bytes 196612
  0.7 17.7 %copy-start.2 = (f32[4,16,16]{2,1,0:T(8,128)S(1)}, f32[4,16,16]{2,1,0:T(8,128)}, u32[]{:S(2)}) copy-start(f32[4,16,16]{2,1,0:T(8,128)} %param.11) | copy-start | bytes 12292
  1.7 25.3 %collective-permute-start.3 = (bf16[512,128]{1,0:T(8,128)(2,1)S(1)}, bf16[512,128]{1,0:T(8,128)(2,1)S(1)}, u32[]{:S(2)}, u32[]{:S(2)}) collective-permute-start(bf16[512,128]{1,0:T(8,128)(2,1)S(1)} %get-tuple-element.20), channel_id=1, source_target_pairs={{0,131},{1,130},{2,129},{3,128},{4,135},{5,134},{6,133},{7,132},{8... | collective-permute-start | bytes 393224 | tf_op jit(solution)/shard_map/ppermute | solution.py:26
  12.0 16.5 %collective-permute-start.1 = (bf16[512,128]{1,0:T(8,128)(2,1)S(1)}, bf16[512,128]{1,0:T(8,128)(2,1)S(1)}, u32[]{:S(2)}, u32[]{:S(2)}) collective-permute-start(bf16[512,128]{1,0:T(8,128)(2,1)S(1)} %get-tuple-element.20), channel_id=1, source_target_pairs={{0,129},{1,128},{2,131},{3,130},{4,133},{5,132},{6,135},{7,134},{8... | collective-permute-start | bytes 393224 | tf_op jit(solution)/shard_map/ppermute | solution.py:26
  12.0 19.1 %collective-permute-start.2 = (bf16[512,128]{1,0:T(8,128)(2,1)S(1)}, bf16[512,128]{1,0:T(8,128)(2,1)S(1)}, u32[]{:S(2)}, u32[]{:S(2)}) collective-permute-start(bf16[512,128]{1,0:T(8,128)(2,1)S(1)} %get-tuple-element.21), channel_id=1, source_target_pairs={{0,130},{1,131},{2,128},{3,129},{4,134},{5,135},{6,132},{7,133},{8... | collective-permute-start | bytes 393224 | tf_op jit(solution)/shard_map/ppermute | solution.py:26
  17.9 18.0 %collective-permute-start = (bf16[512,128]{1,0:T(8,128)(2,1)S(1)}, bf16[512,128]{1,0:T(8,128)(2,1)S(1)}, u32[]{:S(2)}, u32[]{:S(2)}) collective-permute-start(bf16[512,128]{1,0:T(8,128)(2,1)S(1)} %get-tuple-element.21), channel_id=1, source_target_pairs={{0,128},{1,129},{2,130},{3,131},{4,132},{5,133},{6,134},{7,135},{8... | collective-permute-start | bytes 393224 | tf_op jit(solution)/shard_map/ppermute | solution.py:26
  18.3 1.2 %copy-start.1 = (bf16[2,128,2048]{2,1,0:T(8,128)(2,1)S(1)}, bf16[2,128,2048]{2,1,0:T(8,128)(2,1)}, u32[]{:S(2)}) copy-start(bf16[2,128,2048]{2,1,0:T(8,128)(2,1)} %right_ref.1) | copy-start | bytes 3145732
  23.1 0.7 copy-start.4
  23.7 0.7 copy-start.5
  25.6 0.7 copy-start.6
  26.9 9.0 %copy-start.3 = (f32[4,16,16]{2,1,0:T(8,128)S(1)}, f32[4,16,16]{2,1,0:T(8,128)}, u32[]{:S(2)}) copy-start(f32[4,16,16]{2,1,0:T(8,128)} %refs_4_.1) | copy-start | bytes 12292
  56.9 28.6 %collective-permute-start.4 = (bf16[128,512]{1,0:T(8,128)(2,1)S(1)}, bf16[128,512]{1,0:T(8,128)(2,1)S(1)}, u32[]{:S(2)}, u32[]{:S(2)}) collective-permute-start(bf16[128,512]{1,0:T(8,128)(2,1)S(1)} %get-tuple-element.17), channel_id=1, source_target_pairs={{0,1},{1,0},{2,3},{3,2},{4,5},{5,4},{6,7},{7,6},{8,9},{9,8},{10,11... | collective-permute-start | bytes 393224 | tf_op jit(solution)/shard_map/ppermute | solution.py:26
  59.3 26.2 %collective-permute-start.5 = (bf16[512,128]{1,0:T(8,128)(2,1)S(1)}, bf16[512,128]{1,0:T(8,128)(2,1)S(1)}, u32[]{:S(2)}, u32[]{:S(2)}) collective-permute-start(bf16[512,128]{1,0:T(8,128)(2,1)S(1)} %get-tuple-element.18), channel_id=1, source_target_pairs={{0,128},{1,129},{2,130},{3,131},{4,132},{5,133},{6,134},{7,135},{8... | collective-permute-start | bytes 393224 | tf_op jit(solution)/shard_map/ppermute | solution.py:26
  61.2 24.3 %collective-permute-start.6 = (bf16[512,128]{1,0:T(8,128)(2,1)S(1)}, bf16[512,128]{1,0:T(8,128)(2,1)S(1)}, u32[]{:S(2)}, u32[]{:S(2)}) collective-permute-start(bf16[512,128]{1,0:T(8,128)(2,1)S(1)} %get-tuple-element.19), channel_id=1, source_target_pairs={{0,129},{1,128},{2,131},{3,130},{4,133},{5,132},{6,135},{7,134},{8... | collective-permute-start | bytes 393224 | tf_op jit(solution)/shard_map/ppermute | solution.py:26

commit v5 on v3

--- a/solution.py
+++ b/solution.py
@@ -69,16 +69,22 @@
                 }
                 for r in range(q, last):
                     mat[r] = jnp.where(inside, unit if r == q else 0.0, mat[r])
+                pivot = jnp.broadcast_to(cols[q][0][0:1, :], (8, n))
                 for m in range(8):
-                    pivot = jnp.broadcast_to(cols[q][m][m : m + 1, :], (8, n))
                     scale = lax.rsqrt(pivot)
+                    weights = {
+                        j: jnp.broadcast_to(cols[q][m][j : j + 1, :], (8, n)) * scale
+                        for j in range(m + 1, 8)
+                    }
+                    if m < 7:
+                        ahead = jnp.broadcast_to(cols[q][m + 1][m + 1 : m + 2, :], (8, n))
+                        pivot = ahead - weights[m + 1] * weights[m + 1]
+                    below = {r: cols[r][m] * scale for r in range(q, last)}
                     head = jnp.broadcast_to(mat[q][m : m + 1, :], (8, n)) * scale
-                    below = {r: cols[r][m] * scale for r in range(q, last)}
+                    for j in range(m + 1, 8):
+                        for r in range(q, last):
+                            cols[r][j] = cols[r][j] - below[r] * weights[j]
                     below[q] = jnp.where(sub > m, below[q], 0.0)
-                    for j in range(m + 1, 8):
-                        weight = jnp.broadcast_to(below[q][j : j + 1, :], (8, n))
-                        for r in range(q, last):
-                            cols[r][j] = cols[r][j] - below[r] * weight
                     for r in range(q, last):
                         mat[r] = mat[r] - below[r] * head
                     mat[q] = jnp.where(sub == m, head, mat[q])
@@ -153,10 +159,24 @@
     local_ref[...] = gated[:, pl.ds(offset, local_cols)]
 
 
-def gate_chunk(left_ref, slot, live, first_row, left_mix_ref, out_ref, out_first):
-    chunk_rows, states = left_ref.shape[1:]
+def build_left_mix(left_ops_ref, left_mix):
+    terms, _, wide = left_mix.shape
+    tall_pick = as_weights(one_hot((wide, SITE), lambda r: r % SITE, lambda c: c))
+    wide_pick = as_weights(one_hot((SITE, wide), lambda r: r, lambda c: c % SITE))
+    group = one_hot((wide, wide), lambda r: r // SITE, lambda c: c // SITE)
+    for t in range(terms):
+        for part, piece in enumerate(two_parts(left_ops_ref[t])):
+            tall = dot_over(tall_pick, piece, 1, 1).astype(jnp.bfloat16)
+            full = dot_over(tall, wide_pick, 1, 0)
+            left_mix[t, part * wide : (part + 1) * wide, :] = jnp.where(group, full, 0.0).astype(
+                jnp.bfloat16
+            )
+
+
+def gate_chunk(left_ref, live, first_row, left_mix_ref, gated, out_first):
+    chunk_rows, states = left_ref.shape
     terms, _, wide = left_mix_ref.shape
-    turned = left_ref[slot].T
+    turned = left_ref[...].T
     pieces = []
     for b in range(chunk_rows // wide):
         lane = lax.broadcasted_iota(jnp.int32, (states, wide), 1)
@@ -168,62 +188,57 @@
     for t in range(terms):
         mixed = dot_over(tall, left_mix_ref[t], 1, 0).astype(jnp.bfloat16)
         for b in range(len(pieces)):
-            out_ref[
-                slot, t * states : (t + 1) * states, out_first + b * wide : out_first + (b + 1) * wide
+            gated[
+                t * states : (t + 1) * states, out_first + b * wide : out_first + (b + 1) * wide
             ] = mixed[b * states : (b + 1) * states, :]
 
 
-def own_kernel(row_ref, live_ref, left_ref, left_ops_ref, gated_ref, gram_ref, left_mix_ref):
-    terms = left_ops_ref.shape[0]
-    wide = SITE * SITE
-    tall_pick = as_weights(one_hot((wide, SITE), lambda r: r % SITE, lambda c: c))
-    wide_pick = as_weights(one_hot((SITE, wide), lambda r: r, lambda c: c % SITE))
-    group = one_hot((wide, wide), lambda r: r // SITE, lambda c: c // SITE)
-    for t in range(terms):
-        for part, piece in enumerate(two_parts(left_ops_ref[t])):
-            tall = dot_over(tall_pick, piece, 1, 1).astype(jnp.bfloat16)
-            full = dot_over(tall, wide_pick, 1, 0)
-            left_mix_ref[t, part * wide : (part + 1) * wide, :] = jnp.where(
-                group, full, 0.0
-            ).astype(jnp.bfloat16)
-    slots, chunk_rows = left_ref.shape[:2]
+def gate_sector(row_ref, live, left_refs, left_mix, gated):
+    chunks = len(left_refs)
+    chunk_rows = left_refs[0].shape[0]
+    for c in range(chunks):
+        first_row = lax.rem(row_ref[0] + (chunks - c), chunks) * chunk_rows
+        gate_chunk(left_refs[c], live, first_row, left_mix, gated, c * chunk_rows)
+    return two_parts(dot_over(gated[...], gated[...], 1, 1))
+
+
+def left_kernel(row_ref, live_ref, left_ops_ref, *refs):
+    left_refs = refs[:-5]
+    own_ref, high_ref, low_ref, left_mix, gated = refs[-5:]
+    build_left_mix(left_ops_ref, left_mix)
+    high_ref[...], low_ref[...] = gate_sector(row_ref, live_ref[0], left_refs, left_mix, gated)
+    own_ref[...] = gated[:, : own_ref.shape[1]]
+
+
+def krylov_kernel(row_ref, live_ref, kept_ref, weight_ref, *refs):
+    chunks = len(refs) - 16
+    left_refs = refs[:chunks]
+    (left_mix, first_own, first_high, first_low, start_ref) = refs[chunks : chunks + 5]
+    square_refs = refs[chunks + 5 : chunks + 9]
+    (basis_ref, image_ref) = refs[chunks + 9 : chunks + 11]
+    (gated, second_high, second_low, block, final) = refs[chunks + 11 :]
+    slots, keep, bond = image_ref.shape
+    chunk_rows = left_refs[0].shape[0]
+    second_high[...], second_low[...] = gate_sector(row_ref, live_ref[1], left_refs, left_mix, gated)
+    gram_refs = ((first_high, first_low), (second_high, second_low))
     for s in range(slots):
-        gate_chunk(left_ref, s, live_ref[s], row_ref[0] * chunk_rows, left_mix_ref, gated_ref, 0)
-        gram_ref[s] = dot_over(gated_ref[s], gated_ref[s], 1, 1)
-
-
-def krylov_kernel(row_ref, live_ref, kept_ref, weight_ref, *refs):
-    chunks = len(refs) - 15
-    left_refs = refs[:chunks]
-    (left_mix_ref, own_ref, own_gram_ref, start_ref) = refs[chunks : chunks + 4]
-    square_refs = refs[chunks + 4 : chunks + 8]
-    (basis_ref, image_ref) = refs[chunks + 8 : chunks + 10]
-    (gated, gram_high, gram_low, block, final) = refs[chunks + 10 :]
-    slots, chunk_rows, states = left_refs[0].shape
-    bond = own_ref.shape[1]
-    keep = block.shape[1]
-    for s in range(slots):
-        for c in range(chunks):
-            first_row = lax.rem(row_ref[0] + (chunks - c), chunks + 1) * chunk_rows
-            gate_chunk(left_refs[c], s, live_ref[s], first_row, left_mix_ref, gated, c * chunk_rows)
-        gram = own_gram_ref[s] + dot_over(gated[s], gated[s], 1, 1)
-        gram_high[s], gram_low[s] = two_parts(gram)
         spots = lax.broadcasted_iota(jnp.int32, (keep, bond), 1)
         block[s] = jnp.where(spots == start_ref[s], 1.0, 0.0)
 
     def step(index, carry):
         images = [
-            three_pass(two_parts(block[s]), (gram_high[s], gram_low[s]), 0) for s in range(slots)
+            three_pass(two_parts(block[s]), (gram_refs[s][0][...], gram_refs[s][1][...]), 0)
+            for s in range(slots)
         ]
         grams = [dot_over(images[s], block[s], 1, 1, highest) for s in range(slots)]
-        inverses = lower_inverse(grams, WINDOW)
+        inverses = [two_parts(inverse) for inverse in lower_inverse(grams, WINDOW)]
         for s in range(slots):
-            image_ref[s] = three_pass(two_parts(inverses[s]), two_parts(images[s]), 0)
+            image_ref[s] = three_pass(inverses[s], two_parts(images[s]), 0)
 
         @pl.when(index == ITERS)
         def _():
             for s in range(slots):
-                final[s] = three_pass(two_parts(inverses[s]), two_parts(block[s]), 0)
+                final[s] = three_pass(inverses[s], two_parts(block[s]), 0)
 
         @pl.when(index < ITERS)
         def _():
@@ -235,9 +250,9 @@
         return carry
 
     lax.fori_loop(0, ITERS + 1, step, 0)
-    for s in range(slots):
+    for s, rows in enumerate((first_own[...], gated[:, :chunk_rows])):
         high, low = two_parts(final[s])
-        basis = dot_over(high, own_ref[s], 1, 0) + dot_over(low, own_ref[s], 1, 0)
+        basis = dot_over(high, rows, 1, 0) + dot_over(low, rows, 1, 0)
         keeps = lax.broadcasted_iota(jnp.int32, basis.shape, 0) < kept_ref[s]
         basis_ref[s] = jnp.where(keeps, basis, 0.0).T.astype(jnp.bfloat16)
 
@@ -261,10 +276,12 @@
     total_ref[...] = jnp.broadcast_to(total, total_ref.shape)
 
 
-def scale_kernel(totals_ref, part_ref, right_ref):
+def finish_kernel(totals_ref, part_ref, sent_ref, basis_ref, right_ref):
+    basis_ref[...] = sent_ref[...].astype(jnp.float32)
     total = jnp.sum(totals_ref[...], axis=0, keepdims=True)[:, :1]
+    factor = 1.0 / jnp.sqrt(total)
     for s in range(part_ref.shape[0]):
-        right_ref[s] = part_ref[s] * (1.0 / jnp.sqrt(total))
+        right_ref[s] = part_ref[s] * factor
 
 
 def smem():
@@ -310,46 +327,48 @@
     )(row, right_block, right_ops.reshape(terms * SITE, SITE))
 
 
-def gate_own(row, live, left, left_ops):
-    slots, chunk_rows, states = left.shape
+def gate_left(row, live, left_chunks, left_ops):
+    chunk_rows, states = left_chunks[0].shape
     terms = left_ops.shape[0]
     bond, wide = terms * states, SITE * SITE
     return pl.pallas_call(
-        own_kernel,
-        in_specs=[smem()] * 2 + [vmem()] * 2,
-        out_specs=[vmem()] * 3,
+        left_kernel,
+        in_specs=[smem()] * 2 + [vmem()] * (1 + len(left_chunks)),
+        out_specs=[vmem()] * 4,
         out_shape=[
-            shape_of((slots, bond, chunk_rows), jnp.bfloat16),
-            shape_of((slots, bond, bond), jnp.float32),
+            shape_of((bond, chunk_rows), jnp.bfloat16),
+            shape_of((bond, bond), jnp.bfloat16),
+            shape_of((bond, bond), jnp.bfloat16),
             shape_of((terms, 2 * wide, wide), jnp.bfloat16),
         ],
-        name="own_gate",
-        **kernel_options(8, 2e9),
-    )(row, live, left, left_ops)
-
-
-def krylov_part(row, live, kept, weight, left_chunks, left_mix, own, own_gram, start, squares):
-    slots, chunk_rows, states = left_chunks[0].shape
-    bond = own.shape[1]
-    keep = start.shape[1]
+        scratch_shapes=[pltpu.VMEM((bond, len(left_chunks) * chunk_rows), jnp.bfloat16)],
+        name="left_gate",
+        **kernel_options(10, 4e9),
+    )(row, live, left_ops, *left_chunks)
+
+
+def krylov_part(row, live, kept, weight, left_chunks, left_mix, first, start, squares):
+    chunk_rows, _ = left_chunks[0].shape
+    bond = squares[0].shape[0]
+    slots, keep, _ = start.shape
     return pl.pallas_call(
         krylov_kernel,
-        in_specs=[smem()] * 4 + [vmem()] * (len(left_chunks) + 4 + len(squares)),
+        in_specs=[smem()] * 4 + [vmem()] * (len(left_chunks) + 2 + len(first) + len(squares)),
         out_specs=[vmem()] * 2,
         out_shape=[
             shape_of((slots, chunk_rows, keep), jnp.bfloat16),
             shape_of((slots, keep, bond), jnp.float32),
         ],
         scratch_shapes=[
-            pltpu.VMEM((slots, bond, len(left_chunks) * chunk_rows), jnp.bfloat16),
-            pltpu.VMEM((slots, bond, bond), jnp.bfloat16),
-            pltpu.VMEM((slots, bond, bond), jnp.bfloat16),
+            pltpu.VMEM((bond, len(left_chunks) * chunk_rows), jnp.bfloat16),
+            pltpu.VMEM((bond, bond), jnp.bfloat16),
+            pltpu.VMEM((bond, bond), jnp.bfloat16),
             pltpu.VMEM((slots, keep, bond), jnp.float32),
             pltpu.VMEM((slots, keep, bond), jnp.float32),
         ],
         name="krylov",
-        **kernel_options(16, 2e10),
-    )(row, live, kept, weight, *left_chunks, left_mix, own, own_gram, start, *squares)
+        **kernel_options(14, 2e10),
+    )(row, live, kept, weight, *left_chunks, left_mix, *first, start, *squares)
 
 
 def truncated(kept, weight, image, squares, locals_, peers):
@@ -368,15 +387,15 @@
     )(kept, weight, image, *squares, *locals_)
 
 
-def scaled(totals, part):
+def finished(totals, part, sent):
     return pl.pallas_call(
-        scale_kernel,
-        in_specs=[vmem()] * 2,
-        out_specs=vmem(),
-        out_shape=shape_of(part.shape, jnp.float32),
-        name="scale",
+        finish_kernel,
+        in_specs=[vmem()] * 3,
+        out_specs=[vmem()] * 2,
+        out_shape=[shape_of(sent.shape, jnp.float32), shape_of(part.shape, jnp.float32)],
+        name="finish",
         **kernel_options(4, 1e6),
-    )(totals, part)
+    )(totals, part, sent)
 
 
 def on_device(left_block, right_block, left_ops, right_ops, charges, live_states, kept, start):
@@ -392,26 +411,33 @@
     weight = jnp.exp(-chemical * cut(charges, right_first).astype(jnp.float32))
     start_here = cut(start, left_first)[:, :, None]
     local_cols = right_block.shape[2] // lax.axis_size("row")
-    left_theirs = from_partner(left_block, SEC, top_bit)
+    rows = lax.axis_size("row")
+
+    def over_rows(chunk):
+        sent = [
+            lax.ppermute(chunk, "row", [(i, (i + d) % rows) for i in range(rows)])
+            for d in range(1, rows)
+        ]
+        return [chunk, *sent]
+
+    theirs = [from_partner(left_block[s], SEC, top_bit) for s in range(slots)]
     first = list(gate_right(0, row, right_block, right_ops, local_cols))
-    left_theirs, first[0], row_later = lax.optimization_barrier((left_theirs, first[0], row))
-    rows = lax.axis_size("row")
-    left_chunks = [
-        lax.ppermute(left_theirs, "row", [(i, (i + d) % rows) for i in range(rows)])
-        for d in range(1, rows)
-    ]
-    second = gate_right(1, row_later, right_block, right_ops, local_cols)
-    own, own_gram, left_mix = gate_own(row_later, live, left_theirs, left_ops)
+    theirs[0], first[0], row_second = lax.optimization_barrier((theirs[0], first[0], row))
+    first_chunks = over_rows(theirs[0])
+    second = list(gate_right(1, row_second, right_block, right_ops, local_cols))
+    theirs[1], second[0], row_left = lax.optimization_barrier((theirs[1], second[0], row))
+    second_chunks = over_rows(theirs[1])
+    *first_left, left_mix = gate_left(row_left, live, first_chunks, left_ops)
     squares = (*first[:2], *second[:2])
     basis, image = krylov_part(
-        row, live, kept_here, weight, left_chunks, left_mix, own, own_gram, start_here, squares
+        row, live, kept_here, weight, second_chunks, left_mix, first_left, start_here, squares
     )
     basis = from_partner(basis, SEC, top_bit)
     right_part, total = truncated(
         kept_here, weight, image, squares, (first[2], second[2]), lax.axis_size(SEC)
     )
     totals = lax.all_to_all(total, SEC, split_axis=0, concat_axis=0, tiled=True)
-    return basis.astype(jnp.float32), scaled(totals, right_part)
+    return tuple(finished(totals, right_part, basis))
 
 
 def solution(mesh):

time: 85.9 us -> 83.4 us (0.971)
  starting transfers between devices: 11.8 us -> 19.4 us
  waiting for transfers between devices: 8.08 us -> 2.07 us
  blocking collectives: 24.8 us -> 21.3 us
  other arithmetic: 1.56 us -> 0.08 us
  local copies, waits for them, and re-layouts: 3.6 us -> 5.08 us
    ppermute x3 -> x6, waiting for transfers between devices: 8.07 us -> 2.06 us  [over_rows(): lax.ppermute(chunk, 'row', [(i, (i + d) % rows) for i in range(rows)])]
    ppermute x2 -> x3, starting transfers between devices: 7.92 us -> 12.1 us  [from_partner(): return lax.ppermute(value, axis, pairs)]
    all_to_all x1, blocking collectives: 24.8 us -> 21.3 us  [on_device(): totals = lax.all_to_all(total, SEC, split_axis=0, concat_axis=0, tiled=True)]
    ppermute x3 -> x6, starting transfers between devices: 3.86 us -> 7.32 us  [over_rows(): lax.ppermute(chunk, 'row', [(i, (i + d) % rows) for i in range(rows)])]
    pallas_call x1, Pallas kernels: 23.2 us -> 21.3 us  [krylov_part(): pl.pallas_call(krylov_kernel, in_specs=[smem()] * 4 + [vmem()] * (len(lef...]
    unnamed x8 -> x16, local copies, waits for them, and re-layouts: 2 us -> 3.77 us
    dynamic_slice x2, local copies, waits for them, and re-layouts: 1.46 us -> 0.15 us  [on_device(): cut = lambda table, first: lax.dynamic_slice_in_dim(table, first, slots, 0)]
    squeeze x0 -> x1, local copies, waits for them, and re-layouts: none -> 1.02 us  [on_device(): theirs = [from_partner(left_block[s], SEC, top_bit) for s in range(slots)]]
  transfers between devices with their start and end apart: 5 -> 9, of which waited for: 2 -> 2; matrix products, arithmetic and copies ran while one was open for 3% -> 0% of each run, Pallas kernels for 14% -> 14%
where the time goes in v5:
time: 83.4 us; the launch traced here: 83.1 us
  Pallas kernels  34.3 us (41%)
  blocking collectives  21.3 us (26%)
  starting transfers between devices  19.4 us (23%)
  local copies, waits for them, and re-layouts  5.08 us (6%)
  waiting for transfers between devices  2.07 us (2%)
    pallas_call x1, Pallas kernels, krylov_part(): pl.pallas_call(krylov_kernel, in_specs=[smem()] * 4 + [vmem()] * (len(lef...  21.3 us
    all_to_all x1, blocking collectives, on_device(): totals = lax.all_to_all(total, SEC, split_axis=0, concat_axis=0, tiled=True)  21.3 us
    ppermute x3, starting transfers between devices, from_partner(): return lax.ppermute(value, axis, pairs)  12.1 us
    ppermute x6, starting transfers between devices, over_rows(): lax.ppermute(chunk, 'row', [(i, (i + d) % rows) for i in range(rows)])  7.32 us
    pallas_call x2, Pallas kernels, gate_right(): pl.pallas_call(functools.partial(right_kernel, slot), in_specs=[smem(), p...  6.84 us
    unnamed x16, local copies, waits for them, and re-layouts  3.77 us
    pallas_call x1, Pallas kernels, gate_left(): pl.pallas_call(left_kernel, in_specs=[smem()] * 2 + [vmem()] * (1 + len(l...  3.71 us
    ppermute x6, waiting for transfers between devices, over_rows(): lax.ppermute(chunk, 'row', [(i, (i + d) % rows) for i in range(rows)])  2.06 us
  transfers between devices with their start and end apart: 9, of which 2 were waited for; matrix products, arithmetic and copies ran while one was open for 0% of the time, Pallas kernels for 14%

profile of v5, /device:TPU:1, one launch (start us, length us, event | category | flops | bytes accessed | tf_op | source)
XLA Modules:
  0.0 83.1 jit_solution(16563513921020895773)
XLA Ops:
  0.6 0.0 copy-start
  0.6 1.0 %slice_bitcast_fusion = (bf16[512,128]{1,0:T(8,128)(2,1)S(1)}, bf16[512,128]{1,0:T(8,128)(2,1)S(1)}) fusion(bf16[2,512,128]{2,1,0:T(8,128)(2,1)} %param.8), kind=kLoop, calls=%fused_computation | loop fusion | bytes 524288 | tf_op jit(solution)/shard_map/squeeze | solution.py:423
  1.7 7.8 %collective-permute-start.1 = (bf16[512,128]{1,0:T(8,128)(2,1)S(1)}, bf16[512,128]{1,0:T(8,128)(2,1)S(1)}, u32[]{:S(2)}, u32[]{:S(2)}) collective-permute-start(bf16[512,128]{1,0:T(8,128)(2,1)S(1)} %get-tuple-element.42), channel_id=1, source_target_pairs={{0,128},{4,132},{8,136},{12,140},{16,144},{20,148},{24,152},{28,15... | collective-permute-start | bytes 393224 | tf_op jit(solution)/shard_map/ppermute | solution.py:24
  9.5 0.0 copy-start.3
  9.5 0.1 collective-permute-start
  9.6 0.6 copy-done.3
  10.2 0.0 copy-start.1
  10.3 1.2 %copy-done.1 = bf16[2,128,2048]{2,1,0:T(8,128)(2,1)S(1)} copy-done((bf16[2,128,2048]{2,1,0:T(8,128)(2,1)S(1)}, bf16[2,128,2048]{2,1,0:T(8,128)(2,1)}, u32[]{:S(2)}) %copy-start.1) | copy-done | bytes 1048600
  11.5 0.0 copy-start.2
  11.5 3.4 %right_gate.2 = (bf16[512,512]{1,0:T(8,128)(2,1)S(1)}, bf16[512,512]{1,0:T(8,128)(2,1)S(1)}, bf16[512,512]{1,0:T(8,128)(2,1)S(1)}) custom-call(s32[1]{0:T(128)} %bitcast.row_ref, bf16[2,128,2048]{2,1,0:T(8,128)(2,1)S(1)} %copy-done.1, f32[64,16]{1,0:T(8,128)S(1)} %bitcast.14), custom_call_target="tpu_custom_call" | custom-call | flops 4000000000 | bytes 2097152 | tf_op jit(solution)/shard_map/right_gate/pallas_call | solution.py:310
  14.9 0.0 copy-done
  14.9 0.0 copy-start.5
  14.9 0.6 copy-done.5
  15.6 0.1 dynamic_slice.14.live_ref
  15.7 0.1 copy.11.refs_8_
  15.8 0.0 copy-start.6
  15.8 0.7 copy-done.6
  16.5 0.0 copy-start.7
  16.5 0.1 dynamic_slice.12.kept_ref
  16.5 0.6 copy-done.7
  17.1 0.1 multiply_exponential_fusion.weight_ref
  17.2 0.0 collective-permute-done.1.refs_0_
  17.2 0.0 copy-start.4
  17.2 2.8 %collective-permute-start.7 = (bf16[512,128]{1,0:T(8,128)(2,1)S(1)}, bf16[512,128]{1,0:T(8,128)(2,1)S(1)}, u32[]{:S(2)}, u32[]{:S(2)}) collective-permute-start(bf16[512,128]{1,0:T(8,128)(2,1)S(1)} %collective-permute-done.1.refs_0_), channel_id=1, source_target_pairs={{0,3},{1,0},{2,1},{3,2},{4,7},{5,4},{6,5},{7,6},{8,11},{9,8},{10,9... | collective-permute-start | bytes 393224 | tf_op jit(solution)/shard_map/ppermute | solution.py:418
  20.0 0.3 collective-permute-start.6
  20.4 0.7 collective-permute-start.5
  21.0 0.0 copy-done.2
  21.0 3.4 %right_gate.3 = (bf16[512,512]{1,0:T(8,128)(2,1)S(1)}, bf16[512,512]{1,0:T(8,128)(2,1)S(1)}, bf16[512,512]{1,0:T(8,128)(2,1)S(1)}) custom-call(s32[1]{0:T(128)} %bitcast.row_ref, bf16[2,128,2048]{2,1,0:T(8,128)(2,1)S(1)} %copy-done.2, f32[64,16]{1,0:T(8,128)S(1)} %bitcast.15), custom_call_target="tpu_custom_call" | custom-call | flops 4000000000 | bytes 2097152 | tf_op jit(solution)/shard_map/right_gate/pallas_call | solution.py:310
  24.5 0.0 collective-permute-done.refs_0_
  24.5 2.1 %collective-permute-start.4 = (bf16[512,128]{1,0:T(8,128)(2,1)S(1)}, bf16[512,128]{1,0:T(8,128)(2,1)S(1)}, u32[]{:S(2)}, u32[]{:S(2)}) collective-permute-start(bf16[512,128]{1,0:T(8,128)(2,1)S(1)} %collective-permute-done.refs_0_), channel_id=1, source_target_pairs={{0,3},{1,0},{2,1},{3,2},{4,7},{5,4},{6,5},{7,6},{8,11},{9,8},{10,9... | collective-permute-start | bytes 393224 | tf_op jit(solution)/shard_map/ppermute | solution.py:418
  26.6 1.4 %collective-permute-start.3 = (bf16[512,128]{1,0:T(8,128)(2,1)S(1)}, bf16[512,128]{1,0:T(8,128)(2,1)S(1)}, u32[]{:S(2)}, u32[]{:S(2)}) collective-permute-start(bf16[512,128]{1,0:T(8,128)(2,1)S(1)} %collective-permute-done.refs_0_), channel_id=1, source_target_pairs={{0,2},{1,3},{2,0},{3,1},{4,6},{5,7},{6,4},{7,5},{8,10},{9,11},{10,... | collective-permute-start | bytes 393224 | tf_op jit(solution)/shard_map/ppermute | solution.py:418
  28.0 0.0 collective-permute-done.7.refs_3_
  28.0 0.0 collective-permute-start.2
  28.0 0.0 collective-permute-done.6.refs_2_
  28.0 1.3 %collective-permute-done.5.refs_1_ = bf16[512,128]{1,0:T(8,128)(2,1)S(1)} collective-permute-done((bf16[512,128]{1,0:T(8,128)(2,1)S(1)}, bf16[512,128]{1,0:T(8,128)(2,1)S(1)}, u32[]{:S(2)}, u32[]{:S(2)}) %collective-permute-start.5) | collective-permute-done | bytes 131104 | tf_op jit(solution)/shard_map/ppermute | solution.py:418
  29.3 0.0 copy-done.4
  29.3 3.7 %left_gate.1 = (bf16[512,512]{1,0:T(8,128)(2,1)S(1)}, bf16[512,512]{1,0:T(8,128)(2,1)S(1)}, bf16[512,512]{1,0:T(8,128)(2,1)S(1)}, bf16[4,512,256]{2,1,0:T(8,128)(2,1)S(1)}) custom-call(s32[1]{0:T(128)} %bitcast.row_ref, s32[2]{0:T(128)S(1)} %dynamic_slice.14.live_ref, f32[4,16,16]{2,1,0:T(8,128)S(1)} %copy-done.4, ...), custom_call_target="tpu_custom_call" | custom-call | flops 4000000000 | bytes 2097152 | tf_op jit(solution)/shard_map/left_gate/pallas_call | solution.py:334
  33.0 0.0 collective-permute-done.4.refs_3_
  33.0 0.0 collective-permute-done.3.refs_2_
  33.0 0.8 collective-permute-done.2.refs_1_
  33.8 21.3 %krylov.1 = (bf16[2,512,128]{2,1,0:T(8,128)(2,1)S(1)}, f32[2,128,512]{2,1,0:T(8,128)S(1)}) custom-call(s32[1]{0:T(128)} %bitcast.row_ref, s32[2]{0:T(128)S(1)} %dynamic_slice.14.live_ref, s32[2]{0:T(128)S(1)} %dynamic_slice.12.kept_ref, f32[2]{0:T(128)S(1)} %multiply_exponential_fusion.weight_ref, bf16[512,128]{1,0:T(8,128)(2,1)S(1)} %collective-permute-done.refs_0_, ...), custom_call_target="tpu_custom_call" | custom-call | flops 20000000000 | bytes 2097152 | tf_op jit(solution)/shard_map/krylov/pallas_call | solution.py:354
  55.1 4.2 %collective-permute-start.8 = (bf16[2,512,128]{2,1,0:T(8,128)(2,1)S(1)}, bf16[2,512,128]{2,1,0:T(8,128)(2,1)S(1)}, u32[]{:S(2)}, u32[]{:S(2)}) collective-permute-start(bf16[2,512,128]{2,1,0:T(8,128)(2,1)S(1)} %get-tuple-element.41), channel_id=1, source_target_pairs={{0,128},{4,132},{8,136},{12,140},{16,144},{20,148},{24,152},{28,15... | collective-permute-start | bytes 786440 | tf_op jit(solution)/shard_map/ppermute | solution.py:24
  59.3 1.4 %truncate.1 = (f32[2,128,512]{2,1,0:T(8,128)S(1)}, f32[64,128]{1,0:T(8,128)S(1)}) custom-call(s32[2]{0:T(128)S(1)} %dynamic_slice.12.kept_ref, f32[2]{0:T(128)S(1)} %multiply_exponential_fusion.weight_ref, f32[2,128,512]{2,1,0:T(8,128)S(1)} %get-tuple-element.36.image_ref, bf16[512,512]{1,0:T(8,128)(2,1)S(1)} %get-tuple-element.32.refs_9_.refs_0_, ...), custom_call_target="tpu_custom_call" | custom-call | flops 2000000000 | bytes 2097152 | tf_op jit(solution)/shard_map/truncate/pallas_call | solution.py:377
  60.8 21.3 %all_to_all.11 = f32[64,1,128]{2,1,0:T(1,128)S(1)} all-to-all(f32[64,1,128]{2,1,0:T(1,128)S(1)} %bitcast.13), channel_id=1, replica_groups=mesh['sec_0'=8,'sec_1'=4,'sec_2'=2,'row'=4] {'sec_0','sec_1','sec_2'}, dimensions={0} | all-to-all | bytes 65536 | tf_op jit(solution)/shard_map/all_to_all | solution.py:439
  82.1 0.0 collective-permute-done.8.sent_ref
  82.1 1.0 %finish.1 = (f32[2,512,128]{2,1,0:T(8,128)}, f32[2,128,512]{2,1,0:T(8,128)}) custom-call(f32[64,128]{1,0:T(8,128)S(1)} %bitcast.12, f32[2,128,512]{2,1,0:T(8,128)S(1)} %get-tuple-element.40.part_ref, bf16[2,512,128]{2,1,0:T(8,128)(2,1)S(1)} %collective-permute-done.8.sent_ref), custom_call_target="tpu_custom_call" | custom-call | flops 1000000 | bytes 2097152 | tf_op jit(solution)/shard_map/finish/pallas_call | solution.py:391
  (1 shorter events, 0.0 us)
Async XLA Ops:
  0.6 14.3 %copy-start = (s32[128,128]{1,0:T(8,128)S(1)}, s32[128,128]{1,0:T(8,128)}, u32[]{:S(2)}) copy-start(s32[128,128]{1,0:T(8,128)} %param.15) | copy-start | bytes 196612
  1.7 15.5 %collective-permute-start.1 = (bf16[512,128]{1,0:T(8,128)(2,1)S(1)}, bf16[512,128]{1,0:T(8,128)(2,1)S(1)}, u32[]{:S(2)}, u32[]{:S(2)}) collective-permute-start(bf16[512,128]{1,0:T(8,128)(2,1)S(1)} %get-tuple-element.42), channel_id=1, source_target_pairs={{0,128},{4,132},{8,136},{12,140},{16,144},{20,148},{24,152},{28,15... | collective-permute-start | bytes 393224 | tf_op jit(solution)/shard_map/ppermute | solution.py:24
  9.5 0.8 copy-start.3
  9.5 15.0 %collective-permute-start = (bf16[512,128]{1,0:T(8,128)(2,1)S(1)}, bf16[512,128]{1,0:T(8,128)(2,1)S(1)}, u32[]{:S(2)}, u32[]{:S(2)}) collective-permute-start(bf16[512,128]{1,0:T(8,128)(2,1)S(1)} %get-tuple-element.43), channel_id=1, source_target_pairs={{0,128},{4,132},{8,136},{12,140},{16,144},{20,148},{24,152},{28,15... | collective-permute-start | bytes 393224 | tf_op jit(solution)/shard_map/ppermute | solution.py:24
  10.2 1.2 %copy-start.1 = (bf16[2,128,2048]{2,1,0:T(8,128)(2,1)S(1)}, bf16[2,128,2048]{2,1,0:T(8,128)(2,1)}, u32[]{:S(2)}) copy-start(bf16[2,128,2048]{2,1,0:T(8,128)(2,1)} %right_ref.3) | copy-start | bytes 3145732
  11.5 9.6 %copy-start.2 = (bf16[2,128,2048]{2,1,0:T(8,128)(2,1)S(1)}, bf16[2,128,2048]{2,1,0:T(8,128)(2,1)}, u32[]{:S(2)}) copy-start(bf16[2,128,2048]{2,1,0:T(8,128)(2,1)} %right_ref.3) | copy-start | bytes 3145732
  14.9 0.7 copy-start.5
  15.8 0.7 copy-start.6
  16.5 0.7 copy-start.7
  17.2 12.1 %copy-start.4 = (f32[4,16,16]{2,1,0:T(8,128)S(1)}, f32[4,16,16]{2,1,0:T(8,128)}, u32[]{:S(2)}) copy-start(f32[4,16,16]{2,1,0:T(8,128)} %left_ops_ref.1) | copy-start | bytes 12292
  17.2 10.8 %collective-permute-start.7 = (bf16[512,128]{1,0:T(8,128)(2,1)S(1)}, bf16[512,128]{1,0:T(8,128)(2,1)S(1)}, u32[]{:S(2)}, u32[]{:S(2)}) collective-permute-start(bf16[512,128]{1,0:T(8,128)(2,1)S(1)} %collective-permute-done.1.refs_0_), channel_id=1, source_target_pairs={{0,3},{1,0},{2,1},{3,2},{4,7},{5,4},{6,5},{7,6},{8,11},{9,8},{10,9... | collective-permute-start | bytes 393224 | tf_op jit(solution)/shard_map/ppermute | solution.py:418
  20.0 8.0 %collective-permute-start.6 = (bf16[512,128]{1,0:T(8,128)(2,1)S(1)}, bf16[512,128]{1,0:T(8,128)(2,1)S(1)}, u32[]{:S(2)}, u32[]{:S(2)}) collective-permute-start(bf16[512,128]{1,0:T(8,128)(2,1)S(1)} %collective-permute-done.1.refs_0_), channel_id=1, source_target_pairs={{0,2},{1,3},{2,0},{3,1},{4,6},{5,7},{6,4},{7,5},{8,10},{9,11},{10,... | collective-permute-start | bytes 393224 | tf_op jit(solution)/shard_map/ppermute | solution.py:418
  20.4 8.9 %collective-permute-start.5 = (bf16[512,128]{1,0:T(8,128)(2,1)S(1)}, bf16[512,128]{1,0:T(8,128)(2,1)S(1)}, u32[]{:S(2)}, u32[]{:S(2)}) collective-permute-start(bf16[512,128]{1,0:T(8,128)(2,1)S(1)} %collective-permute-done.1.refs_0_), channel_id=1, source_target_pairs={{0,1},{1,2},{2,3},{3,0},{4,5},{5,6},{6,7},{7,4},{8,9},{9,10},{10,1... | collective-permute-start | bytes 393224 | tf_op jit(solution)/shard_map/ppermute | solution.py:418
  24.5 8.5 %collective-permute-start.4 = (bf16[512,128]{1,0:T(8,128)(2,1)S(1)}, bf16[512,128]{1,0:T(8,128)(2,1)S(1)}, u32[]{:S(2)}, u32[]{:S(2)}) collective-permute-start(bf16[512,128]{1,0:T(8,128)(2,1)S(1)} %collective-permute-done.refs_0_), channel_id=1, source_target_pairs={{0,3},{1,0},{2,1},{3,2},{4,7},{5,4},{6,5},{7,6},{8,11},{9,8},{10,9... | collective-permute-start | bytes 393224 | tf_op jit(solution)/shard_map/ppermute | solution.py:418
  26.6 6.5 %collective-permute-start.3 = (bf16[512,128]{1,0:T(8,128)(2,1)S(1)}, bf16[512,128]{1,0:T(8,128)(2,1)S(1)}, u32[]{:S(2)}, u32[]{:S(2)}) collective-permute-start(bf16[512,128]{1,0:T(8,128)(2,1)S(1)} %collective-permute-done.refs_0_), channel_id=1, source_target_pairs={{0,2},{1,3},{2,0},{3,1},{4,6},{5,7},{6,4},{7,5},{8,10},{9,11},{10,... | collective-permute-start | bytes 393224 | tf_op jit(solution)/shard_map/ppermute | solution.py:418
  28.0 5.8 %collective-permute-start.2 = (bf16[512,128]{1,0:T(8,128)(2,1)S(1)}, bf16[512,128]{1,0:T(8,128)(2,1)S(1)}, u32[]{:S(2)}, u32[]{:S(2)}) collective-permute-start(bf16[512,128]{1,0:T(8,128)(2,1)S(1)} %collective-permute-done.refs_0_), channel_id=1, source_target_pairs={{0,1},{1,2},{2,3},{3,0},{4,5},{5,6},{6,7},{7,4},{8,9},{9,10},{10,1... | collective-permute-start | bytes 393224 | tf_op jit(solution)/shard_map/ppermute | solution.py:418
  55.1 27.0 %collective-permute-start.8 = (bf16[2,512,128]{2,1,0:T(8,128)(2,1)S(1)}, bf16[2,512,128]{2,1,0:T(8,128)(2,1)S(1)}, u32[]{:S(2)}, u32[]{:S(2)}) collective-permute-start(bf16[2,512,128]{2,1,0:T(8,128)(2,1)S(1)} %get-tuple-element.41), channel_id=1, source_target_pairs={{0,128},{4,132},{8,136},{12,140},{16,144},{20,148},{24,152},{28,15... | collective-permute-start | bytes 786440 | tf_op jit(solution)/shard_map/ppermute | solution.py:24

commit v6 on v5

--- a/solution.py
+++ b/solution.py
@@ -54,6 +54,7 @@
     n = grams[0].shape[0]
     lane = lax.broadcasted_iota(jnp.int32, (8, n), 1)
     sub = lax.broadcasted_iota(jnp.int32, (8, n), 0)
+    spots = [jnp.full((8, n), m, jnp.int32) for m in range(8)]
     rows = [[g[8 * q : 8 * q + 8, :] for q in range(n // 8)] for g in grams]
     span = window // 8
     for first in range(0, n // 8, span):
@@ -64,7 +65,7 @@
             unit = (lane - k == sub).astype(jnp.float32)
             for mat in rows:
                 cols = {
-                    r: [jnp.broadcast_to(mat[r][:, k + m : k + m + 1], (8, n)) for m in range(8)]
+                    r: [jnp.take_along_axis(mat[r], spots[m] + k, axis=1) for m in range(8)]
                     for r in range(q, last)
                 }
                 for r in range(q, last):
@@ -113,7 +114,8 @@
 
 
 def right_kernel(
-    slot, row_ref, right_ref, right_ops_ref, high_ref, low_ref, local_ref, right_mix, gated, right, sem
+    slot, rows, place_ref, right_ref, right_ops_ref, high_ref, low_ref, local_ref,
+    right_mix, gated, right, sem,
 ):
     states = right.shape[0]
     terms = gated.shape[0] // states
@@ -155,7 +157,7 @@
                         i * states : (i + 1) * states,
                     ] = mixed[i * SITE : (i + 1) * SITE, h * states : (h + 1) * states]
     high_ref[...], low_ref[...] = two_parts(dot_over(gated[...], gated[...], 1, 1))
-    offset = pl.multiple_of(row_ref[0] * local_cols, local_cols)
+    offset = pl.multiple_of(lax.rem(place_ref[0], rows) * local_cols, local_cols)
     local_ref[...] = gated[:, pl.ds(offset, local_cols)]
 
 
@@ -193,24 +195,38 @@
             ] = mixed[b * states : (b + 1) * states, :]
 
 
-def gate_sector(row_ref, live, left_refs, left_mix, gated):
+def gate_sector(row, live, left_refs, left_mix, gated):
     chunks = len(left_refs)
     chunk_rows = left_refs[0].shape[0]
     for c in range(chunks):
-        first_row = lax.rem(row_ref[0] + (chunks - c), chunks) * chunk_rows
+        first_row = lax.rem(row + (chunks - c), chunks) * chunk_rows
         gate_chunk(left_refs[c], live, first_row, left_mix, gated, c * chunk_rows)
     return two_parts(dot_over(gated[...], gated[...], 1, 1))
 
 
-def left_kernel(row_ref, live_ref, left_ops_ref, *refs):
+def place(place_ref, rows, slots, sectors):
+    row = lax.rem(place_ref[0], rows)
+    right_first = lax.div(place_ref[0], rows) * slots
+    return row, lax.rem(right_first + sectors // 2, sectors), right_first
+
+
+def weight_of(charges_ref, sector):
+    charge = charges_ref[sector].astype(jnp.float32)
+    return jnp.exp(jnp.full((1, 1), -chemical * charge, jnp.float32))
+
+
+def left_kernel(slots, place_ref, live_ref, left_ops_ref, *refs):
     left_refs = refs[:-5]
+    row, left_first, _ = place(place_ref, len(left_refs), slots, live_ref.shape[0])
     own_ref, high_ref, low_ref, left_mix, gated = refs[-5:]
     build_left_mix(left_ops_ref, left_mix)
-    high_ref[...], low_ref[...] = gate_sector(row_ref, live_ref[0], left_refs, left_mix, gated)
+    high_ref[...], low_ref[...] = gate_sector(
+        row, live_ref[left_first], left_refs, left_mix, gated
+    )
     own_ref[...] = gated[:, : own_ref.shape[1]]
 
 
-def krylov_kernel(row_ref, live_ref, kept_ref, weight_ref, *refs):
+def krylov_kernel(place_ref, live_ref, kept_ref, charges_ref, *refs):
     chunks = len(refs) - 16
     left_refs = refs[:chunks]
     (left_mix, first_own, first_high, first_low, start_ref) = refs[chunks : chunks + 5]
@@ -219,11 +235,17 @@
     (gated, second_high, second_low, block, final) = refs[chunks + 11 :]
     slots, keep, bond = image_ref.shape
     chunk_rows = left_refs[0].shape[0]
-    second_high[...], second_low[...] = gate_sector(row_ref, live_ref[1], left_refs, left_mix, gated)
+    row, left_first, right_first = place(place_ref, chunks, slots, live_ref.shape[0])
+    second_high[...], second_low[...] = gate_sector(
+        row, live_ref[left_first + 1], left_refs, left_mix, gated
+    )
     gram_refs = ((first_high, first_low), (second_high, second_low))
     for s in range(slots):
-        spots = lax.broadcasted_iota(jnp.int32, (keep, bond), 1)
-        block[s] = jnp.where(spots == start_ref[s], 1.0, 0.0)
+        columns = start_ref[pl.ds(left_first + s, 1), :].astype(jnp.float32)
+        columns = jnp.broadcast_to(columns, (8, keep)).T[:, :1]
+        spots = lax.broadcasted_iota(jnp.int32, (keep, bond), 1).astype(jnp.float32)
+        block[s] = jnp.where(spots == columns, 1.0, 0.0)
+    weights = [weight_of(charges_ref, right_first + s) for s in range(slots)]
 
     def step(index, carry):
         images = [
@@ -244,7 +266,7 @@
         def _():
             for s in range(slots):
                 squares = (square_refs[2 * s][...], square_refs[2 * s + 1][...])
-                scale = weight_ref[s] * weight_ref[s]
+                scale = weights[s] * weights[s]
                 block[s] = scale * three_pass(two_parts(image_ref[s]), squares, 0)
 
         return carry
@@ -253,26 +275,29 @@
     for s, rows in enumerate((first_own[...], gated[:, :chunk_rows])):
         high, low = two_parts(final[s])
         basis = dot_over(high, rows, 1, 0) + dot_over(low, rows, 1, 0)
-        keeps = lax.broadcasted_iota(jnp.int32, basis.shape, 0) < kept_ref[s]
+        keeps = lax.broadcasted_iota(jnp.int32, basis.shape, 0) < kept_ref[right_first + s]
         basis_ref[s] = jnp.where(keeps, basis, 0.0).T.astype(jnp.bfloat16)
 
 
-def truncate_kernel(kept_ref, weight_ref, image_ref, *refs):
+def truncate_kernel(rows, place_ref, kept_ref, charges_ref, image_ref, *refs):
+    _, _, right_first = place(place_ref, rows, image_ref.shape[0], kept_ref.shape[0])
     square_refs, local_refs, (right_ref, total_ref) = refs[:4], refs[4:6], refs[6:]
     total = jnp.zeros((1, 1), jnp.float32)
     for s in range(image_ref.shape[0]):
         image = image_ref[s]
         high, low = two_parts(image)
-        keeps = lax.broadcasted_iota(jnp.int32, image.shape, 0) < kept_ref[s]
-        scale = weight_ref[s] * weight_ref[s]
+        kept = kept_ref[right_first + s]
+        weight = weight_of(charges_ref, right_first + s)
+        keeps = lax.broadcasted_iota(jnp.int32, image.shape, 0) < kept
+        scale = weight * weight
         squares = (square_refs[2 * s][...], square_refs[2 * s + 1][...])
         squared = scale * three_pass((high, low), squares, 0) * image
         squared = jnp.where(keeps, squared, 0.0)
         total += jnp.sum(jnp.sum(squared, axis=0, keepdims=True), axis=1, keepdims=True)
         local = local_refs[s][...]
         part = dot_over(high, local, 1, 0) + dot_over(low, local, 1, 0)
-        keeps = lax.broadcasted_iota(jnp.int32, part.shape, 0) < kept_ref[s]
-        right_ref[s] = jnp.where(keeps, part * weight_ref[s], 0.0)
+        keeps = lax.broadcasted_iota(jnp.int32, part.shape, 0) < kept
+        right_ref[s] = jnp.where(keeps, part * weight, 0.0)
     total_ref[...] = jnp.broadcast_to(total, total_ref.shape)
 
 
@@ -308,7 +333,7 @@
     terms = right_ops.shape[0]
     bond, wide = terms * states, SITE * SITE
     return pl.pallas_call(
-        functools.partial(right_kernel, slot),
+        functools.partial(right_kernel, slot, cols // local_cols),
         in_specs=[smem(), pl.BlockSpec(memory_space=pltpu.HBM), vmem()],
         out_specs=[vmem()] * 3,
         out_shape=[
@@ -327,12 +352,12 @@
     )(row, right_block, right_ops.reshape(terms * SITE, SITE))
 
 
-def gate_left(row, live, left_chunks, left_ops):
+def gate_left(slots, row, live, left_chunks, left_ops):
     chunk_rows, states = left_chunks[0].shape
     terms = left_ops.shape[0]
     bond, wide = terms * states, SITE * SITE
     return pl.pallas_call(
-        left_kernel,
+        functools.partial(left_kernel, slots),
         in_specs=[smem()] * 2 + [vmem()] * (1 + len(left_chunks)),
         out_specs=[vmem()] * 4,
         out_shape=[
@@ -347,10 +372,10 @@
     )(row, live, left_ops, *left_chunks)
 
 
-def krylov_part(row, live, kept, weight, left_chunks, left_mix, first, start, squares):
+def krylov_part(slots, row, live, kept, charges, left_chunks, left_mix, first, start, squares):
     chunk_rows, _ = left_chunks[0].shape
     bond = squares[0].shape[0]
-    slots, keep, _ = start.shape
+    keep = start.shape[1]
     return pl.pallas_call(
         krylov_kernel,
         in_specs=[smem()] * 4 + [vmem()] * (len(left_chunks) + 2 + len(first) + len(squares)),
@@ -368,15 +393,15 @@
         ],
         name="krylov",
         **kernel_options(14, 2e10),
-    )(row, live, kept, weight, *left_chunks, left_mix, *first, start, *squares)
-
-
-def truncated(kept, weight, image, squares, locals_, peers):
+    )(row, live, kept, charges, *left_chunks, left_mix, *first, start, *squares)
+
+
+def truncated(rows, row, kept, charges, image, squares, locals_, peers):
     slots, keep, _ = image.shape
     local_cols = locals_[0].shape[1]
     return pl.pallas_call(
-        truncate_kernel,
-        in_specs=[smem()] * 2 + [vmem()] * (1 + len(squares) + len(locals_)),
+        functools.partial(truncate_kernel, rows),
+        in_specs=[smem()] * 3 + [vmem()] * (1 + len(squares) + len(locals_)),
         out_specs=[vmem()] * 2,
         out_shape=[
             shape_of((slots, keep, local_cols), jnp.float32),
@@ -384,7 +409,7 @@
         ],
         name="truncate",
         **kernel_options(8, 2e9),
-    )(kept, weight, image, *squares, *locals_)
+    )(row, kept, charges, image, *squares, *locals_)
 
 
 def finished(totals, part, sent):
@@ -400,16 +425,8 @@
 
 def on_device(left_block, right_block, left_ops, right_ops, charges, live_states, kept, start):
     slots = left_block.shape[0]
-    sectors = slots * lax.axis_size(SEC)
     top_bit = lax.axis_size(SEC).bit_length() - 2
-    right_first = lax.axis_index(SEC) * slots
-    left_first = (right_first + sectors // 2) % sectors
-    cut = lambda table, first: lax.dynamic_slice_in_dim(table, first, slots, 0)
-    row = lax.axis_index("row").astype(jnp.int32).reshape(1)
-    live = cut(live_states, left_first)
-    kept_here = cut(kept, right_first)
-    weight = jnp.exp(-chemical * cut(charges, right_first).astype(jnp.float32))
-    start_here = cut(start, left_first)[:, :, None]
+    row = lax.axis_index(SEC_ROW).astype(jnp.int32).reshape(1)
     local_cols = right_block.shape[2] // lax.axis_size("row")
     rows = lax.axis_size("row")
 
@@ -427,14 +444,14 @@
     second = list(gate_right(1, row_second, right_block, right_ops, local_cols))
     theirs[1], second[0], row_left = lax.optimization_barrier((theirs[1], second[0], row))
     second_chunks = over_rows(theirs[1])
-    *first_left, left_mix = gate_left(row_left, live, first_chunks, left_ops)
+    *first_left, left_mix = gate_left(slots, row_left, live_states, first_chunks, left_ops)
     squares = (*first[:2], *second[:2])
     basis, image = krylov_part(
-        row, live, kept_here, weight, second_chunks, left_mix, first_left, start_here, squares
+        slots, row, live_states, kept, charges, second_chunks, left_mix, first_left, start, squares
     )
     basis = from_partner(basis, SEC, top_bit)
     right_part, total = truncated(
-        kept_here, weight, image, squares, (first[2], second[2]), lax.axis_size(SEC)
+        rows, row, kept, charges, image, squares, (first[2], second[2]), lax.axis_size(SEC)
     )
     totals = lax.all_to_all(total, SEC, split_axis=0, concat_axis=0, tiled=True)
     return tuple(finished(totals, right_part, basis))

time: 83.4 us -> 82.5 us (0.989)
  local copies, waits for them, and re-layouts: 5.08 us -> 2.9 us
  blocking collectives: 21.3 us -> 23.1 us
  starting transfers between devices: 19.4 us -> 21.1 us
  Pallas kernels: 34.3 us -> 32.9 us
    unnamed x16 -> x14, local copies, waits for them, and re-layouts: 3.77 us -> 1.92 us
    all_to_all x1, blocking collectives: 21.3 us -> 23.1 us  [on_device(): totals = lax.all_to_all(total, SEC, split_axis=0, concat_axis=0, tiled=True)]
    ppermute x3, starting transfers between devices: 12.1 us -> 13.8 us  [from_partner(): return lax.ppermute(value, axis, pairs)]
    pallas_call x1, Pallas kernels: 21.3 us -> 19.9 us  [krylov_part(): pl.pallas_call(krylov_kernel, in_specs=[smem()] * 4 + [vmem()] * (len(lef...]
  transfers between devices with their start and end apart: 9 -> 9, of which waited for: 2 -> 2; matrix products, arithmetic and copies ran while one was open for 0% -> 0% of each run, Pallas kernels for 14% -> 15%
where the time goes in v6:
time: 82.5 us; the launch traced here: 82.4 us
  Pallas kernels  32.9 us (40%)
  blocking collectives  23.1 us (28%)
  starting transfers between devices  21.1 us (26%)
  local copies, waits for them, and re-layouts  2.9 us (4%)
  waiting for transfers between devices  1.55 us (2%)
    all_to_all x1, blocking collectives, on_device(): totals = lax.all_to_all(total, SEC, split_axis=0, concat_axis=0, tiled=True)  23.1 us
    pallas_call x1, Pallas kernels, krylov_part(): pl.pallas_call(krylov_kernel, in_specs=[smem()] * 4 + [vmem()] * (len(lef...  19.9 us
    ppermute x3, starting transfers between devices, from_partner(): return lax.ppermute(value, axis, pairs)  13.8 us
    ppermute x6, starting transfers between devices, over_rows(): lax.ppermute(chunk, 'row', [(i, (i + d) % rows) for i in range(rows)])  7.39 us
    pallas_call x2, Pallas kernels, gate_right(): pl.pallas_call(functools.partial(right_kernel, slot, cols // local_cols),...  6.87 us
    pallas_call x1, Pallas kernels, gate_left(): pl.pallas_call(functools.partial(left_kernel, slots), in_specs=[smem()] *...  3.72 us
    unnamed x14, local copies, waits for them, and re-layouts  1.92 us
  transfers between devices with their start and end apart: 9, of which 2 were waited for; matrix products, arithmetic and copies ran while one was open for 0% of the time, Pallas kernels for 15%

profile of v6, /device:TPU:1, one launch (start us, length us, event | category | flops | bytes accessed | tf_op | source)
XLA Modules:
  0.0 82.4 jit_solution(4122283946011522084)
XLA Ops:
  0.6 1.0 %slice_bitcast_fusion = (bf16[512,128]{1,0:T(8,128)(2,1)S(1)}, bf16[512,128]{1,0:T(8,128)(2,1)S(1)}) fusion(bf16[2,512,128]{2,1,0:T(8,128)(2,1)} %param.8), kind=kLoop, calls=%fused_computation | loop fusion | bytes 524288 | tf_op jit(solution)/shard_map/squeeze | solution.py:440
  1.6 0.0 copy-start.2
  1.6 7.8 %collective-permute-start.1 = (bf16[512,128]{1,0:T(8,128)(2,1)S(1)}, bf16[512,128]{1,0:T(8,128)(2,1)S(1)}, u32[]{:S(2)}, u32[]{:S(2)}) collective-permute-start(bf16[512,128]{1,0:T(8,128)(2,1)S(1)} %get-tuple-element.42), channel_id=1, source_target_pairs={{0,128},{4,132},{8,136},{12,140},{16,144},{20,148},{24,152},{28,15... | collective-permute-start | bytes 393224 | tf_op jit(solution)/shard_map/ppermute | solution.py:24
  9.5 0.1 collective-permute-start
  9.6 0.0 copy-done.2
  9.6 0.0 copy-start
  9.6 1.2 %copy-done = bf16[2,128,2048]{2,1,0:T(8,128)(2,1)S(1)} copy-done((bf16[2,128,2048]{2,1,0:T(8,128)(2,1)S(1)}, bf16[2,128,2048]{2,1,0:T(8,128)(2,1)}, u32[]{:S(2)}) %copy-start) | copy-done | bytes 1048600
  10.8 3.4 %right_gate.2 = (bf16[512,512]{1,0:T(8,128)(2,1)S(1)}, bf16[512,512]{1,0:T(8,128)(2,1)S(1)}, bf16[512,512]{1,0:T(8,128)(2,1)S(1)}) custom-call(s32[1]{0:T(128)} %bitcast.place_ref, bf16[2,128,2048]{2,1,0:T(8,128)(2,1)S(1)} %copy-done, f32[64,16]{1,0:T(8,128)S(1)} %bitcast.12), custom_call_target="tpu_custom_call" | custom-call | flops 4000000000 | bytes 2097152 | tf_op jit(solution)/shard_map/right_gate/pallas_call | solution.py:335
  14.2 0.0 collective-permute-done.1.refs_0_
  14.2 0.0 copy-start.3
  14.3 2.9 %collective-permute-start.7 = (bf16[512,128]{1,0:T(8,128)(2,1)S(1)}, bf16[512,128]{1,0:T(8,128)(2,1)S(1)}, u32[]{:S(2)}, u32[]{:S(2)}) collective-permute-start(bf16[512,128]{1,0:T(8,128)(2,1)S(1)} %collective-permute-done.1.refs_0_), channel_id=1, source_target_pairs={{0,3},{1,0},{2,1},{3,2},{4,7},{5,4},{6,5},{7,6},{8,11},{9,8},{10,9... | collective-permute-start | bytes 393224 | tf_op jit(solution)/shard_map/ppermute | solution.py:435
  17.1 0.3 collective-permute-start.6
  17.4 0.7 collective-permute-start.5
  18.1 3.4 %right_gate.3 = (bf16[512,512]{1,0:T(8,128)(2,1)S(1)}, bf16[512,512]{1,0:T(8,128)(2,1)S(1)}, bf16[512,512]{1,0:T(8,128)(2,1)S(1)}) custom-call(s32[1]{0:T(128)} %bitcast.place_ref, bf16[2,128,2048]{2,1,0:T(8,128)(2,1)S(1)} %copy-done, f32[64,16]{1,0:T(8,128)S(1)} %bitcast.13), custom_call_target="tpu_custom_call" | custom-call | flops 4000000000 | bytes 2097152 | tf_op jit(solution)/shard_map/right_gate/pallas_call | solution.py:335
  21.6 0.0 copy-start.4
  21.6 0.0 collective-permute-done.refs_0_
  21.6 0.0 copy-start.1
  21.6 2.1 %collective-permute-start.4 = (bf16[512,128]{1,0:T(8,128)(2,1)S(1)}, bf16[512,128]{1,0:T(8,128)(2,1)S(1)}, u32[]{:S(2)}, u32[]{:S(2)}) collective-permute-start(bf16[512,128]{1,0:T(8,128)(2,1)S(1)} %collective-permute-done.refs_0_), channel_id=1, source_target_pairs={{0,3},{1,0},{2,1},{3,2},{4,7},{5,4},{6,5},{7,6},{8,11},{9,8},{10,9... | collective-permute-start | bytes 393224 | tf_op jit(solution)/shard_map/ppermute | solution.py:435
  23.7 1.4 %collective-permute-start.3 = (bf16[512,128]{1,0:T(8,128)(2,1)S(1)}, bf16[512,128]{1,0:T(8,128)(2,1)S(1)}, u32[]{:S(2)}, u32[]{:S(2)}) collective-permute-start(bf16[512,128]{1,0:T(8,128)(2,1)S(1)} %collective-permute-done.refs_0_), channel_id=1, source_target_pairs={{0,2},{1,3},{2,0},{3,1},{4,6},{5,7},{6,4},{7,5},{8,10},{9,11},{10,... | collective-permute-start | bytes 393224 | tf_op jit(solution)/shard_map/ppermute | solution.py:435
  25.1 0.0 collective-permute-done.7.refs_3_
  25.1 0.0 collective-permute-start.2
  25.1 0.0 collective-permute-done.6.refs_2_
  25.1 0.0 collective-permute-done.5.refs_1_
  25.1 0.0 copy-done.3
  25.2 0.0 copy-done.4
  25.2 3.7 %left_gate.1 = (bf16[512,512]{1,0:T(8,128)(2,1)S(1)}, bf16[512,512]{1,0:T(8,128)(2,1)S(1)}, bf16[512,512]{1,0:T(8,128)(2,1)S(1)}, bf16[4,512,256]{2,1,0:T(8,128)(2,1)S(1)}) custom-call(s32[1]{0:T(128)} %bitcast.place_ref, s32[128]{0:T(128)S(1)} %copy-done.4, f32[4,16,16]{2,1,0:T(8,128)S(1)} %copy-done.3, ...), custom_call_target="tpu_custom_call" | custom-call | flops 4000000000 | bytes 2097152 | tf_op jit(solution)/shard_map/left_gate/pallas_call | solution.py:359
  28.9 0.0 collective-permute-done.4.refs_3_
  28.9 0.2 collective-permute-done.3.refs_2_
  29.1 1.4 %collective-permute-done.2.refs_1_ = bf16[512,128]{1,0:T(8,128)(2,1)S(1)} collective-permute-done((bf16[512,128]{1,0:T(8,128)(2,1)S(1)}, bf16[512,128]{1,0:T(8,128)(2,1)S(1)}, u32[]{:S(2)}, u32[]{:S(2)}) %collective-permute-start.2) | collective-permute-done | bytes 131104 | tf_op jit(solution)/shard_map/ppermute | solution.py:435
  30.4 0.0 copy-start.5
  30.4 0.0 copy-start.6
  30.4 0.0 copy-done.1
  30.4 0.6 copy-done.5
  31.1 0.0 copy-done.6
  31.1 19.9 %krylov.1 = (bf16[2,512,128]{2,1,0:T(8,128)(2,1)S(1)}, f32[2,128,512]{2,1,0:T(8,128)S(1)}) custom-call(s32[1]{0:T(128)} %bitcast.place_ref, s32[128]{0:T(128)S(1)} %copy-done.4, s32[128]{0:T(128)S(1)} %copy-done.5, s32[128]{0:T(128)S(1)} %copy-done.6, bf16[512,128]{1,0:T(8,128)(2,1)S(1)} %collective-permute-done.refs_0_, ...), custom_call_target="tpu_custom_call" | custom-call | flops 20000000000 | bytes 2097152 | tf_op jit(solution)/shard_map/krylov/pallas_call | solution.py:379
  51.0 5.8 %collective-permute-start.8 = (bf16[2,512,128]{2,1,0:T(8,128)(2,1)S(1)}, bf16[2,512,128]{2,1,0:T(8,128)(2,1)S(1)}, u32[]{:S(2)}, u32[]{:S(2)}) collective-permute-start(bf16[2,512,128]{2,1,0:T(8,128)(2,1)S(1)} %get-tuple-element.41), channel_id=1, source_target_pairs={{0,128},{4,132},{8,136},{12,140},{16,144},{20,148},{24,152},{28,15... | collective-permute-start | bytes 786440 | tf_op jit(solution)/shard_map/ppermute | solution.py:24
  56.8 1.4 %truncate.1 = (f32[2,128,512]{2,1,0:T(8,128)S(1)}, f32[64,128]{1,0:T(8,128)S(1)}) custom-call(s32[1]{0:T(128)} %bitcast.place_ref, s32[128]{0:T(128)S(1)} %copy-done.5, s32[128]{0:T(128)S(1)} %copy-done.6, f32[2,128,512]{2,1,0:T(8,128)S(1)} %get-tuple-element.36.image_ref, bf16[512,512]{1,0:T(8,128)(2,1)S(1)} %get-tuple-element.32.refs_9_.refs_0_, ...), custom_call_target="tpu_custom_call" | custom-call | flops 2000000000 | bytes 2097152 | tf_op jit(solution)/shard_map/truncate/pallas_call | solution.py:402
  58.2 23.1 %all_to_all.11 = f32[64,1,128]{2,1,0:T(1,128)S(1)} all-to-all(f32[64,1,128]{2,1,0:T(1,128)S(1)} %bitcast.11), channel_id=1, replica_groups=mesh['sec_0'=8,'sec_1'=4,'sec_2'=2,'row'=4] {'sec_0','sec_1','sec_2'}, dimensions={0} | all-to-all | bytes 65536 | tf_op jit(solution)/shard_map/all_to_all | solution.py:456
  81.4 0.0 collective-permute-done.8.sent_ref
  81.4 1.0 %finish.1 = (f32[2,512,128]{2,1,0:T(8,128)}, f32[2,128,512]{2,1,0:T(8,128)}) custom-call(f32[64,128]{1,0:T(8,128)S(1)} %bitcast.10, f32[2,128,512]{2,1,0:T(8,128)S(1)} %get-tuple-element.40.part_ref, bf16[2,512,128]{2,1,0:T(8,128)(2,1)S(1)} %collective-permute-done.8.sent_ref), custom_call_target="tpu_custom_call" | custom-call | flops 1000000 | bytes 2097152 | tf_op jit(solution)/shard_map/finish/pallas_call | solution.py:416
Async XLA Ops:
  1.6 7.9 %copy-start.2 = (f32[4,16,16]{2,1,0:T(8,128)S(1)}, f32[4,16,16]{2,1,0:T(8,128)}, u32[]{:S(2)}) copy-start(f32[4,16,16]{2,1,0:T(8,128)} %param.11) | copy-start | bytes 12292
  1.6 12.6 %collective-permute-start.1 = (bf16[512,128]{1,0:T(8,128)(2,1)S(1)}, bf16[512,128]{1,0:T(8,128)(2,1)S(1)}, u32[]{:S(2)}, u32[]{:S(2)}) collective-permute-start(bf16[512,128]{1,0:T(8,128)(2,1)S(1)} %get-tuple-element.42), channel_id=1, source_target_pairs={{0,128},{4,132},{8,136},{12,140},{16,144},{20,148},{24,152},{28,15... | collective-permute-start | bytes 393224 | tf_op jit(solution)/shard_map/ppermute | solution.py:24
  9.5 12.1 %collective-permute-start = (bf16[512,128]{1,0:T(8,128)(2,1)S(1)}, bf16[512,128]{1,0:T(8,128)(2,1)S(1)}, u32[]{:S(2)}, u32[]{:S(2)}) collective-permute-start(bf16[512,128]{1,0:T(8,128)(2,1)S(1)} %get-tuple-element.43), channel_id=1, source_target_pairs={{0,128},{4,132},{8,136},{12,140},{16,144},{20,148},{24,152},{28,15... | collective-permute-start | bytes 393224 | tf_op jit(solution)/shard_map/ppermute | solution.py:24
  9.6 1.2 %copy-start = (bf16[2,128,2048]{2,1,0:T(8,128)(2,1)S(1)}, bf16[2,128,2048]{2,1,0:T(8,128)(2,1)}, u32[]{:S(2)}) copy-start(bf16[2,128,2048]{2,1,0:T(8,128)(2,1)} %right_ref.3) | copy-start | bytes 3145732
  14.2 10.9 %copy-start.3 = (f32[4,16,16]{2,1,0:T(8,128)S(1)}, f32[4,16,16]{2,1,0:T(8,128)}, u32[]{:S(2)}) copy-start(f32[4,16,16]{2,1,0:T(8,128)} %left_ops_ref.1) | copy-start | bytes 12292
  14.3 10.9 %collective-permute-start.7 = (bf16[512,128]{1,0:T(8,128)(2,1)S(1)}, bf16[512,128]{1,0:T(8,128)(2,1)S(1)}, u32[]{:S(2)}, u32[]{:S(2)}) collective-permute-start(bf16[512,128]{1,0:T(8,128)(2,1)S(1)} %collective-permute-done.1.refs_0_), channel_id=1, source_target_pairs={{0,3},{1,0},{2,1},{3,2},{4,7},{5,4},{6,5},{7,6},{8,11},{9,8},{10,9... | collective-permute-start | bytes 393224 | tf_op jit(solution)/shard_map/ppermute | solution.py:435
  17.1 8.0 %collective-permute-start.6 = (bf16[512,128]{1,0:T(8,128)(2,1)S(1)}, bf16[512,128]{1,0:T(8,128)(2,1)S(1)}, u32[]{:S(2)}, u32[]{:S(2)}) collective-permute-start(bf16[512,128]{1,0:T(8,128)(2,1)S(1)} %collective-permute-done.1.refs_0_), channel_id=1, source_target_pairs={{0,2},{1,3},{2,0},{3,1},{4,6},{5,7},{6,4},{7,5},{8,10},{9,11},{10,... | collective-permute-start | bytes 393224 | tf_op jit(solution)/shard_map/ppermute | solution.py:435
  17.4 7.7 %collective-permute-start.5 = (bf16[512,128]{1,0:T(8,128)(2,1)S(1)}, bf16[512,128]{1,0:T(8,128)(2,1)S(1)}, u32[]{:S(2)}, u32[]{:S(2)}) collective-permute-start(bf16[512,128]{1,0:T(8,128)(2,1)S(1)} %collective-permute-done.1.refs_0_), channel_id=1, source_target_pairs={{0,1},{1,2},{2,3},{3,0},{4,5},{5,6},{6,7},{7,4},{8,9},{9,10},{10,1... | collective-permute-start | bytes 393224 | tf_op jit(solution)/shard_map/ppermute | solution.py:435
  21.6 3.6 %copy-start.4 = (s32[128]{0:T(128)S(1)}, s32[128]{0:T(128)}, u32[]{:S(2)}) copy-start(s32[128]{0:T(128)} %live_ref.3) | copy-start | bytes 1540
  21.6 8.9 %copy-start.1 = (s32[128,128]{1,0:T(8,128)S(1)}, s32[128,128]{1,0:T(8,128)}, u32[]{:S(2)}) copy-start(s32[128,128]{1,0:T(8,128)} %refs_8_.1) | copy-start | bytes 196612
  21.6 7.3 %collective-permute-start.4 = (bf16[512,128]{1,0:T(8,128)(2,1)S(1)}, bf16[512,128]{1,0:T(8,128)(2,1)S(1)}, u32[]{:S(2)}, u32[]{:S(2)}) collective-permute-start(bf16[512,128]{1,0:T(8,128)(2,1)S(1)} %collective-permute-done.refs_0_), channel_id=1, source_target_pairs={{0,3},{1,0},{2,1},{3,2},{4,7},{5,4},{6,5},{7,6},{8,11},{9,8},{10,9... | collective-permute-start | bytes 393224 | tf_op jit(solution)/shard_map/ppermute | solution.py:435
  23.7 5.3 %collective-permute-start.3 = (bf16[512,128]{1,0:T(8,128)(2,1)S(1)}, bf16[512,128]{1,0:T(8,128)(2,1)S(1)}, u32[]{:S(2)}, u32[]{:S(2)}) collective-permute-start(bf16[512,128]{1,0:T(8,128)(2,1)S(1)} %collective-permute-done.refs_0_), channel_id=1, source_target_pairs={{0,2},{1,3},{2,0},{3,1},{4,6},{5,7},{6,4},{7,5},{8,10},{9,11},{10,... | collective-permute-start | bytes 393224 | tf_op jit(solution)/shard_map/ppermute | solution.py:435
  25.1 5.3 %collective-permute-start.2 = (bf16[512,128]{1,0:T(8,128)(2,1)S(1)}, bf16[512,128]{1,0:T(8,128)(2,1)S(1)}, u32[]{:S(2)}, u32[]{:S(2)}) collective-permute-start(bf16[512,128]{1,0:T(8,128)(2,1)S(1)} %collective-permute-done.refs_0_), channel_id=1, source_target_pairs={{0,1},{1,2},{2,3},{3,0},{4,5},{5,6},{6,7},{7,4},{8,9},{9,10},{10,1... | collective-permute-start | bytes 393224 | tf_op jit(solution)/shard_map/ppermute | solution.py:435
  30.4 0.7 copy-start.5
  30.4 0.7 copy-start.6
  51.0 30.4 %collective-permute-start.8 = (bf16[2,512,128]{2,1,0:T(8,128)(2,1)S(1)}, bf16[2,512,128]{2,1,0:T(8,128)(2,1)S(1)}, u32[]{:S(2)}, u32[]{:S(2)}) collective-permute-start(bf16[2,512,128]{2,1,0:T(8,128)(2,1)S(1)} %get-tuple-element.41), channel_id=1, source_target_pairs={{0,128},{4,132},{8,136},{12,140},{16,144},{20,148},{24,152},{28,15... | collective-permute-start | bytes 786440 | tf_op jit(solution)/shard_map/ppermute | solution.py:24

commit v7 on v6

--- a/solution.py
+++ b/solution.py
@@ -113,16 +113,16 @@
     )
 
 
-def right_kernel(
-    slot, rows, place_ref, right_ref, right_ops_ref, high_ref, low_ref, local_ref,
-    right_mix, gated, right, sem,
-):
-    states = right.shape[0]
+def right_kernel(rows, place_ref, right_ref, right_ops_ref, *refs):
+    *out_refs, right_mix, gated, right, sems = refs
+    slots, states = right.shape[:2]
     terms = gated.shape[0] // states
     wide = SITE * SITE
-    local_cols = local_ref.shape[1]
-    fetch = pltpu.make_async_copy(right_ref.at[slot], right, sem)
-    fetch.start()
+    fetches = [
+        pltpu.make_async_copy(right_ref.at[s], right.at[s], sems.at[s]) for s in range(slots)
+    ]
+    for fetch in fetches:
+        fetch.start()
     spread = as_weights(one_hot((terms * wide, terms * SITE), lambda r: r // SITE, lambda c: c))
     widen = as_weights(one_hot((SITE, wide), lambda r: r, lambda c: c // SITE))
     same = one_hot((terms * wide, wide), lambda r: r % SITE, lambda c: c % SITE)
@@ -132,33 +132,40 @@
         right_mix[:, part * wide : (part + 1) * wide] = jnp.where(same, full, 0.0).astype(
             jnp.bfloat16
         )
-    fetch.wait()
-    for pair in range(states // (2 * SITE)):
-        base = pair * 2 * SITE
-        halves = [
-            jnp.concatenate(
-                [
-                    right[base + h * SITE : base + (h + 1) * SITE, j * states : (j + 1) * states]
-                    for j in range(SITE)
-                ],
-                axis=0,
-            )
-            for h in range(2)
-        ]
-        block = jnp.concatenate(halves, axis=1)
-        block = jnp.concatenate([block, block], axis=0)
-        for t in range(terms):
-            mixed = dot_over(right_mix[t * wide : (t + 1) * wide, :], block, 1, 0)
-            mixed = mixed.astype(jnp.bfloat16)
-            for h in range(2):
-                for i in range(SITE):
-                    gated[
-                        t * states + base + h * SITE : t * states + base + (h + 1) * SITE,
-                        i * states : (i + 1) * states,
-                    ] = mixed[i * SITE : (i + 1) * SITE, h * states : (h + 1) * states]
-    high_ref[...], low_ref[...] = two_parts(dot_over(gated[...], gated[...], 1, 1))
-    offset = pl.multiple_of(lax.rem(place_ref[0], rows) * local_cols, local_cols)
-    local_ref[...] = gated[:, pl.ds(offset, local_cols)]
+    for s in range(slots):
+        high_ref, low_ref, local_ref = out_refs[3 * s : 3 * s + 3]
+        local_cols = local_ref.shape[1]
+        fetches[s].wait()
+        for pair in range(states // (2 * SITE)):
+            base = pair * 2 * SITE
+            halves = [
+                jnp.concatenate(
+                    [
+                        right[
+                            s,
+                            base + h * SITE : base + (h + 1) * SITE,
+                            j * states : (j + 1) * states,
+                        ]
+                        for j in range(SITE)
+                    ],
+                    axis=0,
+                )
+                for h in range(2)
+            ]
+            block = jnp.concatenate(halves, axis=1)
+            block = jnp.concatenate([block, block], axis=0)
+            for t in range(terms):
+                mixed = dot_over(right_mix[t * wide : (t + 1) * wide, :], block, 1, 0)
+                mixed = mixed.astype(jnp.bfloat16)
+                for h in range(2):
+                    for i in range(SITE):
+                        gated[
+                            t * states + base + h * SITE : t * states + base + (h + 1) * SITE,
+                            i * states : (i + 1) * states,
+                        ] = mixed[i * SITE : (i + 1) * SITE, h * states : (h + 1) * states]
+        high_ref[...], low_ref[...] = two_parts(dot_over(gated[...], gated[...], 1, 1))
+        offset = pl.multiple_of(lax.rem(place_ref[0], rows) * local_cols, local_cols)
+        local_ref[...] = gated[:, pl.ds(offset, local_cols)]
 
 
 def build_left_mix(left_ops_ref, left_mix):
@@ -328,27 +335,28 @@
     )
 
 
-def gate_right(slot, row, right_block, right_ops, local_cols):
-    _, states, cols = right_block.shape
+def gate_right(row, right_block, right_ops, local_cols):
+    slots, states, cols = right_block.shape
     terms = right_ops.shape[0]
     bond, wide = terms * states, SITE * SITE
     return pl.pallas_call(
-        functools.partial(right_kernel, slot, cols // local_cols),
+        functools.partial(right_kernel, cols // local_cols),
         in_specs=[smem(), pl.BlockSpec(memory_space=pltpu.HBM), vmem()],
-        out_specs=[vmem()] * 3,
+        out_specs=[vmem()] * (3 * slots),
         out_shape=[
             shape_of((bond, bond), jnp.bfloat16),
             shape_of((bond, bond), jnp.bfloat16),
             shape_of((bond, local_cols), jnp.bfloat16),
-        ],
+        ]
+        * slots,
         scratch_shapes=[
             pltpu.VMEM((terms * wide, 2 * wide), jnp.bfloat16),
             pltpu.VMEM((bond, cols), jnp.bfloat16),
-            pltpu.VMEM((states, cols), jnp.bfloat16),
-            pltpu.SemaphoreType.DMA,
+            pltpu.VMEM((slots, states, cols), jnp.bfloat16),
+            pltpu.SemaphoreType.DMA((slots,)),
         ],
         name="right_gate",
-        **kernel_options(12, 4e9),
+        **kernel_options(12, 8e9),
     )(row, right_block, right_ops.reshape(terms * SITE, SITE))
 
 
@@ -438,13 +446,11 @@
         return [chunk, *sent]
 
     theirs = [from_partner(left_block[s], SEC, top_bit) for s in range(slots)]
-    first = list(gate_right(0, row, right_block, right_ops, local_cols))
-    theirs[0], first[0], row_second = lax.optimization_barrier((theirs[0], first[0], row))
-    first_chunks = over_rows(theirs[0])
-    second = list(gate_right(1, row_second, right_block, right_ops, local_cols))
-    theirs[1], second[0], row_left = lax.optimization_barrier((theirs[1], second[0], row))
-    second_chunks = over_rows(theirs[1])
-    *first_left, left_mix = gate_left(slots, row_left, live_states, first_chunks, left_ops)
+    right_sides = gate_right(row, right_block, right_ops, local_cols)
+    theirs, right_sides = lax.optimization_barrier((theirs, right_sides))
+    first, second = right_sides[:3], right_sides[3:]
+    first_chunks, second_chunks = over_rows(theirs[0]), over_rows(theirs[1])
+    *first_left, left_mix = gate_left(slots, row, live_states, first_chunks, left_ops)
     squares = (*first[:2], *second[:2])
     basis, image = krylov_part(
         slots, row, live_states, kept, charges, second_chunks, left_mix, first_left, start, squares

time: 82.5 us -> 83.9 us (1.017)
  waiting for transfers between devices: 1.55 us -> 4.09 us
  Pallas kernels: 32.9 us -> 32 us
    ppermute x6, waiting for transfers between devices: 1.54 us -> 3.55 us  [over_rows(): lax.ppermute(chunk, 'row', [(i, (i + d) % rows) for i in range(rows)])]
    pallas_call x2 -> x1, Pallas kernels: 6.87 us -> 5.99 us  [gate_right(): pl.pallas_call(functools.partial(right_kernel, cols // local_cols), in_sp...]
  transfers between devices with their start and end apart: 9 -> 9, of which waited for: 2 -> 4; matrix products, arithmetic and copies ran while one was open for 0% -> 0% of each run, Pallas kernels for 15% -> 13%
where the time goes in v7:
time: 83.9 us; the launch traced here: 83.7 us
  Pallas kernels  32 us (38%)
  blocking collectives  22.4 us (27%)
  starting transfers between devices  21.6 us (26%)
  waiting for transfers between devices  4.09 us (5%)
  local copies, waits for them, and re-layouts  2.9 us (3%)
    all_to_all x1, blocking collectives, on_device(): totals = lax.all_to_all(total, SEC, split_axis=0, concat_axis=0, tiled=True)  22.4 us
    pallas_call x1, Pallas kernels, krylov_part(): pl.pallas_call(krylov_kernel, in_specs=[smem()] * 4 + [vmem()] * (len(lef...  19.9 us
    ppermute x3, starting transfers between devices, from_partner(): return lax.ppermute(value, axis, pairs)  14.5 us
    ppermute x6, starting transfers between devices, over_rows(): lax.ppermute(chunk, 'row', [(i, (i + d) % rows) for i in range(rows)])  7.17 us
    pallas_call x1, Pallas kernels, gate_right(): pl.pallas_call(functools.partial(right_kernel, cols // local_cols), in_sp...  5.99 us
    pallas_call x1, Pallas kernels, gate_left(): pl.pallas_call(functools.partial(left_kernel, slots), in_specs=[smem()] *...  3.72 us
    ppermute x6, waiting for transfers between devices, over_rows(): lax.ppermute(chunk, 'row', [(i, (i + d) % rows) for i in range(rows)])  3.55 us
    unnamed x14, local copies, waits for them, and re-layouts  1.91 us
  transfers between devices with their start and end apart: 9, of which 4 were waited for; matrix products, arithmetic and copies ran while one was open for 0% of the time, Pallas kernels for 13%

profile of v7, /device:TPU:1, one launch (start us, length us, event | category | flops | bytes accessed | tf_op | source)
XLA Modules:
  0.0 83.7 jit_solution(15627562464838294839)
XLA Ops:
  0.6 1.0 %slice_bitcast_fusion = (bf16[512,128]{1,0:T(8,128)(2,1)S(1)}, bf16[512,128]{1,0:T(8,128)(2,1)S(1)}) fusion(bf16[2,512,128]{2,1,0:T(8,128)(2,1)} %param.8), kind=kLoop, calls=%fused_computation | loop fusion | bytes 524288 | tf_op jit(solution)/shard_map/squeeze | solution.py:448
  1.6 0.0 copy-start.2
  1.6 7.8 %collective-permute-start.1 = (bf16[512,128]{1,0:T(8,128)(2,1)S(1)}, bf16[512,128]{1,0:T(8,128)(2,1)S(1)}, u32[]{:S(2)}, u32[]{:S(2)}) collective-permute-start(bf16[512,128]{1,0:T(8,128)(2,1)S(1)} %get-tuple-element.46), channel_id=1, source_target_pairs={{0,128},{4,132},{8,136},{12,140},{16,144},{20,148},{24,152},{28,15... | collective-permute-start | bytes 393224 | tf_op jit(solution)/shard_map/ppermute | solution.py:24
  9.5 0.1 collective-permute-start
  9.6 0.0 copy-done.2
  9.6 0.0 copy-start
  9.6 1.2 %copy-done = bf16[2,128,2048]{2,1,0:T(8,128)(2,1)S(1)} copy-done((bf16[2,128,2048]{2,1,0:T(8,128)(2,1)S(1)}, bf16[2,128,2048]{2,1,0:T(8,128)(2,1)}, u32[]{:S(2)}) %copy-start) | copy-done | bytes 1048600
  10.8 0.0 copy-start.3
  10.8 6.0 %right_gate.1 = (bf16[512,512]{1,0:T(8,128)(2,1)S(1)}, bf16[512,512]{1,0:T(8,128)(2,1)S(1)}, bf16[512,512]{1,0:T(8,128)(2,1)S(1)}, bf16[512,512]{1,0:T(8,128)(2,...) custom-call(s32[1]{0:T(128)} %bitcast.place_ref, bf16[2,128,2048]{2,1,0:T(8,128)(2,1)S(1)} %copy-done, ...), custom_call_target="tpu_custom_call" | custom-call | flops 8000000000 | bytes 2097152 | tf_op jit(solution)/shard_map/right_gate/pallas_call | solution.py:342
  16.8 0.0 collective-permute-done.1.refs_0_
  16.8 0.5 collective-permute-done.refs_0_
  17.3 0.0 copy-start.4
  17.3 0.0 copy-start.1
  17.3 2.7 %collective-permute-start.7 = (bf16[512,128]{1,0:T(8,128)(2,1)S(1)}, bf16[512,128]{1,0:T(8,128)(2,1)S(1)}, u32[]{:S(2)}, u32[]{:S(2)}) collective-permute-start(bf16[512,128]{1,0:T(8,128)(2,1)S(1)} %collective-permute-done.refs_0_), channel_id=1, source_target_pairs={{0,3},{1,0},{2,1},{3,2},{4,7},{5,4},{6,5},{7,6},{8,11},{9,8},{10,9... | collective-permute-start | bytes 393224 | tf_op jit(solution)/shard_map/ppermute | solution.py:443
  20.1 0.3 collective-permute-start.6
  20.4 0.7 collective-permute-start.5
  21.1 2.0 %collective-permute-start.4 = (bf16[512,128]{1,0:T(8,128)(2,1)S(1)}, bf16[512,128]{1,0:T(8,128)(2,1)S(1)}, u32[]{:S(2)}, u32[]{:S(2)}) collective-permute-start(bf16[512,128]{1,0:T(8,128)(2,1)S(1)} %collective-permute-done.1.refs_0_), channel_id=1, source_target_pairs={{0,3},{1,0},{2,1},{3,2},{4,7},{5,4},{6,5},{7,6},{8,11},{9,8},{10,9... | collective-permute-start | bytes 393224 | tf_op jit(solution)/shard_map/ppermute | solution.py:443
  23.1 1.4 %collective-permute-start.3 = (bf16[512,128]{1,0:T(8,128)(2,1)S(1)}, bf16[512,128]{1,0:T(8,128)(2,1)S(1)}, u32[]{:S(2)}, u32[]{:S(2)}) collective-permute-start(bf16[512,128]{1,0:T(8,128)(2,1)S(1)} %collective-permute-done.1.refs_0_), channel_id=1, source_target_pairs={{0,2},{1,3},{2,0},{3,1},{4,6},{5,7},{6,4},{7,5},{8,10},{9,11},{10,... | collective-permute-start | bytes 393224 | tf_op jit(solution)/shard_map/ppermute | solution.py:443
  24.5 0.0 collective-permute-done.7.refs_3_
  24.5 0.0 collective-permute-start.2
  24.5 1.0 %collective-permute-done.6.refs_2_ = bf16[512,128]{1,0:T(8,128)(2,1)S(1)} collective-permute-done((bf16[512,128]{1,0:T(8,128)(2,1)S(1)}, bf16[512,128]{1,0:T(8,128)(2,1)S(1)}, u32[]{:S(2)}, u32[]{:S(2)}) %collective-permute-start.6) | collective-permute-done | bytes 131104 | tf_op jit(solution)/shard_map/ppermute | solution.py:443
  25.5 1.3 %collective-permute-done.5.refs_1_ = bf16[512,128]{1,0:T(8,128)(2,1)S(1)} collective-permute-done((bf16[512,128]{1,0:T(8,128)(2,1)S(1)}, bf16[512,128]{1,0:T(8,128)(2,1)S(1)}, u32[]{:S(2)}, u32[]{:S(2)}) %collective-permute-start.5) | collective-permute-done | bytes 131104 | tf_op jit(solution)/shard_map/ppermute | solution.py:443
  26.8 0.0 copy-done.3
  26.8 0.0 copy-done.4
  26.8 3.7 %left_gate.1 = (bf16[512,512]{1,0:T(8,128)(2,1)S(1)}, bf16[512,512]{1,0:T(8,128)(2,1)S(1)}, bf16[512,512]{1,0:T(8,128)(2,1)S(1)}, bf16[4,512,256]{2,1,0:T(8,128)(2,1)S(1)}) custom-call(s32[1]{0:T(128)} %bitcast.place_ref, s32[128]{0:T(128)S(1)} %copy-done.4, f32[4,16,16]{2,1,0:T(8,128)S(1)} %copy-done.3, bf16[512,128]{1,0:T(8,128)(2,1)S(1)} %collective-permute-done.refs_0_, ...), custom_call_target="tpu_custom_call" | custom-call | flops 4000000000 | bytes 2097152 | tf_op jit(solution)/shard_map/left_gate/pallas_call | solution.py:367
  30.5 0.0 collective-permute-done.4.refs_3_
  30.5 0.0 collective-permute-done.3.refs_2_
  30.5 1.3 %collective-permute-done.2.refs_1_ = bf16[512,128]{1,0:T(8,128)(2,1)S(1)} collective-permute-done((bf16[512,128]{1,0:T(8,128)(2,1)S(1)}, bf16[512,128]{1,0:T(8,128)(2,1)S(1)}, u32[]{:S(2)}, u32[]{:S(2)}) %collective-permute-start.2) | collective-permute-done | bytes 131104 | tf_op jit(solution)/shard_map/ppermute | solution.py:443
  31.8 0.0 copy-start.5
  31.8 0.0 copy-start.6
  31.8 0.0 copy-done.1
  31.8 0.6 copy-done.5
  32.5 0.0 copy-done.6
  32.5 19.9 %krylov.1 = (bf16[2,512,128]{2,1,0:T(8,128)(2,1)S(1)}, f32[2,128,512]{2,1,0:T(8,128)S(1)}) custom-call(s32[1]{0:T(128)} %bitcast.place_ref, s32[128]{0:T(128)S(1)} %copy-done.4, s32[128]{0:T(128)S(1)} %copy-done.5, s32[128]{0:T(128)S(1)} %copy-done.6, bf16[512,128]{1,0:T(8,128)(2,1)S(1)} %collective-permute-done.1.refs_0_, ...), custom_call_target="tpu_custom_call" | custom-call | flops 20000000000 | bytes 2097152 | tf_op jit(solution)/shard_map/krylov/pallas_call | solution.py:387
  52.4 6.5 %collective-permute-start.8 = (bf16[2,512,128]{2,1,0:T(8,128)(2,1)S(1)}, bf16[2,512,128]{2,1,0:T(8,128)(2,1)S(1)}, u32[]{:S(2)}, u32[]{:S(2)}) collective-permute-start(bf16[2,512,128]{2,1,0:T(8,128)(2,1)S(1)} %get-tuple-element.45), channel_id=1, source_target_pairs={{0,128},{4,132},{8,136},{12,140},{16,144},{20,148},{24,152},{28,15... | collective-permute-start | bytes 786440 | tf_op jit(solution)/shard_map/ppermute | solution.py:24
  58.9 1.4 %truncate.1 = (f32[2,128,512]{2,1,0:T(8,128)S(1)}, f32[64,128]{1,0:T(8,128)S(1)}) custom-call(s32[1]{0:T(128)} %bitcast.place_ref, s32[128]{0:T(128)S(1)} %copy-done.5, s32[128]{0:T(128)S(1)} %copy-done.6, f32[2,128,512]{2,1,0:T(8,128)S(1)} %get-tuple-element.40.image_ref, bf16[512,512]{1,0:T(8,128)(2,1)S(1)} %get-tuple-element.36.refs_9_.refs_0_, ...), custom_call_target="tpu_custom_call" | custom-call | flops 2000000000 | bytes 2097152 | tf_op jit(solution)/shard_map/truncate/pallas_call | solution.py:410
  60.3 22.4 %all_to_all.11 = f32[64,1,128]{2,1,0:T(1,128)S(1)} all-to-all(f32[64,1,128]{2,1,0:T(1,128)S(1)} %bitcast.11), channel_id=1, replica_groups=mesh['sec_0'=8,'sec_1'=4,'sec_2'=2,'row'=4] {'sec_0','sec_1','sec_2'}, dimensions={0} | all-to-all | bytes 65536 | tf_op jit(solution)/shard_map/all_to_all | solution.py:462
  82.7 0.0 collective-permute-done.8.sent_ref
  82.7 1.0 %finish.1 = (f32[2,512,128]{2,1,0:T(8,128)}, f32[2,128,512]{2,1,0:T(8,128)}) custom-call(f32[64,128]{1,0:T(8,128)S(1)} %bitcast.10, f32[2,128,512]{2,1,0:T(8,128)S(1)} %get-tuple-element.44.part_ref, bf16[2,512,128]{2,1,0:T(8,128)(2,1)S(1)} %collective-permute-done.8.sent_ref), custom_call_target="tpu_custom_call" | custom-call | flops 1000000 | bytes 2097152 | tf_op jit(solution)/shard_map/finish/pallas_call | solution.py:424
Async XLA Ops:
  1.6 7.9 %copy-start.2 = (f32[4,16,16]{2,1,0:T(8,128)S(1)}, f32[4,16,16]{2,1,0:T(8,128)}, u32[]{:S(2)}) copy-start(f32[4,16,16]{2,1,0:T(8,128)} %param.11) | copy-start | bytes 12292
  1.6 15.2 %collective-permute-start.1 = (bf16[512,128]{1,0:T(8,128)(2,1)S(1)}, bf16[512,128]{1,0:T(8,128)(2,1)S(1)}, u32[]{:S(2)}, u32[]{:S(2)}) collective-permute-start(bf16[512,128]{1,0:T(8,128)(2,1)S(1)} %get-tuple-element.46), channel_id=1, source_target_pairs={{0,128},{4,132},{8,136},{12,140},{16,144},{20,148},{24,152},{28,15... | collective-permute-start | bytes 393224 | tf_op jit(solution)/shard_map/ppermute | solution.py:24
  9.5 7.9 %collective-permute-start = (bf16[512,128]{1,0:T(8,128)(2,1)S(1)}, bf16[512,128]{1,0:T(8,128)(2,1)S(1)}, u32[]{:S(2)}, u32[]{:S(2)}) collective-permute-start(bf16[512,128]{1,0:T(8,128)(2,1)S(1)} %get-tuple-element.47), channel_id=1, source_target_pairs={{0,128},{4,132},{8,136},{12,140},{16,144},{20,148},{24,152},{28,15... | collective-permute-start | bytes 393224 | tf_op jit(solution)/shard_map/ppermute | solution.py:24
  9.6 1.2 %copy-start = (bf16[2,128,2048]{2,1,0:T(8,128)(2,1)S(1)}, bf16[2,128,2048]{2,1,0:T(8,128)(2,1)}, u32[]{:S(2)}) copy-start(bf16[2,128,2048]{2,1,0:T(8,128)(2,1)} %right_ref.1) | copy-start | bytes 3145732
  10.8 16.0 %copy-start.3 = (f32[4,16,16]{2,1,0:T(8,128)S(1)}, f32[4,16,16]{2,1,0:T(8,128)}, u32[]{:S(2)}) copy-start(f32[4,16,16]{2,1,0:T(8,128)} %left_ops_ref.1) | copy-start | bytes 12292
  17.3 9.5 %copy-start.4 = (s32[128]{0:T(128)S(1)}, s32[128]{0:T(128)}, u32[]{:S(2)}) copy-start(s32[128]{0:T(128)} %live_ref.3) | copy-start | bytes 1540
  17.3 14.5 %copy-start.1 = (s32[128,128]{1,0:T(8,128)S(1)}, s32[128,128]{1,0:T(8,128)}, u32[]{:S(2)}) copy-start(s32[128,128]{1,0:T(8,128)} %refs_8_.1) | copy-start | bytes 196612
  17.3 7.2 %collective-permute-start.7 = (bf16[512,128]{1,0:T(8,128)(2,1)S(1)}, bf16[512,128]{1,0:T(8,128)(2,1)S(1)}, u32[]{:S(2)}, u32[]{:S(2)}) collective-permute-start(bf16[512,128]{1,0:T(8,128)(2,1)S(1)} %collective-permute-done.refs_0_), channel_id=1, source_target_pairs={{0,3},{1,0},{2,1},{3,2},{4,7},{5,4},{6,5},{7,6},{8,11},{9,8},{10,9... | collective-permute-start | bytes 393224 | tf_op jit(solution)/shard_map/ppermute | solution.py:443
  20.1 5.4 %collective-permute-start.6 = (bf16[512,128]{1,0:T(8,128)(2,1)S(1)}, bf16[512,128]{1,0:T(8,128)(2,1)S(1)}, u32[]{:S(2)}, u32[]{:S(2)}) collective-permute-start(bf16[512,128]{1,0:T(8,128)(2,1)S(1)} %collective-permute-done.refs_0_), channel_id=1, source_target_pairs={{0,2},{1,3},{2,0},{3,1},{4,6},{5,7},{6,4},{7,5},{8,10},{9,11},{10,... | collective-permute-start | bytes 393224 | tf_op jit(solution)/shard_map/ppermute | solution.py:443
  20.4 6.4 %collective-permute-start.5 = (bf16[512,128]{1,0:T(8,128)(2,1)S(1)}, bf16[512,128]{1,0:T(8,128)(2,1)S(1)}, u32[]{:S(2)}, u32[]{:S(2)}) collective-permute-start(bf16[512,128]{1,0:T(8,128)(2,1)S(1)} %collective-permute-done.refs_0_), channel_id=1, source_target_pairs={{0,1},{1,2},{2,3},{3,0},{4,5},{5,6},{6,7},{7,4},{8,9},{9,10},{10,1... | collective-permute-start | bytes 393224 | tf_op jit(solution)/shard_map/ppermute | solution.py:443
  21.1 9.4 %collective-permute-start.4 = (bf16[512,128]{1,0:T(8,128)(2,1)S(1)}, bf16[512,128]{1,0:T(8,128)(2,1)S(1)}, u32[]{:S(2)}, u32[]{:S(2)}) collective-permute-start(bf16[512,128]{1,0:T(8,128)(2,1)S(1)} %collective-permute-done.1.refs_0_), channel_id=1, source_target_pairs={{0,3},{1,0},{2,1},{3,2},{4,7},{5,4},{6,5},{7,6},{8,11},{9,8},{10,9... | collective-permute-start | bytes 393224 | tf_op jit(solution)/shard_map/ppermute | solution.py:443
  23.1 7.4 %collective-permute-start.3 = (bf16[512,128]{1,0:T(8,128)(2,1)S(1)}, bf16[512,128]{1,0:T(8,128)(2,1)S(1)}, u32[]{:S(2)}, u32[]{:S(2)}) collective-permute-start(bf16[512,128]{1,0:T(8,128)(2,1)S(1)} %collective-permute-done.1.refs_0_), channel_id=1, source_target_pairs={{0,2},{1,3},{2,0},{3,1},{4,6},{5,7},{6,4},{7,5},{8,10},{9,11},{10,... | collective-permute-start | bytes 393224 | tf_op jit(solution)/shard_map/ppermute | solution.py:443
  24.5 7.3 %collective-permute-start.2 = (bf16[512,128]{1,0:T(8,128)(2,1)S(1)}, bf16[512,128]{1,0:T(8,128)(2,1)S(1)}, u32[]{:S(2)}, u32[]{:S(2)}) collective-permute-start(bf16[512,128]{1,0:T(8,128)(2,1)S(1)} %collective-permute-done.1.refs_0_), channel_id=1, source_target_pairs={{0,1},{1,2},{2,3},{3,0},{4,5},{5,6},{6,7},{7,4},{8,9},{9,10},{10,1... | collective-permute-start | bytes 393224 | tf_op jit(solution)/shard_map/ppermute | solution.py:443
  31.8 0.7 copy-start.5
  31.8 0.7 copy-start.6
  52.4 30.4 %collective-permute-start.8 = (bf16[2,512,128]{2,1,0:T(8,128)(2,1)S(1)}, bf16[2,512,128]{2,1,0:T(8,128)(2,1)S(1)}, u32[]{:S(2)}, u32[]{:S(2)}) collective-permute-start(bf16[2,512,128]{2,1,0:T(8,128)(2,1)S(1)} %get-tuple-element.45), channel_id=1, source_target_pairs={{0,128},{4,132},{8,136},{12,140},{16,144},{20,148},{24,152},{28,15... | collective-permute-start | bytes 786440 | tf_op jit(solution)/shard_map/ppermute | solution.py:24

commit v8 on v6

--- a/solution.py
+++ b/solution.py
@@ -437,8 +437,10 @@
         ]
         return [chunk, *sent]
 
-    theirs = [from_partner(left_block[s], SEC, top_bit) for s in range(slots)]
+    theirs = [from_partner(left_block[0], SEC, top_bit)]
     first = list(gate_right(0, row, right_block, right_ops, local_cols))
+    second_block, first[0] = lax.optimization_barrier((left_block[1], first[0]))
+    theirs.append(from_partner(second_block, SEC, top_bit))
     theirs[0], first[0], row_second = lax.optimization_barrier((theirs[0], first[0], row))
     first_chunks = over_rows(theirs[0])
     second = list(gate_right(1, row_second, right_block, right_ops, local_cols))

time: 82.5 us -> 80.1 us (0.971)
  starting transfers between devices: 21.1 us -> 18.5 us
  waiting for transfers between devices: 1.55 us -> 3.82 us
  blocking collectives: 23.1 us -> 21.1 us
    ppermute x3, starting transfers between devices: 13.8 us -> 10.9 us  [from_partner(): return lax.ppermute(value, axis, pairs)]
    all_to_all x1, blocking collectives: 23.1 us -> 21.1 us  [on_device(): totals = lax.all_to_all(total, SEC, split_axis=0, concat_axis=0, tiled=True)]
    ppermute x6, waiting for transfers between devices: 1.54 us -> 3.01 us  [over_rows(): lax.ppermute(chunk, 'row', [(i, (i + d) % rows) for i in range(rows)])]
  transfers between devices with their start and end apart: 9 -> 9, of which waited for: 2 -> 4; matrix products, arithmetic and copies ran while one was open for 0% -> 0% of each run, Pallas kernels for 15% -> 15%
where the time goes in v8:
time: 80.1 us; the launch traced here: 79.9 us
  Pallas kernels  32.9 us (41%)
  blocking collectives  21.1 us (26%)
  starting transfers between devices  18.5 us (23%)
  waiting for transfers between devices  3.82 us (5%)
  local copies, waits for them, and re-layouts  2.9 us (4%)
    all_to_all x1, blocking collectives, on_device(): totals = lax.all_to_all(total, SEC, split_axis=0, concat_axis=0, tiled=True)  21.1 us
    pallas_call x1, Pallas kernels, krylov_part(): pl.pallas_call(krylov_kernel, in_specs=[smem()] * 4 + [vmem()] * (len(lef...  19.9 us
    ppermute x3, starting transfers between devices, from_partner(): return lax.ppermute(value, axis, pairs)  10.9 us
    ppermute x6, starting transfers between devices, over_rows(): lax.ppermute(chunk, 'row', [(i, (i + d) % rows) for i in range(rows)])  7.57 us
    pallas_call x2, Pallas kernels, gate_right(): pl.pallas_call(functools.partial(right_kernel, slot, cols // local_cols),...  6.87 us
    pallas_call x1, Pallas kernels, gate_left(): pl.pallas_call(functools.partial(left_kernel, slots), in_specs=[smem()] *...  3.72 us
    ppermute x6, waiting for transfers between devices, over_rows(): lax.ppermute(chunk, 'row', [(i, (i + d) % rows) for i in range(rows)])  3.01 us
    unnamed x14, local copies, waits for them, and re-layouts  1.91 us
  transfers between devices with their start and end apart: 9, of which 4 were waited for; matrix products, arithmetic and copies ran while one was open for 0% of the time, Pallas kernels for 15%

profile of v8, /device:TPU:1, one launch (start us, length us, event | category | flops | bytes accessed | tf_op | source)
XLA Modules:
  0.0 79.9 jit_solution(14128669605661833362)
XLA Ops:
  0.6 1.0 %slice_bitcast_fusion = (bf16[512,128]{1,0:T(8,128)(2,1)S(1)}, bf16[512,128]{1,0:T(8,128)(2,1)S(1)}) fusion(bf16[2,512,128]{2,1,0:T(8,128)(2,1)} %param.8), kind=kLoop, calls=%fused_computation | loop fusion | bytes 524288 | tf_op jit(solution)/shard_map/squeeze | solution.py:440
  1.6 0.0 copy-start.2
  1.6 7.8 %collective-permute-start.1 = (bf16[512,128]{1,0:T(8,128)(2,1)S(1)}, bf16[512,128]{1,0:T(8,128)(2,1)S(1)}, u32[]{:S(2)}, u32[]{:S(2)}) collective-permute-start(bf16[512,128]{1,0:T(8,128)(2,1)S(1)} %get-tuple-element.46), channel_id=1, source_target_pairs={{0,128},{4,132},{8,136},{12,140},{16,144},{20,148},{24,152},{28,15... | collective-permute-start | bytes 393224 | tf_op jit(solution)/shard_map/ppermute | solution.py:24
  9.5 0.0 copy-done.2
  9.5 0.0 copy-start
  9.5 1.2 %copy-done = bf16[2,128,2048]{2,1,0:T(8,128)(2,1)S(1)} copy-done((bf16[2,128,2048]{2,1,0:T(8,128)(2,1)S(1)}, bf16[2,128,2048]{2,1,0:T(8,128)(2,1)}, u32[]{:S(2)}) %copy-start) | copy-done | bytes 1048600
  10.7 3.4 %right_gate.2 = (bf16[512,512]{1,0:T(8,128)(2,1)S(1)}, bf16[512,512]{1,0:T(8,128)(2,1)S(1)}, bf16[512,512]{1,0:T(8,128)(2,1)S(1)}) custom-call(s32[1]{0:T(128)} %bitcast.place_ref, bf16[2,128,2048]{2,1,0:T(8,128)(2,1)S(1)} %copy-done, f32[64,16]{1,0:T(8,128)S(1)} %bitcast.12), custom_call_target="tpu_custom_call" | custom-call | flops 4000000000 | bytes 2097152 | tf_op jit(solution)/shard_map/right_gate/pallas_call | solution.py:335
  14.1 0.0 copy-start.3
  14.1 0.7 collective-permute-start
  14.9 0.0 collective-permute-done.1.refs_0_
  14.9 2.8 %collective-permute-start.7 = (bf16[512,128]{1,0:T(8,128)(2,1)S(1)}, bf16[512,128]{1,0:T(8,128)(2,1)S(1)}, u32[]{:S(2)}, u32[]{:S(2)}) collective-permute-start(bf16[512,128]{1,0:T(8,128)(2,1)S(1)} %collective-permute-done.1.refs_0_), channel_id=1, source_target_pairs={{0,3},{1,0},{2,1},{3,2},{4,7},{5,4},{6,5},{7,6},{8,11},{9,8},{10,9... | collective-permute-start | bytes 393224 | tf_op jit(solution)/shard_map/ppermute | solution.py:435
  17.7 0.3 collective-permute-start.6
  18.0 0.7 collective-permute-start.5
  18.7 3.4 %right_gate.3 = (bf16[512,512]{1,0:T(8,128)(2,1)S(1)}, bf16[512,512]{1,0:T(8,128)(2,1)S(1)}, bf16[512,512]{1,0:T(8,128)(2,1)S(1)}) custom-call(s32[1]{0:T(128)} %bitcast.place_ref, bf16[2,128,2048]{2,1,0:T(8,128)(2,1)S(1)} %copy-done, f32[64,16]{1,0:T(8,128)S(1)} %bitcast.13), custom_call_target="tpu_custom_call" | custom-call | flops 4000000000 | bytes 2097152 | tf_op jit(solution)/shard_map/right_gate/pallas_call | solution.py:335
  22.1 0.0 copy-start.4
  22.1 0.8 %collective-permute-done.refs_0_ = bf16[512,128]{1,0:T(8,128)(2,1)S(1)} collective-permute-done((bf16[512,128]{1,0:T(8,128)(2,1)S(1)}, bf16[512,128]{1,0:T(8,128)(2,1)S(1)}, u32[]{:S(2)}, u32[]{:S(2)}) %collective-permute-start) | collective-permute-done | bytes 131104 | tf_op jit(solution)/shard_map/ppermute | solution.py:24
  22.9 0.0 copy-start.1
  22.9 3.0 %collective-permute-start.4 = (bf16[512,128]{1,0:T(8,128)(2,1)S(1)}, bf16[512,128]{1,0:T(8,128)(2,1)S(1)}, u32[]{:S(2)}, u32[]{:S(2)}) collective-permute-start(bf16[512,128]{1,0:T(8,128)(2,1)S(1)} %collective-permute-done.refs_0_), channel_id=1, source_target_pairs={{0,3},{1,0},{2,1},{3,2},{4,7},{5,4},{6,5},{7,6},{8,11},{9,8},{10,9... | collective-permute-start | bytes 393224 | tf_op jit(solution)/shard_map/ppermute | solution.py:435
  25.9 0.1 collective-permute-start.3
  26.0 0.0 collective-permute-done.7.refs_3_
  26.0 0.7 collective-permute-start.2
  26.7 0.0 collective-permute-done.6.refs_2_
  26.7 0.2 collective-permute-done.5.refs_1_
  27.0 0.0 copy-done.3
  27.0 0.0 copy-done.4
  27.0 3.7 %left_gate.1 = (bf16[512,512]{1,0:T(8,128)(2,1)S(1)}, bf16[512,512]{1,0:T(8,128)(2,1)S(1)}, bf16[512,512]{1,0:T(8,128)(2,1)S(1)}, bf16[4,512,256]{2,1,0:T(8,128)(2,1)S(1)}) custom-call(s32[1]{0:T(128)} %bitcast.place_ref, s32[128]{0:T(128)S(1)} %copy-done.4, f32[4,16,16]{2,1,0:T(8,128)S(1)} %copy-done.3, ...), custom_call_target="tpu_custom_call" | custom-call | flops 4000000000 | bytes 2097152 | tf_op jit(solution)/shard_map/left_gate/pallas_call | solution.py:359
  30.7 0.0 collective-permute-done.4.refs_3_
  30.7 0.6 collective-permute-done.3.refs_2_
  31.4 2.1 %collective-permute-done.2.refs_1_ = bf16[512,128]{1,0:T(8,128)(2,1)S(1)} collective-permute-done((bf16[512,128]{1,0:T(8,128)(2,1)S(1)}, bf16[512,128]{1,0:T(8,128)(2,1)S(1)}, u32[]{:S(2)}, u32[]{:S(2)}) %collective-permute-start.2) | collective-permute-done | bytes 131104 | tf_op jit(solution)/shard_map/ppermute | solution.py:435
  33.5 0.0 copy-start.5
  33.5 0.0 copy-start.6
  33.5 0.0 copy-done.1
  33.5 0.6 copy-done.5
  34.1 0.0 copy-done.6
  34.1 19.9 %krylov.1 = (bf16[2,512,128]{2,1,0:T(8,128)(2,1)S(1)}, f32[2,128,512]{2,1,0:T(8,128)S(1)}) custom-call(s32[1]{0:T(128)} %bitcast.place_ref, s32[128]{0:T(128)S(1)} %copy-done.4, s32[128]{0:T(128)S(1)} %copy-done.5, s32[128]{0:T(128)S(1)} %copy-done.6, bf16[512,128]{1,0:T(8,128)(2,1)S(1)} %collective-permute-done.refs_0_, ...), custom_call_target="tpu_custom_call" | custom-call | flops 20000000000 | bytes 2097152 | tf_op jit(solution)/shard_map/krylov/pallas_call | solution.py:379
  54.1 2.3 %collective-permute-start.8 = (bf16[2,512,128]{2,1,0:T(8,128)(2,1)S(1)}, bf16[2,512,128]{2,1,0:T(8,128)(2,1)S(1)}, u32[]{:S(2)}, u32[]{:S(2)}) collective-permute-start(bf16[2,512,128]{2,1,0:T(8,128)(2,1)S(1)} %get-tuple-element.45), channel_id=1, source_target_pairs={{0,128},{4,132},{8,136},{12,140},{16,144},{20,148},{24,152},{28,15... | collective-permute-start | bytes 786440 | tf_op jit(solution)/shard_map/ppermute | solution.py:24
  56.4 1.4 %truncate.1 = (f32[2,128,512]{2,1,0:T(8,128)S(1)}, f32[64,128]{1,0:T(8,128)S(1)}) custom-call(s32[1]{0:T(128)} %bitcast.place_ref, s32[128]{0:T(128)S(1)} %copy-done.5, s32[128]{0:T(128)S(1)} %copy-done.6, f32[2,128,512]{2,1,0:T(8,128)S(1)} %get-tuple-element.40.image_ref, bf16[512,512]{1,0:T(8,128)(2,1)S(1)} %get-tuple-element.36.refs_9_.refs_0_, ...), custom_call_target="tpu_custom_call" | custom-call | flops 2000000000 | bytes 2097152 | tf_op jit(solution)/shard_map/truncate/pallas_call | solution.py:402
  57.8 21.1 %all_to_all.11 = f32[64,1,128]{2,1,0:T(1,128)S(1)} all-to-all(f32[64,1,128]{2,1,0:T(1,128)S(1)} %bitcast.11), channel_id=1, replica_groups=mesh['sec_0'=8,'sec_1'=4,'sec_2'=2,'row'=4] {'sec_0','sec_1','sec_2'}, dimensions={0} | all-to-all | bytes 65536 | tf_op jit(solution)/shard_map/all_to_all | solution.py:458
  78.9 0.0 collective-permute-done.8.sent_ref
  78.9 1.0 %finish.1 = (f32[2,512,128]{2,1,0:T(8,128)}, f32[2,128,512]{2,1,0:T(8,128)}) custom-call(f32[64,128]{1,0:T(8,128)S(1)} %bitcast.10, f32[2,128,512]{2,1,0:T(8,128)S(1)} %get-tuple-element.44.part_ref, bf16[2,512,128]{2,1,0:T(8,128)(2,1)S(1)} %collective-permute-done.8.sent_ref), custom_call_target="tpu_custom_call" | custom-call | flops 1000000 | bytes 2097152 | tf_op jit(solution)/shard_map/finish/pallas_call | solution.py:416
Async XLA Ops:
  1.6 7.8 %copy-start.2 = (f32[4,16,16]{2,1,0:T(8,128)S(1)}, f32[4,16,16]{2,1,0:T(8,128)}, u32[]{:S(2)}) copy-start(f32[4,16,16]{2,1,0:T(8,128)} %param.11) | copy-start | bytes 12292
  1.6 13.3 %collective-permute-start.1 = (bf16[512,128]{1,0:T(8,128)(2,1)S(1)}, bf16[512,128]{1,0:T(8,128)(2,1)S(1)}, u32[]{:S(2)}, u32[]{:S(2)}) collective-permute-start(bf16[512,128]{1,0:T(8,128)(2,1)S(1)} %get-tuple-element.46), channel_id=1, source_target_pairs={{0,128},{4,132},{8,136},{12,140},{16,144},{20,148},{24,152},{28,15... | collective-permute-start | bytes 393224 | tf_op jit(solution)/shard_map/ppermute | solution.py:24
  9.5 1.2 %copy-start = (bf16[2,128,2048]{2,1,0:T(8,128)(2,1)S(1)}, bf16[2,128,2048]{2,1,0:T(8,128)(2,1)}, u32[]{:S(2)}) copy-start(bf16[2,128,2048]{2,1,0:T(8,128)(2,1)} %right_ref.3) | copy-start | bytes 3145732
  14.1 12.8 %copy-start.3 = (f32[4,16,16]{2,1,0:T(8,128)S(1)}, f32[4,16,16]{2,1,0:T(8,128)}, u32[]{:S(2)}) copy-start(f32[4,16,16]{2,1,0:T(8,128)} %left_ops_ref.1) | copy-start | bytes 12292
  14.1 8.8 %collective-permute-start = (bf16[512,128]{1,0:T(8,128)(2,1)S(1)}, bf16[512,128]{1,0:T(8,128)(2,1)S(1)}, u32[]{:S(2)}, u32[]{:S(2)}) collective-permute-start(bf16[512,128]{1,0:T(8,128)(2,1)S(1)} %get-tuple-element.25), channel_id=1, source_target_pairs={{0,128},{4,132},{8,136},{12,140},{16,144},{20,148},{24,152},{28,15... | collective-permute-start | bytes 393224 | tf_op jit(solution)/shard_map/ppermute | solution.py:24
  14.9 11.1 %collective-permute-start.7 = (bf16[512,128]{1,0:T(8,128)(2,1)S(1)}, bf16[512,128]{1,0:T(8,128)(2,1)S(1)}, u32[]{:S(2)}, u32[]{:S(2)}) collective-permute-start(bf16[512,128]{1,0:T(8,128)(2,1)S(1)} %collective-permute-done.1.refs_0_), channel_id=1, source_target_pairs={{0,3},{1,0},{2,1},{3,2},{4,7},{5,4},{6,5},{7,6},{8,11},{9,8},{10,9... | collective-permute-start | bytes 393224 | tf_op jit(solution)/shard_map/ppermute | solution.py:435
  17.7 9.1 %collective-permute-start.6 = (bf16[512,128]{1,0:T(8,128)(2,1)S(1)}, bf16[512,128]{1,0:T(8,128)(2,1)S(1)}, u32[]{:S(2)}, u32[]{:S(2)}) collective-permute-start(bf16[512,128]{1,0:T(8,128)(2,1)S(1)} %collective-permute-done.1.refs_0_), channel_id=1, source_target_pairs={{0,2},{1,3},{2,0},{3,1},{4,6},{5,7},{6,4},{7,5},{8,10},{9,11},{10,... | collective-permute-start | bytes 393224 | tf_op jit(solution)/shard_map/ppermute | solution.py:435
  18.0 9.0 %collective-permute-start.5 = (bf16[512,128]{1,0:T(8,128)(2,1)S(1)}, bf16[512,128]{1,0:T(8,128)(2,1)S(1)}, u32[]{:S(2)}, u32[]{:S(2)}) collective-permute-start(bf16[512,128]{1,0:T(8,128)(2,1)S(1)} %collective-permute-done.1.refs_0_), channel_id=1, source_target_pairs={{0,1},{1,2},{2,3},{3,0},{4,5},{5,6},{6,7},{7,4},{8,9},{9,10},{10,1... | collective-permute-start | bytes 393224 | tf_op jit(solution)/shard_map/ppermute | solution.py:435
  22.1 4.9 %copy-start.4 = (s32[128]{0:T(128)S(1)}, s32[128]{0:T(128)}, u32[]{:S(2)}) copy-start(s32[128]{0:T(128)} %live_ref.3) | copy-start | bytes 1540
  22.9 10.5 %copy-start.1 = (s32[128,128]{1,0:T(8,128)S(1)}, s32[128,128]{1,0:T(8,128)}, u32[]{:S(2)}) copy-start(s32[128,128]{1,0:T(8,128)} %refs_8_.1) | copy-start | bytes 196612
  22.9 7.8 %collective-permute-start.4 = (bf16[512,128]{1,0:T(8,128)(2,1)S(1)}, bf16[512,128]{1,0:T(8,128)(2,1)S(1)}, u32[]{:S(2)}, u32[]{:S(2)}) collective-permute-start(bf16[512,128]{1,0:T(8,128)(2,1)S(1)} %collective-permute-done.refs_0_), channel_id=1, source_target_pairs={{0,3},{1,0},{2,1},{3,2},{4,7},{5,4},{6,5},{7,6},{8,11},{9,8},{10,9... | collective-permute-start | bytes 393224 | tf_op jit(solution)/shard_map/ppermute | solution.py:435
  25.9 5.4 %collective-permute-start.3 = (bf16[512,128]{1,0:T(8,128)(2,1)S(1)}, bf16[512,128]{1,0:T(8,128)(2,1)S(1)}, u32[]{:S(2)}, u32[]{:S(2)}) collective-permute-start(bf16[512,128]{1,0:T(8,128)(2,1)S(1)} %collective-permute-done.refs_0_), channel_id=1, source_target_pairs={{0,2},{1,3},{2,0},{3,1},{4,6},{5,7},{6,4},{7,5},{8,10},{9,11},{10,... | collective-permute-start | bytes 393224 | tf_op jit(solution)/shard_map/ppermute | solution.py:435
  26.0 7.4 %collective-permute-start.2 = (bf16[512,128]{1,0:T(8,128)(2,1)S(1)}, bf16[512,128]{1,0:T(8,128)(2,1)S(1)}, u32[]{:S(2)}, u32[]{:S(2)}) collective-permute-start(bf16[512,128]{1,0:T(8,128)(2,1)S(1)} %collective-permute-done.refs_0_), channel_id=1, source_target_pairs={{0,1},{1,2},{2,3},{3,0},{4,5},{5,6},{6,7},{7,4},{8,9},{9,10},{10,1... | collective-permute-start | bytes 393224 | tf_op jit(solution)/shard_map/ppermute | solution.py:435
  33.5 0.7 copy-start.5
  33.5 0.7 copy-start.6
  54.1 24.8 %collective-permute-start.8 = (bf16[2,512,128]{2,1,0:T(8,128)(2,1)S(1)}, bf16[2,512,128]{2,1,0:T(8,128)(2,1)S(1)}, u32[]{:S(2)}, u32[]{:S(2)}) collective-permute-start(bf16[2,512,128]{2,1,0:T(8,128)(2,1)S(1)} %get-tuple-element.45), channel_id=1, source_target_pairs={{0,128},{4,132},{8,136},{12,140},{16,144},{20,148},{24,152},{28,15... | collective-permute-start | bytes 786440 | tf_op jit(solution)/shard_map/ppermute | solution.py:24

commit v9 on v8

--- a/solution.py
+++ b/solution.py
@@ -114,24 +114,26 @@
 
 
 def right_kernel(
-    slot, rows, place_ref, right_ref, right_ops_ref, high_ref, low_ref, local_ref,
-    right_mix, gated, right, sem,
+    slot, rows, build, place_ref, right_ref, given_ref, high_ref, low_ref, local_ref, *refs
 ):
+    *made, gated, right, sem = refs
+    right_mix = made[0] if build else given_ref
     states = right.shape[0]
     terms = gated.shape[0] // states
     wide = SITE * SITE
     local_cols = local_ref.shape[1]
     fetch = pltpu.make_async_copy(right_ref.at[slot], right, sem)
     fetch.start()
-    spread = as_weights(one_hot((terms * wide, terms * SITE), lambda r: r // SITE, lambda c: c))
-    widen = as_weights(one_hot((SITE, wide), lambda r: r, lambda c: c // SITE))
-    same = one_hot((terms * wide, wide), lambda r: r % SITE, lambda c: c % SITE)
-    for part, piece in enumerate(two_parts(right_ops_ref[...])):
-        tall = dot_over(spread, piece, 1, 0).astype(jnp.bfloat16)
-        full = dot_over(tall, widen, 1, 0)
-        right_mix[:, part * wide : (part + 1) * wide] = jnp.where(same, full, 0.0).astype(
-            jnp.bfloat16
-        )
+    if build:
+        spread = as_weights(one_hot((terms * wide, terms * SITE), lambda r: r // SITE, lambda c: c))
+        widen = as_weights(one_hot((SITE, wide), lambda r: r, lambda c: c // SITE))
+        same = one_hot((terms * wide, wide), lambda r: r % SITE, lambda c: c % SITE)
+        for part, piece in enumerate(two_parts(given_ref[...])):
+            tall = dot_over(spread, piece, 1, 0).astype(jnp.bfloat16)
+            full = dot_over(tall, widen, 1, 0)
+            right_mix[:, part * wide : (part + 1) * wide] = jnp.where(same, full, 0.0).astype(
+                jnp.bfloat16
+            )
     fetch.wait()
     for pair in range(states // (2 * SITE)):
         base = pair * 2 * SITE
@@ -328,28 +330,30 @@
     )
 
 
-def gate_right(slot, row, right_block, right_ops, local_cols):
+def gate_right(slot, row, right_block, given, local_cols, build):
     _, states, cols = right_block.shape
-    terms = right_ops.shape[0]
-    bond, wide = terms * states, SITE * SITE
+    wide = SITE * SITE
+    terms = given.shape[0] // (SITE if build else wide)
+    bond = terms * states
+    made = [shape_of((terms * wide, 2 * wide), jnp.bfloat16)] if build else []
     return pl.pallas_call(
-        functools.partial(right_kernel, slot, cols // local_cols),
+        functools.partial(right_kernel, slot, cols // local_cols, build),
         in_specs=[smem(), pl.BlockSpec(memory_space=pltpu.HBM), vmem()],
-        out_specs=[vmem()] * 3,
+        out_specs=[vmem()] * (3 + len(made)),
         out_shape=[
             shape_of((bond, bond), jnp.bfloat16),
             shape_of((bond, bond), jnp.bfloat16),
             shape_of((bond, local_cols), jnp.bfloat16),
+            *made,
         ],
         scratch_shapes=[
-            pltpu.VMEM((terms * wide, 2 * wide), jnp.bfloat16),
             pltpu.VMEM((bond, cols), jnp.bfloat16),
             pltpu.VMEM((states, cols), jnp.bfloat16),
             pltpu.SemaphoreType.DMA,
         ],
         name="right_gate",
         **kernel_options(12, 4e9),
-    )(row, right_block, right_ops.reshape(terms * SITE, SITE))
+    )(row, right_block, given)
 
 
 def gate_left(slots, row, live, left_chunks, left_ops):
@@ -438,12 +442,13 @@
         return [chunk, *sent]
 
     theirs = [from_partner(left_block[0], SEC, top_bit)]
-    first = list(gate_right(0, row, right_block, right_ops, local_cols))
+    factors = right_ops.reshape(-1, SITE)
+    *first, right_mix = gate_right(0, row, right_block, factors, local_cols, True)
     second_block, first[0] = lax.optimization_barrier((left_block[1], first[0]))
     theirs.append(from_partner(second_block, SEC, top_bit))
     theirs[0], first[0], row_second = lax.optimization_barrier((theirs[0], first[0], row))
     first_chunks = over_rows(theirs[0])
-    second = list(gate_right(1, row_second, right_block, right_ops, local_cols))
+    second = list(gate_right(1, row_second, right_block, right_mix, local_cols, False))
     theirs[1], second[0], row_left = lax.optimization_barrier((theirs[1], second[0], row))
     second_chunks = over_rows(theirs[1])
     *first_left, left_mix = gate_left(slots, row_left, live_states, first_chunks, left_ops)

time: 80.1 us -> 80.1 us (level)
  starting transfers between devices: 18.5 us -> 17.6 us
  waiting for transfers between devices: 3.82 us -> 4.67 us
    all_to_all x1, blocking collectives: 21.1 us -> 21.9 us  [on_device(): totals = lax.all_to_all(total, SEC, split_axis=0, concat_axis=0, tiled=True)]
    ppermute x3, starting transfers between devices: 10.9 us -> 10.1 us  [from_partner(): return lax.ppermute(value, axis, pairs)]
    ppermute x3, waiting for transfers between devices: 0.81 us -> 1.64 us  [from_partner(): return lax.ppermute(value, axis, pairs)]
    pallas_call x2, Pallas kernels: 6.87 us -> 6.07 us  [gate_right(): pl.pallas_call(functools.partial(right_kernel, slot, cols // local_cols,...]
  transfers between devices with their start and end apart: 9 -> 9, of which waited for: 4 -> 4; matrix products, arithmetic and copies ran while one was open for 0% -> 0% of each run, Pallas kernels for 15% -> 14%
where the time goes in v9:
time: 80.1 us; the launch traced here: 79.9 us
  Pallas kernels  32.1 us (40%)
  blocking collectives  21.9 us (27%)
  starting transfers between devices  17.6 us (22%)
  waiting for transfers between devices  4.67 us (6%)
  local copies, waits for them, and re-layouts  2.9 us (4%)
    all_to_all x1, blocking collectives, on_device(): totals = lax.all_to_all(total, SEC, split_axis=0, concat_axis=0, tiled=True)  21.9 us
    pallas_call x1, Pallas kernels, krylov_part(): pl.pallas_call(krylov_kernel, in_specs=[smem()] * 4 + [vmem()] * (len(lef...  19.9 us
    ppermute x3, starting transfers between devices, from_partner(): return lax.ppermute(value, axis, pairs)  10.1 us
    ppermute x6, starting transfers between devices, over_rows(): lax.ppermute(chunk, 'row', [(i, (i + d) % rows) for i in range(rows)])  7.54 us
    pallas_call x2, Pallas kernels, gate_right(): pl.pallas_call(functools.partial(right_kernel, slot, cols // local_cols,...  6.07 us
    pallas_call x1, Pallas kernels, gate_left(): pl.pallas_call(functools.partial(left_kernel, slots), in_specs=[smem()] *...  3.69 us
    ppermute x6, waiting for transfers between devices, over_rows(): lax.ppermute(chunk, 'row', [(i, (i + d) % rows) for i in range(rows)])  3.03 us
    unnamed x14, local copies, waits for them, and re-layouts  1.91 us
  transfers between devices with their start and end apart: 9, of which 4 were waited for; matrix products, arithmetic and copies ran while one was open for 0% of the time, Pallas kernels for 14%

profile of v9, /device:TPU:1, one launch (start us, length us, event | category | flops | bytes accessed | tf_op | source)
XLA Modules:
  0.0 79.9 jit_solution(15751880425119654718)
XLA Ops:
  0.6 1.0 %slice_bitcast_fusion = (bf16[512,128]{1,0:T(8,128)(2,1)S(1)}, bf16[512,128]{1,0:T(8,128)(2,1)S(1)}) fusion(bf16[2,512,128]{2,1,0:T(8,128)(2,1)} %param.8), kind=kLoop, calls=%fused_computation | loop fusion | bytes 524288 | tf_op jit(solution)/shard_map/squeeze | solution.py:444
  1.6 0.0 copy-start.2
  1.6 7.8 %collective-permute-start.1 = (bf16[512,128]{1,0:T(8,128)(2,1)S(1)}, bf16[512,128]{1,0:T(8,128)(2,1)S(1)}, u32[]{:S(2)}, u32[]{:S(2)}) collective-permute-start(bf16[512,128]{1,0:T(8,128)(2,1)S(1)} %get-tuple-element.48), channel_id=1, source_target_pairs={{0,128},{4,132},{8,136},{12,140},{16,144},{20,148},{24,152},{28,15... | collective-permute-start | bytes 393224 | tf_op jit(solution)/shard_map/ppermute | solution.py:24
  9.5 0.0 copy-done.2
  9.5 0.0 copy-start
  9.5 1.2 %copy-done = bf16[2,128,2048]{2,1,0:T(8,128)(2,1)S(1)} copy-done((bf16[2,128,2048]{2,1,0:T(8,128)(2,1)S(1)}, bf16[2,128,2048]{2,1,0:T(8,128)(2,1)}, u32[]{:S(2)}) %copy-start) | copy-done | bytes 1048600
  10.7 3.5 %right_gate.2 = (bf16[512,512]{1,0:T(8,128)(2,1)S(1)}, bf16[512,512]{1,0:T(8,128)(2,1)S(1)}, bf16[512,512]{1,0:T(8,128)(2,1)S(1)}, bf16[1024,512]{1,0:T(8,128)(2,1)S(1)}) custom-call(s32[1]{0:T(128)} %bitcast.place_ref, bf16[2,128,2048]{2,1,0:T(8,128)(2,1)S(1)} %copy-done, f32[64,16]{1,0:T(8,128)S(1)} %bitcast.12), custom_call_target="tpu_custom_call" | custom-call | flops 4000000000 | bytes 2097152 | tf_op jit(solution)/shard_map/right_gate/pallas_call | solution.py:339
  14.2 0.7 collective-permute-start
  14.9 0.0 collective-permute-done.1.refs_0_
  14.9 2.8 %collective-permute-start.7 = (bf16[512,128]{1,0:T(8,128)(2,1)S(1)}, bf16[512,128]{1,0:T(8,128)(2,1)S(1)}, u32[]{:S(2)}, u32[]{:S(2)}) collective-permute-start(bf16[512,128]{1,0:T(8,128)(2,1)S(1)} %collective-permute-done.1.refs_0_), channel_id=1, source_target_pairs={{0,3},{1,0},{2,1},{3,2},{4,7},{5,4},{6,5},{7,6},{8,11},{9,8},{10,9... | collective-permute-start | bytes 393224 | tf_op jit(solution)/shard_map/ppermute | solution.py:439
  17.7 0.3 collective-permute-start.6
  18.0 0.7 collective-permute-start.5
  18.7 0.0 copy-start.3
  18.7 2.6 %right_gate.3 = (bf16[512,512]{1,0:T(8,128)(2,1)S(1)}, bf16[512,512]{1,0:T(8,128)(2,1)S(1)}, bf16[512,512]{1,0:T(8,128)(2,1)S(1)}) custom-call(s32[1]{0:T(128)} %bitcast.place_ref, bf16[2,128,2048]{2,1,0:T(8,128)(2,1)S(1)} %copy-done, bf16[1024,512]{1,0:T(8,128)(2,1)S(1)} %get-tuple-element.29.given_ref), custom_call_target="tpu_custom_call" | custom-call | flops 4000000000 | bytes 2097152 | tf_op jit(solution)/shard_map/right_gate/pallas_call | solution.py:339
  21.3 0.0 copy-start.4
  21.3 1.6 %collective-permute-done.refs_0_ = bf16[512,128]{1,0:T(8,128)(2,1)S(1)} collective-permute-done((bf16[512,128]{1,0:T(8,128)(2,1)S(1)}, bf16[512,128]{1,0:T(8,128)(2,1)S(1)}, u32[]{:S(2)}, u32[]{:S(2)}) %collective-permute-start) | collective-permute-done | bytes 131104 | tf_op jit(solution)/shard_map/ppermute | solution.py:24
  23.0 0.0 copy-start.1
  23.0 3.0 %collective-permute-start.4 = (bf16[512,128]{1,0:T(8,128)(2,1)S(1)}, bf16[512,128]{1,0:T(8,128)(2,1)S(1)}, u32[]{:S(2)}, u32[]{:S(2)}) collective-permute-start(bf16[512,128]{1,0:T(8,128)(2,1)S(1)} %collective-permute-done.refs_0_), channel_id=1, source_target_pairs={{0,3},{1,0},{2,1},{3,2},{4,7},{5,4},{6,5},{7,6},{8,11},{9,8},{10,9... | collective-permute-start | bytes 393224 | tf_op jit(solution)/shard_map/ppermute | solution.py:439
  25.9 0.1 collective-permute-start.3
  26.0 0.0 collective-permute-done.7.refs_3_
  26.0 0.7 collective-permute-start.2
  26.7 0.0 collective-permute-done.6.refs_2_
  26.7 0.2 collective-permute-done.5.refs_1_
  27.0 0.0 copy-done.3
  27.0 0.0 copy-done.4
  27.0 3.7 %left_gate.1 = (bf16[512,512]{1,0:T(8,128)(2,1)S(1)}, bf16[512,512]{1,0:T(8,128)(2,1)S(1)}, bf16[512,512]{1,0:T(8,128)(2,1)S(1)}, bf16[4,512,256]{2,1,0:T(8,128)(2,1)S(1)}) custom-call(s32[1]{0:T(128)} %bitcast.place_ref, s32[128]{0:T(128)S(1)} %copy-done.4, f32[4,16,16]{2,1,0:T(8,128)S(1)} %copy-done.3, ...), custom_call_target="tpu_custom_call" | custom-call | flops 4000000000 | bytes 2097152 | tf_op jit(solution)/shard_map/left_gate/pallas_call | solution.py:363
  30.7 0.0 collective-permute-done.4.refs_3_
  30.7 0.7 collective-permute-done.3.refs_2_
  31.4 2.1 %collective-permute-done.2.refs_1_ = bf16[512,128]{1,0:T(8,128)(2,1)S(1)} collective-permute-done((bf16[512,128]{1,0:T(8,128)(2,1)S(1)}, bf16[512,128]{1,0:T(8,128)(2,1)S(1)}, u32[]{:S(2)}, u32[]{:S(2)}) %collective-permute-start.2) | collective-permute-done | bytes 131104 | tf_op jit(solution)/shard_map/ppermute | solution.py:439
  33.5 0.0 copy-start.5
  33.5 0.0 copy-start.6
  33.5 0.0 copy-done.1
  33.5 0.6 copy-done.5
  34.1 0.0 copy-done.6
  34.1 19.9 %krylov.1 = (bf16[2,512,128]{2,1,0:T(8,128)(2,1)S(1)}, f32[2,128,512]{2,1,0:T(8,128)S(1)}) custom-call(s32[1]{0:T(128)} %bitcast.place_ref, s32[128]{0:T(128)S(1)} %copy-done.4, s32[128]{0:T(128)S(1)} %copy-done.5, s32[128]{0:T(128)S(1)} %copy-done.6, bf16[512,128]{1,0:T(8,128)(2,1)S(1)} %collective-permute-done.refs_0_, ...), custom_call_target="tpu_custom_call" | custom-call | flops 20000000000 | bytes 2097152 | tf_op jit(solution)/shard_map/krylov/pallas_call | solution.py:383
  54.0 1.5 %collective-permute-start.8 = (bf16[2,512,128]{2,1,0:T(8,128)(2,1)S(1)}, bf16[2,512,128]{2,1,0:T(8,128)(2,1)S(1)}, u32[]{:S(2)}, u32[]{:S(2)}) collective-permute-start(bf16[2,512,128]{2,1,0:T(8,128)(2,1)S(1)} %get-tuple-element.47), channel_id=1, source_target_pairs={{0,128},{4,132},{8,136},{12,140},{16,144},{20,148},{24,152},{28,15... | collective-permute-start | bytes 786440 | tf_op jit(solution)/shard_map/ppermute | solution.py:24
  55.5 1.4 %truncate.1 = (f32[2,128,512]{2,1,0:T(8,128)S(1)}, f32[64,128]{1,0:T(8,128)S(1)}) custom-call(s32[1]{0:T(128)} %bitcast.place_ref, s32[128]{0:T(128)S(1)} %copy-done.5, s32[128]{0:T(128)S(1)} %copy-done.6, f32[2,128,512]{2,1,0:T(8,128)S(1)} %get-tuple-element.42.image_ref, bf16[512,512]{1,0:T(8,128)(2,1)S(1)} %get-tuple-element.38.refs_9_.refs_0_, ...), custom_call_target="tpu_custom_call" | custom-call | flops 2000000000 | bytes 2097152 | tf_op jit(solution)/shard_map/truncate/pallas_call | solution.py:406
  56.9 21.9 %all_to_all.11 = f32[64,1,128]{2,1,0:T(1,128)S(1)} all-to-all(f32[64,1,128]{2,1,0:T(1,128)S(1)} %bitcast.11), channel_id=1, replica_groups=mesh['sec_0'=8,'sec_1'=4,'sec_2'=2,'row'=4] {'sec_0','sec_1','sec_2'}, dimensions={0} | all-to-all | bytes 65536 | tf_op jit(solution)/shard_map/all_to_all | solution.py:463
  78.8 0.0 collective-permute-done.8.sent_ref
  78.8 1.0 %finish.1 = (f32[2,512,128]{2,1,0:T(8,128)}, f32[2,128,512]{2,1,0:T(8,128)}) custom-call(f32[64,128]{1,0:T(8,128)S(1)} %bitcast.10, f32[2,128,512]{2,1,0:T(8,128)S(1)} %get-tuple-element.46.part_ref, bf16[2,512,128]{2,1,0:T(8,128)(2,1)S(1)} %collective-permute-done.8.sent_ref), custom_call_target="tpu_custom_call" | custom-call | flops 1000000 | bytes 2097152 | tf_op jit(solution)/shard_map/finish/pallas_call | solution.py:420
Async XLA Ops:
  1.6 7.8 %copy-start.2 = (f32[4,16,16]{2,1,0:T(8,128)S(1)}, f32[4,16,16]{2,1,0:T(8,128)}, u32[]{:S(2)}) copy-start(f32[4,16,16]{2,1,0:T(8,128)} %param.11) | copy-start | bytes 12292
  1.6 13.3 %collective-permute-start.1 = (bf16[512,128]{1,0:T(8,128)(2,1)S(1)}, bf16[512,128]{1,0:T(8,128)(2,1)S(1)}, u32[]{:S(2)}, u32[]{:S(2)}) collective-permute-start(bf16[512,128]{1,0:T(8,128)(2,1)S(1)} %get-tuple-element.48), channel_id=1, source_target_pairs={{0,128},{4,132},{8,136},{12,140},{16,144},{20,148},{24,152},{28,15... | collective-permute-start | bytes 393224 | tf_op jit(solution)/shard_map/ppermute | solution.py:24
  9.5 1.2 %copy-start = (bf16[2,128,2048]{2,1,0:T(8,128)(2,1)S(1)}, bf16[2,128,2048]{2,1,0:T(8,128)(2,1)}, u32[]{:S(2)}) copy-start(bf16[2,128,2048]{2,1,0:T(8,128)(2,1)} %right_ref.3) | copy-start | bytes 3145732
  14.2 8.8 %collective-permute-start = (bf16[512,128]{1,0:T(8,128)(2,1)S(1)}, bf16[512,128]{1,0:T(8,128)(2,1)S(1)}, u32[]{:S(2)}, u32[]{:S(2)}) collective-permute-start(bf16[512,128]{1,0:T(8,128)(2,1)S(1)} %get-tuple-element.26), channel_id=1, source_target_pairs={{0,128},{4,132},{8,136},{12,140},{16,144},{20,148},{24,152},{28,15... | collective-permute-start | bytes 393224 | tf_op jit(solution)/shard_map/ppermute | solution.py:24
  14.9 11.1 %collective-permute-start.7 = (bf16[512,128]{1,0:T(8,128)(2,1)S(1)}, bf16[512,128]{1,0:T(8,128)(2,1)S(1)}, u32[]{:S(2)}, u32[]{:S(2)}) collective-permute-start(bf16[512,128]{1,0:T(8,128)(2,1)S(1)} %collective-permute-done.1.refs_0_), channel_id=1, source_target_pairs={{0,3},{1,0},{2,1},{3,2},{4,7},{5,4},{6,5},{7,6},{8,11},{9,8},{10,9... | collective-permute-start | bytes 393224 | tf_op jit(solution)/shard_map/ppermute | solution.py:439
  17.7 9.0 %collective-permute-start.6 = (bf16[512,128]{1,0:T(8,128)(2,1)S(1)}, bf16[512,128]{1,0:T(8,128)(2,1)S(1)}, u32[]{:S(2)}, u32[]{:S(2)}) collective-permute-start(bf16[512,128]{1,0:T(8,128)(2,1)S(1)} %collective-permute-done.1.refs_0_), channel_id=1, source_target_pairs={{0,2},{1,3},{2,0},{3,1},{4,6},{5,7},{6,4},{7,5},{8,10},{9,11},{10,... | collective-permute-start | bytes 393224 | tf_op jit(solution)/shard_map/ppermute | solution.py:439
  18.0 9.0 %collective-permute-start.5 = (bf16[512,128]{1,0:T(8,128)(2,1)S(1)}, bf16[512,128]{1,0:T(8,128)(2,1)S(1)}, u32[]{:S(2)}, u32[]{:S(2)}) collective-permute-start(bf16[512,128]{1,0:T(8,128)(2,1)S(1)} %collective-permute-done.1.refs_0_), channel_id=1, source_target_pairs={{0,1},{1,2},{2,3},{3,0},{4,5},{5,6},{6,7},{7,4},{8,9},{9,10},{10,1... | collective-permute-start | bytes 393224 | tf_op jit(solution)/shard_map/ppermute | solution.py:439
  18.7 8.3 %copy-start.3 = (f32[4,16,16]{2,1,0:T(8,128)S(1)}, f32[4,16,16]{2,1,0:T(8,128)}, u32[]{:S(2)}) copy-start(f32[4,16,16]{2,1,0:T(8,128)} %left_ops_ref.1) | copy-start | bytes 12292
  21.3 5.7 %copy-start.4 = (s32[128]{0:T(128)S(1)}, s32[128]{0:T(128)}, u32[]{:S(2)}) copy-start(s32[128]{0:T(128)} %live_ref.3) | copy-start | bytes 1540
  23.0 10.5 %copy-start.1 = (s32[128,128]{1,0:T(8,128)S(1)}, s32[128,128]{1,0:T(8,128)}, u32[]{:S(2)}) copy-start(s32[128,128]{1,0:T(8,128)} %refs_8_.1) | copy-start | bytes 196612
  23.0 7.7 %collective-permute-start.4 = (bf16[512,128]{1,0:T(8,128)(2,1)S(1)}, bf16[512,128]{1,0:T(8,128)(2,1)S(1)}, u32[]{:S(2)}, u32[]{:S(2)}) collective-permute-start(bf16[512,128]{1,0:T(8,128)(2,1)S(1)} %collective-permute-done.refs_0_), channel_id=1, source_target_pairs={{0,3},{1,0},{2,1},{3,2},{4,7},{5,4},{6,5},{7,6},{8,11},{9,8},{10,9... | collective-permute-start | bytes 393224 | tf_op jit(solution)/shard_map/ppermute | solution.py:439
  25.9 5.4 %collective-permute-start.3 = (bf16[512,128]{1,0:T(8,128)(2,1)S(1)}, bf16[512,128]{1,0:T(8,128)(2,1)S(1)}, u32[]{:S(2)}, u32[]{:S(2)}) collective-permute-start(bf16[512,128]{1,0:T(8,128)(2,1)S(1)} %collective-permute-done.refs_0_), channel_id=1, source_target_pairs={{0,2},{1,3},{2,0},{3,1},{4,6},{5,7},{6,4},{7,5},{8,10},{9,11},{10,... | collective-permute-start | bytes 393224 | tf_op jit(solution)/shard_map/ppermute | solution.py:439
  26.0 7.4 %collective-permute-start.2 = (bf16[512,128]{1,0:T(8,128)(2,1)S(1)}, bf16[512,128]{1,0:T(8,128)(2,1)S(1)}, u32[]{:S(2)}, u32[]{:S(2)}) collective-permute-start(bf16[512,128]{1,0:T(8,128)(2,1)S(1)} %collective-permute-done.refs_0_), channel_id=1, source_target_pairs={{0,1},{1,2},{2,3},{3,0},{4,5},{5,6},{6,7},{7,4},{8,9},{9,10},{10,1... | collective-permute-start | bytes 393224 | tf_op jit(solution)/shard_map/ppermute | solution.py:439
  33.5 0.7 copy-start.5
  33.5 0.7 copy-start.6
  54.0 24.8 %collective-permute-start.8 = (bf16[2,512,128]{2,1,0:T(8,128)(2,1)S(1)}, bf16[2,512,128]{2,1,0:T(8,128)(2,1)S(1)}, u32[]{:S(2)}, u32[]{:S(2)}) collective-permute-start(bf16[2,512,128]{2,1,0:T(8,128)(2,1)S(1)} %get-tuple-element.47), channel_id=1, source_target_pairs={{0,128},{4,132},{8,136},{12,140},{16,144},{20,148},{24,152},{28,15... | collective-permute-start | bytes 786440 | tf_op jit(solution)/shard_map/ppermute | solution.py:24
